TPU v7x, 32 devices: a whole 2x2x4 slice. The times are simulated.
32 devices in a mesh: wide: 8 (over z, x), narrow: 4 (over y, core).
Axes of the slice: x: 2, y: 2, z: 4, core: 2. Of those that a mesh axis runs over, the one named last changes fastest.
Arguments:
- patches: bfloat16 [8192, 768], P(('wide', 'narrow')), may hold values from -6 to 6
- cotangent: float32 [8192, 768], P(('wide', 'narrow')), may hold values from -6 to 6
- mask_index: int32 [16, 450], P('wide'), may hold values from 0 to 511, as said below
- mask_count: int32 [16], P('wide'), may hold values from 100 to 450, as said below
- weights: float32 [2, 12, 768, 768], P(None, None, 'wide', 'narrow')
- first_moment: float32 [2, 12, 768, 768], P(None, None, 'wide', 'narrow'), may hold values from -0.0004272461 to 0.0004272461
- second_moment: float32 [2, 12, 768, 768], P(None, None, 'wide', 'narrow'), may hold values from 3.532127e-11 to 5.651403e-10
- small_params: float32 [5, 768], P(None, 'wide')
- small_first: float32 [5, 768], P(None, 'wide'), may hold values from -0.0012207031 to 0.0012207031
- small_second: float32 [5, 768], P(None, 'wide'), may hold values from 3.1789144e-10 to 5.086263e-09
Outputs:
- block_output: float32 [8192, 768], P(('wide', 'narrow'))
- input_grad: float32 [8192, 768], P(('wide', 'narrow'))
- new_weights: float32 [2, 12, 768, 768], P(None, None, 'wide', 'narrow')
- new_first: float32 [2, 12, 768, 768], P(None, None, 'wide', 'narrow')
- new_second: float32 [2, 12, 768, 768], P(None, None, 'wide', 'narrow')
- new_small: float32 [5, 768], P(None, 'wide')
- new_small_first: float32 [5, 768], P(None, 'wide')
- new_small_second: float32 [5, 768], P(None, 'wide')
- grad_norm: float32 [], replicated
Inputs may be any that keep to these rules, and one draw needn't show every extreme that they name: `mask_index`: row c lists 450 distinct patch positions of clip c; its first mask_count[c] entries are the masked patches, the rest are not masked. `mask_count`: some clip has exactly 450 masked patches and another exactly 100.
All inputs are finite; a program needn't handle non-finite values.
Results may differ from a plain program's by a relative error of at most 0.02.
Values may be sent and summed in bfloat16 or wider, within the bound.
A program may use at most 192 MiB of HBM per device.

v0:
```python
import jax
import jax.numpy as jnp
from jax import lax
from jax.sharding import PartitionSpec as P

D = 768
HD = 64
LAYERS = 2
SEQ = 512
STEP = 10


EPS_NORM = 1e-06
BETA_ONE = 0.9
BETA_TWO = 0.999
EPS_ADAM = 1e-08
DECAY_RATE = 0.05
RATE_SMALL = 0.6
CLIP_MAX = 1.0


def layer_norm(values, gain):
    centre = values - jnp.mean(values, axis=-1, keepdims=True)
    spread = jnp.mean(centre * centre, axis=-1, keepdims=True)
    return centre * lax.rsqrt(spread + EPS_NORM) * gain


def exact_gelu(values):
    return jax.nn.gelu(values, approximate=False)


def gather_rows(share):
    return lax.all_gather(share, "narrow", axis=0, tiled=True)


def gather_grads(share):
    return lax.all_gather(share, "narrow", axis=0, tiled=True)


def branch_total(term, row_count):
    return lax.psum_scatter(
        term(jnp.int32(0), row_count * lax.axis_size("narrow")).astype(jnp.bfloat16),
        "narrow",
        scatter_dimension=0,
        tiled=True,
    ).astype(jnp.float32)


def input_total(term, row_count):
    return lax.psum_scatter(
        term(jnp.int32(0), row_count * lax.axis_size("narrow")).astype(jnp.bfloat16),
        "narrow",
        scatter_dimension=0,
        tiled=True,
    ).astype(jnp.float32)


def heads_of(values, clip_count):
    return values.reshape(clip_count, SEQ, values.shape[1] // HD, HD)


def attend_clip(parts):
    queries, key_rows, value_rows = parts
    scores = jnp.einsum(
        "qhd,khd->hqk", queries, key_rows, preferred_element_type=jnp.float32
    ) * HD ** (-0.5)
    probs = jax.nn.softmax(scores, axis=-1)
    return jnp.einsum(
        "hqk,khd->qhd", probs.astype(jnp.bfloat16), value_rows, preferred_element_type=jnp.float32
    ).astype(jnp.bfloat16)


def attend_back_clip(parts):
    queries, key_rows, value_rows, grad_mix = parts
    scale = HD ** (-0.5)
    scores = (
        jnp.einsum("qhd,khd->hqk", queries, key_rows, preferred_element_type=jnp.float32) * scale
    )
    probs = jax.nn.softmax(scores, axis=-1)
    grad_values = jnp.einsum(
        "hqk,qhd->khd", probs.astype(jnp.bfloat16), grad_mix, preferred_element_type=jnp.float32
    ).astype(jnp.bfloat16)
    grad_probs = jnp.einsum(
        "qhd,khd->hqk", grad_mix, value_rows, preferred_element_type=jnp.float32
    )
    grad_scores = probs * (grad_probs - jnp.sum(probs * grad_probs, axis=-1, keepdims=True))
    grad_scores = grad_scores.astype(jnp.bfloat16)
    grad_queries = (
        jnp.einsum("hqk,khd->qhd", grad_scores, key_rows, preferred_element_type=jnp.float32)
        * scale
    ).astype(jnp.bfloat16)
    grad_keys = (
        jnp.einsum("hqk,qhd->khd", grad_scores, queries, preferred_element_type=jnp.float32) * scale
    ).astype(jnp.bfloat16)
    return (grad_queries, grad_keys, grad_values)


def forward_layer(stream, weight, gain_one, gain_two):
    row_count = stream.shape[0]
    normed = gather_rows(layer_norm(stream, gain_one).astype(jnp.bfloat16))
    all_rows = normed.shape[0]
    clip_count = all_rows // SEQ
    project = jnp.einsum(
        "rd,sde->sre", normed, weight[0:3], preferred_element_type=jnp.float32
    ).astype(jnp.bfloat16)
    mixture = lax.map(
        attend_clip,
        (
            heads_of(project[0], clip_count),
            heads_of(project[1], clip_count),
            heads_of(project[2], clip_count),
        ),
    )
    mixture = mixture.reshape(all_rows, -1)

    def attn_term(first_row, row_num):
        return lax.dot_general(
            mixture, weight[3], (((1,), (1,)), ((), ())), preferred_element_type=jnp.float32
        )

    resid_one = stream + branch_total(attn_term, row_count)
    normed_two = gather_rows(layer_norm(resid_one, gain_two).astype(jnp.bfloat16))
    upward = jnp.einsum("rd,jde->jre", normed_two, weight[4:8], preferred_element_type=jnp.float32)
    hidden = exact_gelu(upward).astype(jnp.bfloat16)

    def mlp_term(first_row, row_num):
        return jnp.einsum("jre,jde->rd", hidden, weight[8:12], preferred_element_type=jnp.float32)

    result = resid_one + branch_total(mlp_term, row_count)
    return (result, (stream, normed, project, mixture, resid_one, normed_two, upward, hidden))


def backward_layer(grad_out, saved, weight, gain_one, gain_two):
    stream, normed, project, mixture, resid_one, normed_two, upward, hidden = saved
    row_count = stream.shape[0]
    all_rows = normed.shape[0]
    clip_count = all_rows // SEQ
    back_mlp = gather_grads(grad_out.astype(jnp.bfloat16))
    grad_down = jnp.einsum("rd,jre->jde", back_mlp, hidden, preferred_element_type=jnp.float32)
    grad_hidden = jnp.einsum(
        "rd,jde->jre", back_mlp, weight[8:12], preferred_element_type=jnp.float32
    )
    gelu_out, gelu_back = jax.vjp(exact_gelu, upward)
    grad_upward = gelu_back(grad_hidden)[0].astype(jnp.bfloat16)
    grad_up = jnp.einsum("rd,jre->jde", normed_two, grad_upward, preferred_element_type=jnp.float32)

    def up_term(first_row, row_num):
        return jnp.einsum(
            "jre,jde->rd", grad_upward, weight[4:8], preferred_element_type=jnp.float32
        )

    grad_normed_two = input_total(up_term, row_count)
    norm_out, norm_back = jax.vjp(layer_norm, resid_one, gain_two)
    part_stream, grad_gain_two = norm_back(grad_normed_two)
    grad_resid = grad_out + part_stream
    back_attn = gather_grads(grad_resid.astype(jnp.bfloat16))
    grad_out_proj = lax.dot_general(
        back_attn, mixture, (((0,), (0,)), ((), ())), preferred_element_type=jnp.float32
    )
    grad_mixture = jnp.dot(back_attn, weight[3], preferred_element_type=jnp.float32).astype(
        jnp.bfloat16
    )
    grad_heads = lax.map(
        attend_back_clip,
        (
            heads_of(project[0], clip_count),
            heads_of(project[1], clip_count),
            heads_of(project[2], clip_count),
            heads_of(grad_mixture, clip_count),
        ),
    )
    grad_project = jnp.stack([piece.reshape(all_rows, -1) for piece in grad_heads])
    grad_qkv = jnp.einsum("rd,sre->sde", normed, grad_project, preferred_element_type=jnp.float32)

    def qkv_term(first_row, row_num):
        return jnp.einsum(
            "sre,sde->rd", grad_project, weight[0:3], preferred_element_type=jnp.float32
        )

    grad_normed = input_total(qkv_term, row_count)
    norm_out_one, norm_back_one = jax.vjp(layer_norm, stream, gain_one)
    part_in, grad_gain_one = norm_back_one(grad_normed)
    grad_matrix = jnp.concatenate([grad_qkv, grad_out_proj[None], grad_up, grad_down], axis=0)
    return (grad_resid + part_in, grad_matrix, grad_gain_one, grad_gain_two)


def masked_rows(mask_index, mask_count, row_count):
    positions = lax.iota(jnp.int32, SEQ)
    slots = lax.iota(jnp.int32, mask_index.shape[1])
    live = slots[None, :] < mask_count[:, None]
    hits = (mask_index[:, :, None] == positions[None, None, :]) & live[:, :, None]
    flag_all = jnp.any(hits, axis=1).astype(jnp.float32).reshape(-1)
    return lax.dynamic_slice_in_dim(flag_all, lax.axis_index("narrow") * row_count, row_count, 0)


def adam_step(weight_in, moment_one, moment_two, gradient, step_rate, decay_rate):
    moment_one = BETA_ONE * moment_one + (1.0 - BETA_ONE) * gradient
    moment_two = BETA_TWO * moment_two + (1.0 - BETA_TWO) * gradient * gradient
    first_hat = moment_one / (1.0 - BETA_ONE**STEP)
    second_hat = moment_two / (1.0 - BETA_TWO**STEP)
    updated = weight_in - step_rate * (
        first_hat / (jnp.sqrt(second_hat) + EPS_ADAM) + decay_rate * weight_in
    )
    return (updated, moment_one, moment_two)


def shards(
    patches,
    cotangent,
    mask_index,
    mask_count,
    weights,
    first_moment,
    second_moment,
    small_params,
    small_first,
    small_second,
):
    row_count = patches.shape[0]
    narrow_size = lax.axis_size("narrow")
    owned_rows = weights.shape[2]
    matrices, small_low = (
        lax.all_gather(weights.astype(jnp.bfloat16), "wide", axis=2, tiled=True),
        lax.all_gather(small_params.astype(jnp.bfloat16), "wide", axis=1, tiled=True),
    )
    gains = small_low.astype(jnp.float32)
    flags = masked_rows(mask_index, mask_count, row_count)[:, None]
    stream = patches.astype(jnp.float32) * (1.0 - flags) + flags * gains[2 * LAYERS][None, :]
    saved_all = []
    for layer_idx in range(LAYERS):
        stream, saved = forward_layer(
            stream, matrices[layer_idx], gains[2 * layer_idx], gains[2 * layer_idx + 1]
        )
        saved_all.append(saved)
    grad_stream = cotangent
    grad_mats = [None] * LAYERS
    grad_gains = [None] * (2 * LAYERS)
    for layer_idx in reversed(range(LAYERS)):
        (
            grad_stream,
            grad_mats[layer_idx],
            grad_gains[2 * layer_idx],
            grad_gains[2 * layer_idx + 1],
        ) = backward_layer(
            grad_stream,
            saved_all[layer_idx],
            matrices[layer_idx],
            gains[2 * layer_idx],
            gains[2 * layer_idx + 1],
        )
    input_grad = grad_stream * (1.0 - flags)
    grad_embed = jnp.sum(grad_stream * flags, axis=0)
    grad_small = jnp.stack(grad_gains + [grad_embed])
    grad_matrix = jnp.stack(grad_mats)
    first_col = lax.axis_index("wide") * owned_rows
    small_total = lax.psum(grad_small, ("wide", "narrow"))
    small_own = lax.dynamic_slice_in_dim(small_total, first_col, owned_rows, 1)
    matrix_total = lax.psum(grad_matrix, "wide")
    matrix_own = lax.dynamic_slice_in_dim(matrix_total, first_col, owned_rows, 2)
    local_square = jnp.sum(matrix_own * matrix_own) + jnp.sum(small_own * small_own) / narrow_size
    grad_norm = jnp.sqrt(lax.psum(local_square, ("wide", "narrow")))
    factor = jnp.minimum(1.0, CLIP_MAX / grad_norm)
    new_weights, new_first, new_second = adam_step(
        weights, first_moment, second_moment, matrix_own * factor, D ** (-0.5), DECAY_RATE
    )
    new_small, new_small_first, new_small_second = adam_step(
        small_params, small_first, small_second, small_own * factor, RATE_SMALL, 0.0
    )
    return (
        stream,
        input_grad,
        new_weights,
        new_first,
        new_second,
        new_small,
        new_small_first,
        new_small_second,
        grad_norm,
    )


def solution(mesh):
    in_specs = (
        P(("wide", "narrow"), None),
        P(("wide", "narrow"), None),
        P("wide", None),
        P("wide"),
        P(None, None, "wide", "narrow"),
        P(None, None, "wide", "narrow"),
        P(None, None, "wide", "narrow"),
        P(None, "wide"),
        P(None, "wide"),
        P(None, "wide"),
    )
    out_specs = (
        P(("wide", "narrow"), None),
        P(("wide", "narrow"), None),
        P(None, None, "wide", "narrow"),
        P(None, None, "wide", "narrow"),
        P(None, None, "wide", "narrow"),
        P(None, "wide"),
        P(None, "wide"),
        P(None, "wide"),
        P(),
    )
    return jax.shard_map(shards, mesh=mesh, in_specs=in_specs, out_specs=out_specs, check_vma=False)
```

profile of v0, /device:TPU:0, one launch (start us, length us, event | category | flops | bytes accessed | tf_op | source)
XLA Modules:
  0.0 1231.1 jit_solution(16849763134676933930)
XLA Ops:
  7.3 4.6 copy.301
  12.4 28.1 %all-gather = bf16[8,96,5]{1,2,0:T(8,128)(2,1)S(1)} all-gather(bf16[1,96,5]{1,2,0:T(8,128)(2,1)S(1)} %convert_bitcast_fusion.3), channel_id=1, replica_groups=mesh['wide'=8,'narrow'=4] {'wide'}, dimensions={0}, use_global_device_ids=true | all-gather | bytes 8640 | tf_op jit(solution)/shard_map/all_gather | solution.py:224
  43.3 109.5 %all-gather.13.cloned.1.call-done = bf16[2,12,768,192]{3,0,1,2:T(2,128)(2,1)} async-done(((bf16[2,12,96,192]{3,0,1,2:T(2,128)(2,1)}), bf16[2,12,768,192]{3,0,1,2:T(2,128)(2,1)}) %all-gather.13.cloned.1.call-update) | async-done | bytes 7077904 | tf_op jit(solution)/shard_map/all_gather | solution.py:223
  152.8 8.1 fusion.350
  160.9 4.4 copy.288
  165.3 7.6 all-gather.11.cloned.1.call-done
  176.9 10.3 while.48
  188.1 3.8 fusion.349
  194.2 28.3 %reduce-scatter.9.cloned.1.call-done = bf16[256,768]{1,0:T(8,128)(2,1)} async-done(((bf16[1024,768]{1,0:T(8,128)(2,1)}), bf16[256,768]{1,0:T(8,128)(2,1)}) %reduce-scatter.9.cloned.1.call-update) | async-done | bytes 393232 | tf_op jit(solution)/shard_map/reduce_scatter | solution.py:41
  227.8 14.5 %fusion.348 = (bf16[1,4,768,192]{3,0,1,2:T(2,128)(2,1)}, bf16[1,4,768,192]{3,0,1,2:T(2,128)(2,1)}, bf16[1,4,768,192]{3,0,1,2:T(2,128)(2,1)S(1)}, bf16[1,4,768,192]{3,0,1,2:T(2,128)(2,1)}) fusion(bf16[2,12,768,192]{3,0,1,2:T(2,128)(2,1)} %all-gather.13.cloned.1.call-done), kind=kLoop, calls=%fused_computation.367 | loop fusion | bytes 9437184 | tf_op jit(solution)/shard_map/slice | solution.py:127
  242.3 8.1 copy.290
  250.4 5.5 copy.291
  259.1 7.6 fusion.214
  270.6 28.3 %reduce-scatter.11.cloned.1.call-done = bf16[256,768]{1,0:T(8,128)(2,1)} async-done(((bf16[1024,768]{1,0:T(8,128)(2,1)}), bf16[256,768]{1,0:T(8,128)(2,1)}) %reduce-scatter.11.cloned.1.call-update) | async-done | bytes 393232 | tf_op jit(solution)/shard_map/reduce_scatter | solution.py:41
  301.5 6.4 copy.292
  308.4 12.9 %all-gather.17.cloned.1.call-done = bf16[1024,768]{1,0:T(8,128)(2,1)} async-done(((bf16[256,768]{1,0:T(8,128)(2,1)}), bf16[1024,768]{1,0:T(8,128)(2,1)}) %all-gather.17.cloned.1.call-update) | async-done | bytes 1572880 | tf_op jit(solution)/shard_map/all_gather | solution.py:33
  326.1 10.6 while.49
  340.3 27.9 %reduce-scatter.13.cloned.1.call-done = bf16[256,768]{1,0:T(8,128)(2,1)} async-done(((bf16[1024,768]{1,0:T(8,128)(2,1)}), bf16[256,768]{1,0:T(8,128)(2,1)}) %reduce-scatter.13.cloned.1.call-update) | async-done | bytes 393232 | tf_op jit(solution)/shard_map/reduce_scatter | solution.py:41
  371.4 8.2 copy.294
  379.6 8.1 copy.295
  395.2 7.7 fusion.212
  402.9 9.3 all-gather.21.cloned.1.call-done
  412.3 5.9 fusion.209
  422.0 4.3 bitcast_convert_fusion.4
  426.4 23.9 %reduce-scatter.17.cloned.1.call-done = bf16[256,768]{1,0:T(8,128)(2,1)} async-done(((bf16[1024,768]{1,0:T(8,128)(2,1)}), bf16[256,768]{1,0:T(8,128)(2,1)}) %reduce-scatter.17.cloned.1.call-update) | async-done | bytes 393232 | tf_op jit(solution)/shard_map/reduce_scatter | solution.py:50
  452.3 29.4 %reduce-scatter.15.cloned.1.call-done = bf16[256,768]{1,0:T(8,128)(2,1)} async-done(((bf16[1024,768]{1,0:T(8,128)(2,1)}), bf16[256,768]{1,0:T(8,128)(2,1)}) %reduce-scatter.15.cloned.1.call-update) | async-done | bytes 393232 | tf_op jit(solution)/shard_map/reduce_scatter | solution.py:41
  486.0 19.6 %all-gather.23.cloned.1.call-done = bf16[1024,768]{1,0:T(8,128)(2,1)} async-done(((bf16[256,768]{1,0:T(8,128)(2,1)}), bf16[1024,768]{1,0:T(8,128)(2,1)}) %all-gather.23.cloned.1.call-update) | async-done | bytes 1572880 | tf_op jit(solution)/shard_map/all_gather | solution.py:37
  511.1 16.1 %while.50 = (s32[]{:T(128)}, bf16[2,512,3,64]{1,3,2,0:T(8,128)(2,1)}, bf16[2,512,3,64]{1,3,2,0:T(8,128)(2,1)}, bf16[2,512,3,64]{1,3,2,0:T(8,128)(2,1)}, bf16[2,5...) while((s32[]{:T(128)}, ...), condition=%wide.region_28.29_spmd, body=%wide.region_24.28_spmd.sunk | while | flops 513244160 | bytes 36613408 | solution.py:163
  534.7 3.9 bitcast_convert_fusion.2
  538.7 28.2 %reduce-scatter.19.cloned.1.call-done = bf16[256,768]{1,0:T(8,128)(2,1)} async-done(((bf16[1024,768]{1,0:T(8,128)(2,1)}), bf16[256,768]{1,0:T(8,128)(2,1)}) %reduce-scatter.19.cloned.1.call-update) | async-done | bytes 393232 | tf_op jit(solution)/shard_map/reduce_scatter | solution.py:50
  572.7 19.5 %all-gather.25.cloned.1.call-done = bf16[1024,768]{1,0:T(8,128)(2,1)} async-done(((bf16[256,768]{1,0:T(8,128)(2,1)}), bf16[1024,768]{1,0:T(8,128)(2,1)}) %all-gather.25.cloned.1.call-update) | async-done | bytes 1572880 | tf_op jit(solution)/shard_map/all_gather | solution.py:37
  592.2 3.3 fusion.357
  601.1 28.3 %reduce-scatter.21.cloned.1.call-done = bf16[256,768]{1,0:T(8,128)(2,1)} async-done(((bf16[1024,768]{1,0:T(8,128)(2,1)}), bf16[256,768]{1,0:T(8,128)(2,1)}) %reduce-scatter.21.cloned.1.call-update) | async-done | bytes 393232 | tf_op jit(solution)/shard_map/reduce_scatter | solution.py:50
  635.0 4.7 convolution_bitcast_fusion.1
  639.7 15.0 %all-gather.27.cloned.1.call-done = bf16[1024,768]{1,0:T(8,128)(2,1)} async-done(((bf16[256,768]{1,0:T(8,128)(2,1)}), bf16[1024,768]{1,0:T(8,128)(2,1)}) %all-gather.27.cloned.1.call-update) | async-done | bytes 1572880 | tf_op jit(solution)/shard_map/all_gather | solution.py:37
  660.4 16.2 %while.51 = (s32[]{:T(128)}, bf16[2,512,3,64]{1,3,2,0:T(8,128)(2,1)}, bf16[2,512,3,64]{1,3,2,0:T(8,128)(2,1)}, bf16[2,512,3,64]{1,3,2,0:T(8,128)(2,1)}, bf16[2,5...) while((s32[]{:T(128)}, ...), condition=%wide.region_39.40_spmd, body=%wide.region_35.39_spmd.sunk | while | flops 513244160 | bytes 36613408 | solution.py:163
  684.0 3.9 bitcast_convert_fusion
  688.4 3.5 convolution_bitcast_fusion
  694.4 3.6 maximum_bitcast_fusion.1
  707.0 11.5 pad_maximum_fusion
  722.2 3.3 copy.273
  738.6 44.1 %psum.22 = f32[5,768]{1,0:T(8,128)S(1)} all-reduce(f32[5,768]{1,0:T(8,128)S(1)} %stack.31), channel_id=1, replica_groups=mesh['wide'=8,'narrow'=4] {'wide','narrow'}, use_global_device_ids=true, to_apply=%region_50.51 | all-reduce | flops 3840 | bytes 30720 | tf_op jit(solution)/shard_map/psum | solution.py:256
  784.0 374.3 %all-reduce.2.cloned.1.call-done = f32[2,12,768,192]{2,3,1,0:T(8,128)} async-done(((f32[2,12,768,192]{2,3,1,0:T(8,128)}), f32[2,12,768,192]{2,3,1,0:T(8,128)}) %all-reduce.2.cloned.1.call-update) | async-done | bytes 14155792 | tf_op jit(solution)/shard_map/psum | solution.py:258
  1158.2 3.6 multiply_reduce_fusion.6
  1164.6 39.5 %psum.23 = f32[]{:T(128)} all-reduce(f32[]{:T(128)S(6)} %add.160), channel_id=1, replica_groups=mesh['wide'=8,'narrow'=4] {'wide','narrow'}, use_global_device_ids=true, to_apply=%region_52.53 | all-reduce | flops 1 | bytes 8 | tf_op jit(solution)/shard_map/psum | solution.py:261
  1204.8 8.7 multiply_subtract_fusion
  1213.5 3.2 copy.277
  1216.7 3.4 copy.278
  (428 shorter events, 184.4 us)
Async XLA Ops:
  7.2 34.1 %copy-start = (bf16[256,768]{1,0:T(8,128)(2,1)S(1)}, bf16[256,768]{1,0:T(8,128)(2,1)}, u32[]{:S(2)}) copy-start(bf16[256,768]{1,0:T(8,128)(2,1)} %param.18) | copy-start | bytes 1179652
  7.2 145.6 %all-gather.13.cloned.1.call-start = ((), (), s32[]{:S(2)}) async-start(), calls=%async_computation.9 | async-start | bytes 10616832 | tf_op jit(solution)/shard_map/all_gather | solution.py:223
  11.8 161.0 %all-gather.11.cloned.1.call-start = ((), (), s32[]{:S(2)}) async-start(), calls=%async_computation.8 | async-start | bytes 1966080 | tf_op jit(solution)/shard_map/all_gather | solution.py:33
  40.6 258.2 %copy-start.58 = (f32[256]{0:T(256)}, f32[256]{0:T(256)S(1)}, u32[]{:S(2)}) copy-start(f32[256]{0:T(256)S(1)} %get-tuple-element.457) | copy-start | bytes 3076
  41.3 119.6 %copy-start.63 = (f32[768]{0:T(1024)}, f32[768]{0:T(1024)S(1)}, u32[]{:S(2)}) copy-start(f32[768]{0:T(1024)S(1)} %get-tuple-element.380) | copy-start | bytes 9220
  41.3 184.0 %copy-start.67 = (f32[768]{0:T(1024)}, f32[768]{0:T(1024)S(1)}, u32[]{:S(2)}) copy-start(f32[768]{0:T(1024)S(1)} %get-tuple-element.379) | copy-start | bytes 9220
  41.5 119.4 %copy-start.70 = (f32[256]{0:T(256)}, f32[256]{0:T(256)S(1)}, u32[]{:S(2)}) copy-start(f32[256]{0:T(256)S(1)} %broadcast_multiply_fusion.4) | copy-start | bytes 3076
  41.9 119.0 %copy-start.84 = (f32[256]{0:T(256)}, f32[256]{0:T(256)S(1)}, u32[]{:S(2)}) copy-start(f32[256]{0:T(256)S(1)} %multiply_reduce_fusion.11) | copy-start | bytes 3076
  41.9 119.0 %copy-start.75 = (f32[256]{0:T(256)}, f32[256]{0:T(256)S(1)}, u32[]{:S(2)}) copy-start(f32[256]{0:T(256)S(1)} %fusion.296) | copy-start | bytes 3076
  43.1 179.4 %reduce-scatter.9.cloned.1.call-start = ((), (), s32[]{:S(2)}) async-start(), calls=%async_computation.10 | async-start | bytes 1966080 | tf_op jit(solution)/shard_map/reduce_scatter | solution.py:41
  192.4 35.2 %copy-start.48 = (bf16[1,1,768,192]{2,3,1,0:T(8,128)(2,1)}, bf16[1,1,768,192]{2,3,1,0:T(8,128)(2,1)S(1)}, u32[]{:S(2)}) copy-start(bf16[1,1,768,192]{2,3,1,0:T(8,128)(2,1)S(1)} %copy.289) | copy-start | bytes 884740
  194.2 61.8 %all-gather.15.cloned.1.call-start = ((), (), s32[]{:S(2)}) async-start(), calls=%async_computation.11 | async-start | bytes 1966080 | tf_op jit(solution)/shard_map/all_gather | solution.py:33
  227.6 71.3 %reduce-scatter.11.cloned.1.call-start = ((), (), s32[]{:S(2)}) async-start(), calls=%async_computation.12 | async-start | bytes 1966080 | tf_op jit(solution)/shard_map/reduce_scatter | solution.py:41
  267.9 31.0 %copy-start.3 = (bf16[256,768]{1,0:T(8,128)(2,1)S(1)}, bf16[256,768]{1,0:T(8,128)(2,1)}, u32[]{:S(2)}) copy-start(bf16[256,768]{1,0:T(8,128)(2,1)} %reduce-scatter.9.cloned.1.call-done) | copy-start | bytes 1179652
  270.5 30.1 %copy-start.65 = (f32[768]{0:T(1024)S(1)}, f32[768]{0:T(1024)}, u32[]{:S(2)}) copy-start(f32[768]{0:T(1024)} %get-tuple-element.378) | copy-start | bytes 9220
  270.5 50.8 %all-gather.17.cloned.1.call-start = ((), (), s32[]{:S(2)}) async-start(), calls=%async_computation.13 | async-start | bytes 1966080 | tf_op jit(solution)/shard_map/all_gather | solution.py:33
  300.2 67.9 %copy-start.1 = (f32[256,768]{1,0:T(8,128)}, f32[256,768]{1,0:T(8,128)S(1)}, u32[]{:S(2)}) copy-start(f32[256,768]{1,0:T(8,128)S(1)} %get-tuple-element.453) | copy-start | bytes 2359300
  300.5 23.6 %copy-start.87 = (f32[256]{0:T(256)}, f32[256]{0:T(256)S(1)}, u32[]{:S(2)}) copy-start(f32[256]{0:T(256)S(1)} %multiply_reduce_fusion.9) | copy-start | bytes 3076
  301.5 66.7 %reduce-scatter.13.cloned.1.call-start = ((), (), s32[]{:S(2)}) async-start(), calls=%async_computation.14 | async-start | bytes 1966080 | tf_op jit(solution)/shard_map/reduce_scatter | solution.py:41
  338.0 31.5 %copy-start.69 = (f32[768]{0:T(1024)S(1)}, f32[768]{0:T(1024)}, u32[]{:S(2)}) copy-start(f32[768]{0:T(1024)} %get-tuple-element.377) | copy-start | bytes 9220
  339.8 30.8 %copy-start.11 = (f32[256,768]{1,0:T(8,128)S(1)}, f32[256,768]{1,0:T(8,128)}, u32[]{:S(2)}) copy-start(f32[256,768]{1,0:T(8,128)} %param.19) | copy-start | bytes 2359300
  339.8 50.5 %all-gather.19.cloned.1.call-start = ((), (), s32[]{:S(2)}) async-start(), calls=%async_computation.15 | async-start | bytes 1966080 | tf_op jit(solution)/shard_map/all_gather | solution.py:33
  370.5 41.7 %all-gather.21.cloned.1.call-start = ((), (), s32[]{:S(2)}) async-start(), calls=%async_computation.17 | async-start | bytes 1966080 | tf_op jit(solution)/shard_map/all_gather | solution.py:37
  371.4 78.9 %reduce-scatter.17.cloned.1.call-start = ((), (), s32[]{:S(2)}) async-start(), calls=%async_computation.18 | async-start | bytes 1966080 | tf_op jit(solution)/shard_map/reduce_scatter | solution.py:50
  421.9 59.7 %reduce-scatter.15.cloned.1.call-start = ((), (), s32[]{:S(2)}) async-start(), calls=%async_computation.16 | async-start | bytes 1966080 | tf_op jit(solution)/shard_map/reduce_scatter | solution.py:41
  426.3 79.2 %all-gather.23.cloned.1.call-start = ((), (), s32[]{:S(2)}) async-start(), calls=%async_computation.19 | async-start | bytes 1966080 | tf_op jit(solution)/shard_map/all_gather | solution.py:37
  483.9 25.6 %copy-start.83 = (f32[256]{0:T(256)}, f32[256]{0:T(256)S(1)}, u32[]{:S(2)}) copy-start(f32[256]{0:T(256)S(1)} %negate_multiply_fusion.5) | copy-start | bytes 3076
  485.8 81.2 %reduce-scatter.19.cloned.1.call-start = ((), (), s32[]{:S(2)}) async-start(), calls=%async_computation.20 | async-start | bytes 1966080 | tf_op jit(solution)/shard_map/reduce_scatter | solution.py:50
  534.7 32.3 %copy-start.2 = (f32[256,768]{1,0:T(8,128)S(1)}, f32[256,768]{1,0:T(8,128)}, u32[]{:S(2)}) copy-start(f32[256,768]{1,0:T(8,128)} %copy-done.1) | copy-start | bytes 2359300
  534.7 32.3 %copy-start.66 = (f32[768]{0:T(1024)S(1)}, f32[768]{0:T(1024)}, u32[]{:S(2)}) copy-start(f32[768]{0:T(1024)} %get-tuple-element.378) | copy-start | bytes 9220
  534.7 32.3 %copy-start.72 = (f32[256]{0:T(256)S(1)}, f32[256]{0:T(256)}, u32[]{:S(2)}) copy-start(f32[256]{0:T(256)} %copy-done.71) | copy-start | bytes 3076
  534.7 33.5 %copy-start.88 = (f32[256]{0:T(256)S(1)}, f32[256]{0:T(256)}, u32[]{:S(2)}) copy-start(f32[256]{0:T(256)} %copy-done.87) | copy-start | bytes 3076
  534.7 33.5 %copy-start.77 = (f32[256]{0:T(256)S(1)}, f32[256]{0:T(256)}, u32[]{:S(2)}) copy-start(f32[256]{0:T(256)} %copy-done.76) | copy-start | bytes 3076
  538.6 31.7 %copy-start.12 = (f32[256,768]{1,0:T(8,128)S(1)}, f32[256,768]{1,0:T(8,128)}, u32[]{:S(2)}) copy-start(f32[256,768]{1,0:T(8,128)} %param.19) | copy-start | bytes 2359300
  538.6 31.7 %copy-start.17 = (f32[256,768]{1,0:T(8,128)S(1)}, f32[256,768]{1,0:T(8,128)}, u32[]{:S(2)}) copy-start(f32[256,768]{1,0:T(8,128)} %copy-done.16) | copy-start | bytes 2359300
  538.7 53.6 %all-gather.25.cloned.1.call-start = ((), (), s32[]{:S(2)}) async-start(), calls=%async_computation.21 | async-start | bytes 1966080 | tf_op jit(solution)/shard_map/all_gather | solution.py:37
  572.4 60.8 %copy-start.15 = (f32[256,768]{1,0:T(8,128)}, f32[256,768]{1,0:T(8,128)S(1)}, u32[]{:S(2)}) copy-start(f32[256,768]{1,0:T(8,128)S(1)} %get-tuple-element.445) | copy-start | bytes 2359300
  572.4 57.0 %reduce-scatter.21.cloned.1.call-start = ((), (), s32[]{:S(2)}) async-start(), calls=%async_computation.22 | async-start | bytes 1966080 | tf_op jit(solution)/shard_map/reduce_scatter | solution.py:50
  598.4 31.0 %copy-start.4 = (bf16[256,768]{1,0:T(8,128)(2,1)S(1)}, bf16[256,768]{1,0:T(8,128)(2,1)}, u32[]{:S(2)}) copy-start(bf16[256,768]{1,0:T(8,128)(2,1)} %reduce-scatter.9.cloned.1.call-done) | copy-start | bytes 1179652
  598.4 31.0 %copy-start.59 = (f32[256]{0:T(256)S(1)}, f32[256]{0:T(256)}, u32[]{:S(2)}) copy-start(f32[256]{0:T(256)} %copy-done.58) | copy-start | bytes 3076
  598.4 31.0 %copy-start.68 = (f32[768]{0:T(1024)S(1)}, f32[768]{0:T(1024)}, u32[]{:S(2)}) copy-start(f32[768]{0:T(1024)} %copy-done.67) | copy-start | bytes 9220
  598.4 31.0 %copy-start.74 = (f32[256]{0:T(256)S(1)}, f32[256]{0:T(256)}, u32[]{:S(2)}) copy-start(f32[256]{0:T(256)} %copy-done.73) | copy-start | bytes 3076
  598.4 31.0 %copy-start.81 = (f32[256]{0:T(256)S(1)}, f32[256]{0:T(256)}, u32[]{:S(2)}) copy-start(f32[256]{0:T(256)} %copy-done.80) | copy-start | bytes 3076
  598.4 33.2 %copy-start.86 = (f32[256]{0:T(256)S(1)}, f32[256]{0:T(256)}, u32[]{:S(2)}) copy-start(f32[256]{0:T(256)} %copy-done.85) | copy-start | bytes 3076
  601.1 53.7 %all-gather.27.cloned.1.call-start = ((), (), s32[]{:S(2)}) async-start(), calls=%async_computation.23 | async-start | bytes 1966080 | tf_op jit(solution)/shard_map/all_gather | solution.py:37
  635.0 96.4 %reduce-scatter.23.cloned.1.call-start = ((), (), s32[]{:S(2)}) async-start(), calls=%async_computation.24 | async-start | bytes 1966080 | tf_op jit(solution)/shard_map/reduce_scatter | solution.py:50
  687.9 470.3 %all-reduce.2.cloned.1.call-start = ((), (), s32[]{:S(2)}) async-start(), calls=%async_computation.25 | async-start | bytes 28311552 | tf_op jit(solution)/shard_map/psum | solution.py:258
  735.0 469.8 %copy-start.9 = (f32[2,12,96,192]{2,3,1,0:T(8,128)S(1)}, f32[2,12,96,192]{2,3,1,0:T(8,128)}, u32[]{:S(2)}) copy-start(f32[2,12,96,192]{2,3,1,0:T(8,128)} %copy.276) | copy-start | bytes 5308420
  (82 other events, 294.4 us)
Sparse Core Ops, SparseCore 0:
  12.0 140.8 all-gather.12
  155.0 17.8 all-gather.10
  194.3 28.1 reduce-scatter.8
  227.7 19.6 all-gather.14
  270.6 28.1 reduce-scatter.10
  301.6 19.6 all-gather.16
  340.0 28.1 reduce-scatter.12
  370.6 19.6 all-gather.18
  392.6 19.6 all-gather.20
  422.1 28.1 reduce-scatter.16
  453.4 28.1 reduce-scatter.14
  485.9 19.6 all-gather.22
  538.8 28.1 reduce-scatter.18
  572.5 19.6 all-gather.24
  601.2 28.1 reduce-scatter.20
  635.1 19.6 all-gather.26
  688.0 28.1 reduce-scatter.22
  720.1 438.0 all-reduce.1
where the time goes:
time: 1240 us; the launch traced here: 1230 us
  waiting for transfers between devices  765 us (62%)
  local copies, waits for them, and re-layouts  136 us (11%)
  blocking collectives  112 us (9%)
  matrix products  108 us (9%)
  other arithmetic  89 us (7%)
  between operations  18.8 us (2%)
    psum x1, waiting for transfers between devices, shards(): matrix_total = lax.psum(grad_matrix, 'wide')  374 us
    reduce_scatter x4, waiting for transfers between devices, branch_total(): lax.psum_scatter(term(jnp.int32(0), row_count * lax.axis_size('narrow'))....  114 us
    all_gather x1, waiting for transfers between devices, shards(): lax.all_gather(weights.astype(jnp.bfloat16), 'wide', axis=2, tiled=True)  110 us
    reduce_scatter x4, waiting for transfers between devices, input_total(): lax.psum_scatter(term(jnp.int32(0), row_count * lax.axis_size('narrow'))....  80.4 us
    unnamed x190, local copies, waits for them, and re-layouts  78 us
    all_gather x4, waiting for transfers between devices, gather_grads(): return lax.all_gather(share, 'narrow', axis=0, tiled=True)  63.5 us
    psum x1, blocking collectives, shards(): small_total = lax.psum(grad_small, ('wide', 'narrow'))  44.1 us
    psum x1, blocking collectives, shards(): grad_norm = jnp.sqrt(lax.psum(local_square, ('wide', 'narrow')))  39.5 us
  transfers between devices with their start and end apart: 18, of which 16 were waited for; matrix products, arithmetic and copies ran while one was open for 11% of the time, Pallas kernels for 0%

commit v1 on v0

--- a/solution.py
+++ b/solution.py
@@ -1,6 +1,10 @@
+import functools
+
 import jax
 import jax.numpy as jnp
 from jax import lax
+from jax.experimental import pallas as pl
+from jax.experimental.pallas import tpu as pltpu
 from jax.sharding import PartitionSpec as P
 
 D = 768
@@ -8,7 +12,6 @@
 LAYERS = 2
 SEQ = 512
 STEP = 10
-
 
 EPS_NORM = 1e-06
 BETA_ONE = 0.9
@@ -17,6 +20,814 @@
 DECAY_RATE = 0.05
 RATE_SMALL = 0.6
 CLIP_MAX = 1.0
+
+MESH = pl.DeviceIdType.MESH
+F32 = jnp.float32
+BF16 = jnp.bfloat16
+
+PAIRS = 12
+PER = 6
+NZ, NX = 4, 2
+ROWS = 96
+HALF = 48
+COL = 192
+WIDE = 2 * COL
+SCALE = HD ** (-0.5)
+TM = 256
+TR = 64
+HEADS_Y = COL // HD
+
+LEAD_ONE, LEAD_TWO, LEAD_THREE = 5, 3, 1
+LAG_TWO, LAG_THREE, LAG_LAST = 1, 2, 3
+
+
+def mm(a, b):
+    return lax.dot_general(a, b, (((1,), (0,)), ((), ())), preferred_element_type=F32)
+
+
+def mm_nt(a, b):
+    return lax.dot_general(a, b, (((1,), (1,)), ((), ())), preferred_element_type=F32)
+
+
+def mm_tn(a, b):
+    return lax.dot_general(a, b, (((0,), (0,)), ((), ())), preferred_element_type=F32)
+
+
+def loop(count, body):
+    def wrapped(i, carry):
+        body(i)
+        return carry
+
+    lax.fori_loop(0, count, wrapped, 0)
+
+
+def rows_at(i, size):
+    return pl.ds(pl.multiple_of(i * size, size), size)
+
+
+def step_kernel(
+    wloc, patch, cot, mask_index, mask_count, small,
+    out_block, out_igrad, out_grad, out_small, out_norm,
+    G, S, R1, NRM, NRM2, QK, V, MIX, GP, HID, GR, ACC, XS, XR, BK, TA, TB, GU, GM, DQK, DV,
+    FL, GAIN, GPIECE, SG, SR, NB, RB0Y, RB0X, RB1, RB2,
+    ag_s, ag_r, rs_s, rs_r, ex_s, ex_r, in_s, in_r, lc_s, gn_s, gn_r, fs_s, fs_r, nm_s, nm_r,
+):
+    wide = lax.axis_index("wide")
+    narrow = lax.axis_index("narrow")
+    z, x = wide // NX, wide % NX
+    y, c = narrow // 2, narrow % 2
+
+    dev_core = (wide, 2 * y + 1 - c)
+    dev_x = (z * NX + 1 - x, narrow)
+    dev_y = (wide, 2 * (1 - y) + c)
+
+    def z_to(k):
+        return (z + k) % NZ
+
+    def z_from(k):
+        return (z + NZ - k) % NZ
+
+    def dev_z(k):
+        return (z_to(k) * NX + x, narrow)
+
+    barrier = pltpu.get_barrier_semaphore()
+    for dev in [dev_core, dev_x, dev_y] + [dev_z(k) for k in range(1, NZ)]:
+        pl.semaphore_signal(barrier, inc=1, device_id=dev, device_id_type=MESH)
+    pl.semaphore_wait(barrier, 3 + NZ - 1)
+
+    def remote(src, dst, send, recv, dev):
+        return pltpu.make_async_remote_copy(
+            src_ref=src, dst_ref=dst, send_sem=send, recv_sem=recv, device_id=dev, device_id_type=MESH
+        )
+
+    def lazy(*what):
+        return lambda: remote(*what)
+
+    ALL = slice(None)
+    partners = {
+        "x": [(3, dev_x, 1 - x, 1 - x)],
+        "y": [(4, dev_y, 1 - y, 1 - y)],
+        "z": [(k - 1, dev_z(k), z_to(k), z_from(k)) for k in range(1, NZ)],
+    }
+    own = {"x": x, "y": y, "z": z}
+
+    def block(p, h, where):
+        return G.at[p, where["y"], where["z"], where["x"], h]
+
+    def gather_order(z_first, h):
+        a, b = ("x", "y") if h == 0 else ("y", "x")
+        return ("z", a, b) if z_first else (a, "z", b)
+
+    def gather_copies(p, h, order, phase):
+        axis = order[phase]
+        have = {q: (ALL if q in order[:phase] else own[q]) for q in own}
+        src = block(p, h, have)
+        sends, recvs = [], []
+        for slot, dev, _, frm in partners[axis]:
+            sends.append(lazy(src, src, ag_s.at[p, h, slot], ag_r.at[p, h, slot], dev))
+            got = block(p, h, {**have, axis: frm})
+            recvs.append(lazy(got, got, ag_s.at[p, h, slot], ag_r.at[p, h, slot], dev))
+        return sends, recvs
+
+    def by_kind(slot_index, action):
+        z_second = (slot_index % 3) == 2
+
+        @pl.when(jnp.logical_not(z_second))
+        def _():
+            action(True)
+
+        @pl.when(z_second)
+        def _():
+            action(False)
+
+    def gather_issue(p, phase):
+        def action(z_first):
+            for h in range(2):
+                order = gather_order(z_first, h)
+                if phase > 0:
+                    for r in gather_copies(p, h, order, phase - 1)[1]:
+                        r().wait_recv()
+                if phase < 3:
+                    for s in gather_copies(p, h, order, phase)[0]:
+                        s().start()
+
+        by_kind(p % PER, action)
+
+    def gather_sent(p):
+        def action(z_first):
+            for h in range(2):
+                for phase in range(3):
+                    for s in gather_copies(p, h, gather_order(z_first, h), phase)[0]:
+                        s().wait_send()
+
+        by_kind(p % PER, action)
+
+    for p in range(PAIRS):
+        for h in range(2):
+            G[p, y, z, x, h] = wloc[p, h]
+
+    half = TM * c
+    BKh = BK.at[pl.ds(pl.multiple_of(half, TM), TM)]
+    GRh = GR.at[pl.ds(pl.multiple_of(half, TM), TM)]
+    other = TM * (1 - c)
+    BKo = BK.at[pl.ds(pl.multiple_of(other, TM), TM)]
+    GRo = GR.at[pl.ds(pl.multiple_of(other, TM), TM)]
+    patch_out = remote(patch, BKh, in_s.at[0], in_r.at[0], dev_core)
+    patch_in = remote(patch, BKo, in_s.at[0], in_r.at[0], dev_core)
+    cot_out = remote(cot, GRh, in_s.at[1], in_r.at[1], dev_core)
+    cot_in = remote(cot, GRo, in_s.at[1], in_r.at[1], dev_core)
+    patch_own = pltpu.make_async_copy(patch, BKh, lc_s.at[0])
+    cot_own = pltpu.make_async_copy(cot, GRh, lc_s.at[1])
+    patch_own.start()
+    cot_own.start()
+    patch_out.start()
+    GPIECE[z, x] = jnp.zeros((8, 128), F32)
+    GPIECE[z, x, 0:5, 0:ROWS] = small[...].astype(BF16).astype(F32)
+    gain_z = [
+        (
+            remote(GPIECE.at[z, x], GPIECE.at[z, x], gn_s.at[k - 1], gn_r.at[k - 1], dev_z(k)),
+            remote(GPIECE.at[z_from(k), x], GPIECE.at[z_from(k), x], gn_s.at[k - 1], gn_r.at[k - 1], dev_z(k)),
+        )
+        for k in range(1, NZ)
+    ]
+    gain_x = (
+        remote(GPIECE.at[:, x], GPIECE.at[:, x], gn_s.at[3], gn_r.at[3], dev_x),
+        remote(GPIECE.at[:, 1 - x], GPIECE.at[:, 1 - x], gn_s.at[3], gn_r.at[3], dev_x),
+    )
+    for s, _ in gain_z:
+        s.start()
+    for p in range(LEAD_ONE):
+        gather_issue(p, 0)
+    cot_out.start()
+
+    index_row = mask_index[pl.ds(y, 1), :]
+    count = mask_count[y]
+    spot = lax.broadcasted_iota(jnp.int32, (SEQ, index_row.shape[1]), 0)
+    live = lax.broadcasted_iota(jnp.int32, (1, index_row.shape[1]), 1) < count
+    hits = jnp.where(jnp.logical_and(spot == index_row, live), 1.0, 0.0)
+    FL[...] = jnp.max(hits, axis=1, keepdims=True)
+
+    for _, r in gain_z:
+        r.wait_recv()
+    gain_x[0].start()
+    gain_x[1].wait_recv()
+    lane = lax.broadcasted_iota(jnp.int32, (128, D), 0)
+    feature = lax.broadcasted_iota(jnp.int32, (128, D), 1)
+    gains = jnp.zeros((8, D), F32)
+    for zz in range(NZ):
+        for xx in range(NX):
+            place = jnp.logical_and(feature - ROWS * (zz * NX + xx) == lane, lane < ROWS)
+            gains = gains + mm(GPIECE[zz, xx].astype(BF16), jnp.where(place, 1.0, 0.0).astype(BF16))
+    GAIN[...] = gains
+
+    patch_own.wait()
+    patch_in.wait_recv()
+    embed = GAIN[4:5, :]
+
+    def mask_tile(i):
+        rows = rows_at(i, TR)
+        flag = FL[rows, :]
+        S[0, rows, :] = BK[rows, :].astype(F32) * (1.0 - flag) + flag * embed
+
+    loop(SEQ // TR, mask_tile)
+
+    def norm_parts(values):
+        centre = values - jnp.mean(values, axis=-1, keepdims=True)
+        spread = jnp.mean(centre * centre, axis=-1, keepdims=True)
+        return centre, lax.rsqrt(spread + EPS_NORM)
+
+    def norm_into(dst, src, gain_row):
+        gain = GAIN[pl.ds(gain_row, 1), :]
+
+        def tile(i):
+            rows = rows_at(i, TR)
+            centre, inv = norm_parts(src[rows, :])
+            dst[rows, :] = (centre * inv * gain).astype(BF16)
+
+        loop(SEQ // TR, tile)
+
+    def matrix(p, yy):
+        return G[p, yy].reshape(D, WIDE)
+
+    def exchange(e, make, take):
+        par = e % 2
+
+        def copies(i, par):
+            rows = rows_at(i, TM)
+            return remote(XS.at[rows], XR.at[par, rows], ex_s.at[i], ex_r.at[par, i], dev_core)
+
+        def give(i):
+            XS[rows_at(i, TM), :] = make(i).astype(BF16)
+            copies(i, par).start()
+
+        loop(SEQ // TM, give)
+
+        def receive(i):
+            copies(i, par).wait_recv()
+
+            def tile(j):
+                rows = pl.ds(pl.multiple_of(i * TM + j * TR, TR), TR)
+                take(rows, XS[rows, :].astype(F32) + XR[par, rows, :].astype(F32))
+
+            loop(TM // TR, tile)
+
+        loop(SEQ // TM, receive)
+        loop(SEQ // TM, lambda i: copies(i, par).wait_send())
+
+    def attend(l, yy):
+        def tile(i):
+            rows = rows_at(i, TM)
+            outs = []
+            for hd in range(HEADS_Y):
+                lo = hd * HD
+                q = QK[l, yy, rows, lo : lo + HD]
+                k = QK[l, yy, :, COL + lo : COL + lo + HD]
+                v = V[l, yy, :, lo : lo + HD]
+                s = mm_nt(q, k) * SCALE
+                e = jnp.exp(s - jnp.max(s, axis=1, keepdims=True))
+                probs = e / jnp.sum(e, axis=1, keepdims=True)
+                outs.append(mm(probs.astype(BF16), v))
+            MIX[l, yy, rows, :] = jnp.concatenate(outs, axis=1).astype(BF16)
+
+        loop(SEQ // TM, tile)
+
+    def attend_back(l, yy):
+        for hd in range(HEADS_Y):
+            lo = hd * HD
+            k = QK[l, yy, :, COL + lo : COL + lo + HD]
+            v = V[l, yy, :, lo : lo + HD]
+
+            def tile(i, carry):
+                dk, dv = carry
+                rows = rows_at(i, TM)
+                q = QK[l, yy, rows, lo : lo + HD]
+                dm = GM[yy, rows, lo : lo + HD]
+                s = mm_nt(k, q) * SCALE
+                e = jnp.exp(s - jnp.max(s, axis=0, keepdims=True))
+                probs = e / jnp.sum(e, axis=0, keepdims=True)
+                dp = mm_nt(v, dm)
+                ds = probs * (dp - jnp.sum(probs * dp, axis=0, keepdims=True))
+                ds = ds.astype(BF16)
+                dv = dv + mm(probs.astype(BF16), dm)
+                dk = dk + mm(ds, q)
+                dq = mm_tn(ds, k) * SCALE
+                DQK[yy, rows, lo : lo + HD] = dq.astype(BF16)
+                return dk, dv
+
+            zero = jnp.zeros((SEQ, HD), F32)
+            dk, dv = lax.fori_loop(0, SEQ // TM, tile, (zero, zero))
+            DQK[yy, :, COL + lo : COL + lo + HD] = (dk * SCALE).astype(BF16)
+            DV[yy, :, lo : lo + HD] = dv.astype(BF16)
+
+    def forward_slot(slot, l):
+        p = l * PER + slot
+        if slot == 0:
+            norm_into(NRM.at[l], S.at[l], 2 * l)
+
+            def project(yy):
+                def tile(i):
+                    rows = rows_at(i, TM)
+                    QK[l, yy, rows, :] = mm(NRM[l, rows, :], matrix(p, yy)).astype(BF16)
+
+                loop(SEQ // TM, tile)
+
+            loop(2, project)
+        elif slot == 1:
+
+            def project_v(yy):
+                def tile(i):
+                    rows = rows_at(i, TM)
+                    V[l, yy, rows, :] = mm(NRM[l, rows, :], matrix(p, yy)[:, :COL]).astype(BF16)
+
+                loop(SEQ // TM, tile)
+                attend(l, yy)
+
+            loop(2, project_v)
+
+            def make(i):
+                rows = rows_at(i, TM)
+                total = mm_nt(MIX[l, 0, rows, :], matrix(p, 0)[:, COL:])
+                return total + mm_nt(MIX[l, 1, rows, :], matrix(p, 1)[:, COL:])
+
+            def take(rows, total):
+                R1[l, rows, :] = S[l, rows, :] + total
+
+            exchange(0, make, take)
+        elif slot in (2, 3):
+            u = slot - 2
+            if u == 0:
+                norm_into(NRM2.at[l], R1.at[l], 2 * l + 1)
+
+            def project_up(yy):
+                def tile(i):
+                    rows = rows_at(i, TM)
+                    ACC[rows, 0:WIDE] = mm(NRM2[l, rows, :], matrix(p, yy))
+
+                loop(SEQ // TM, tile)
+
+                def gelu(i):
+                    rows = rows_at(i, TR)
+                    v = ACC[rows, 0:WIDE]
+                    cdf = 0.5 * (1.0 + lax.erf(v * (2.0 ** -0.5)))
+                    HID[l, u, yy, rows, :] = (v * cdf).astype(BF16)
+                    pdf = jnp.exp(-0.5 * v * v) * 0.3989422804014327
+                    GP[l, u, yy, rows, :] = (cdf + v * pdf).astype(BF16)
+
+                loop(SEQ // TR, gelu)
+
+            loop(2, project_up)
+        elif slot == 4:
+
+            def down(i):
+                rows = rows_at(i, TM)
+                total = mm_nt(HID[l, 0, 0, rows, :], matrix(p, 0))
+                ACC[rows, :] = total + mm_nt(HID[l, 0, 1, rows, :], matrix(p, 1))
+
+            loop(SEQ // TM, down)
+        else:
+
+            def make(i):
+                rows = rows_at(i, TM)
+                total = ACC[rows, :] + mm_nt(HID[l, 1, 0, rows, :], matrix(p, 0))
+                return total + mm_nt(HID[l, 1, 1, rows, :], matrix(p, 1))
+
+            def take(rows, total):
+                value = R1[l, rows, :] + total
+
+                @pl.when(l == 0)
+                def _():
+                    S[1, rows, :] = value
+
+                @pl.when(l == 1)
+                def _():
+                    ACC[rows, :] = value
+
+            exchange(1, make, take)
+
+    def forward_tick(t):
+        for lead, phase in ((LEAD_ONE, 0), (LEAD_TWO, 1), (LEAD_THREE, 2)):
+
+            @pl.when(jnp.logical_and(t + lead >= (LEAD_ONE if phase == 0 else 0), t + lead < PAIRS))
+            def _():
+                gather_issue(t + lead, phase)
+
+        @pl.when(t >= 0)
+        def _():
+            gather_issue(t, 3)
+            for slot in range(PER):
+
+                @pl.when(t % PER == slot)
+                def _():
+                    forward_slot(slot, t // PER)
+
+    lead_in = LEAD_TWO
+
+    loop(PAIRS + lead_in, lambda i: forward_tick(i - lead_in))
+
+    block_copy = pltpu.make_async_copy(ACC.at[pl.ds(pl.multiple_of(half, TM), TM)], out_block, lc_s.at[2])
+    block_copy.start()
+    loop(PAIRS, gather_sent)
+    for s, _ in gain_z:
+        s.wait_send()
+    gain_x[0].wait_send()
+    patch_out.wait_send()
+    block_copy.wait()
+
+    def scatter_copies(p, h, z_first, phase):
+        order = gather_order(z_first, h)[::-1]
+        axis = order[phase]
+        have = {q: (own[q] if q in order[:phase] else ALL) for q in own}
+        sends, recvs = [], []
+        for slot, dev, to, _ in partners[axis]:
+            src = block(p, h, {**have, axis: to})
+            if phase == 0:
+                dst = (RB0Y if h == 0 else RB0X).at[p]
+            elif phase == 1:
+                dst = RB1.at[p, h, pl.ds(2 * slot, 2)] if axis == "z" else RB1.at[p, h, pl.ds(0, NZ)]
+            else:
+                dst = RB2.at[p, h, slot] if axis == "z" else RB2.at[p, h, 0]
+            sends.append(lazy(src, dst, rs_s.at[p, h, slot], rs_r.at[p, h, slot], dev))
+            recvs.append((dst, lazy(dst, dst, rs_s.at[p, h, slot], rs_r.at[p, h, slot], dev)))
+        return sends, recvs, {**have, axis: own[axis]}
+
+    def scatter_issue(p, phase):
+        def action(z_first):
+            for h in range(2):
+                if phase > 0:
+                    _, recvs, where = scatter_copies(p, h, z_first, phase - 1)
+                    for _, r in recvs:
+                        r().wait_recv()
+                    view = block(p, h, where)
+                    total = view[...].astype(F32)
+                    for dst, _ in recvs:
+                        total = total + dst[...].astype(F32)
+                    if phase < 3:
+                        view[...] = total.astype(BF16)
+                    else:
+                        out_grad[p, h] = total
+                        NB[0] += fold(total * total)
+                if phase < 3:
+                    for s in scatter_copies(p, h, z_first, phase)[0]:
+                        s().start()
+
+        by_kind(p % PER, action)
+
+    def fold(sq):
+        sq = jnp.sum(sq.reshape(HALF // 8, 8, WIDE), axis=0)
+        return sq[:, 0:128] + sq[:, 128:256] + sq[:, 256:384]
+
+    def scatter_sent(p):
+        def action(z_first):
+            for h in range(2):
+                for phase in range(3):
+                    for s in scatter_copies(p, h, z_first, phase)[0]:
+                        s().wait_send()
+
+        by_kind(p % PER, action)
+
+    NB[0] = jnp.zeros((8, 128), F32)
+    SG[...] = jnp.zeros_like(SG)
+
+    def transpose_into(dst, src):
+        def tile(i):
+            rows = rows_at(i, 128)
+            dst[:, rows] = jnp.transpose(src[rows, :])
+
+        loop(SEQ // 128, tile)
+
+    def put_grad(p, yy, left, right):
+        def tile(i):
+            G[p, yy, i] = mm(left[rows_at(i, D // NZ), :], right).reshape(NX, 2, HALF, WIDE).astype(BF16)
+
+        loop(NZ, tile)
+
+    def back_exchange(e, make, src, gain_row):
+        gain = GAIN[pl.ds(gain_row, 1), :]
+        def take(rows, dn):
+            centre, inv = norm_parts(src[rows, :])
+            xhat = centre * inv
+            dh = dn * gain
+            dv = inv * (
+                dh
+                - jnp.mean(dh, axis=-1, keepdims=True)
+                - xhat * jnp.mean(dh * xhat, axis=-1, keepdims=True)
+            )
+            GR[rows, :] += dv
+            SG[pl.ds(gain_row, 1), :] += jnp.sum(dn * xhat, axis=0, keepdims=True)
+
+        exchange(e, make, take)
+
+    def cast_rows(dst, src):
+        def tile(i):
+            rows = rows_at(i, TR)
+            dst[rows, :] = src[rows, :].astype(BF16)
+
+        loop(SEQ // TR, tile)
+
+    def backward_slot(s, l):
+        slot = (4, 2, 5, 3, 1, 0)[s]
+        p = l * PER + slot
+        if slot in (4, 5):
+            u = slot - 4
+            if u == 0:
+                cast_rows(BK, GR)
+                transpose_into(TA, BK)
+                transpose_into(TB, NRM2.at[l])
+
+            def down_back(yy):
+                def tile(i):
+                    rows = rows_at(i, TM)
+                    gh = mm(BK[rows, :], matrix(p, yy))
+                    GU[yy, rows, :] = (gh * GP[l, u, yy, rows, :].astype(F32)).astype(BF16)
+
+                loop(SEQ // TM, tile)
+                put_grad(p, yy, TA, HID[l, u, yy])
+
+            loop(2, down_back)
+        elif slot in (2, 3):
+            u = slot - 2
+            if u == 0:
+
+                def part(i):
+                    rows = rows_at(i, TM)
+                    total = mm_nt(GU[0, rows, :], matrix(p, 0))
+                    ACC[rows, :] = total + mm_nt(GU[1, rows, :], matrix(p, 1))
+
+                loop(SEQ // TM, part)
+            else:
+
+                def make(i):
+                    rows = rows_at(i, TM)
+                    total = ACC[rows, :] + mm_nt(GU[0, rows, :], matrix(p, 0))
+                    return total + mm_nt(GU[1, rows, :], matrix(p, 1))
+
+                back_exchange(0, make, R1.at[l], 2 * l + 1)
+            loop(2, lambda yy: put_grad(p, yy, TB, GU[yy]))
+        elif slot == 1:
+            cast_rows(BK, GR)
+            transpose_into(TA, BK)
+            transpose_into(TB, NRM.at[l])
+
+            def attn_back(yy):
+                def tile(i):
+                    rows = rows_at(i, TM)
+                    GM[yy, rows, :] = mm(BK[rows, :], matrix(p, yy)[:, COL:]).astype(BF16)
+
+                loop(SEQ // TM, tile)
+                attend_back(l, yy)
+
+            loop(2, attn_back)
+
+            def part(i):
+                rows = rows_at(i, TM)
+                total = mm_nt(DV[0, rows, :], matrix(p, 0)[:, :COL])
+                ACC[rows, :] = total + mm_nt(DV[1, rows, :], matrix(p, 1)[:, :COL])
+
+            loop(SEQ // TM, part)
+
+            def grads(yy):
+                def tile(i):
+                    rows = rows_at(i, D // NZ)
+                    gv = mm(TB[rows, :], DV[yy])
+                    go = mm(TA[rows, :], MIX[l, yy])
+                    both = jnp.concatenate([gv, go], axis=1)
+                    G[p, yy, i] = both.reshape(NX, 2, HALF, WIDE).astype(BF16)
+
+                loop(NZ, tile)
+
+            loop(2, grads)
+        else:
+
+            def make(i):
+                rows = rows_at(i, TM)
+                total = ACC[rows, :] + mm_nt(DQK[0, rows, :], matrix(p, 0))
+                return total + mm_nt(DQK[1, rows, :], matrix(p, 1))
+
+            back_exchange(1, make, S.at[l], 2 * l)
+            loop(2, lambda yy: put_grad(p, yy, TB, DQK[yy]))
+        return p
+
+    def position(i):
+        s = i % PER
+        slot = jnp.where(s == 0, 4, jnp.where(s == 1, 2, jnp.where(s == 2, 5, jnp.where(s == 3, 3, 5 - s))))
+        return (LAYERS - 1 - i // PER) * PER + slot
+
+    cot_own.wait()
+    cot_in.wait_recv()
+    cot_out.wait_send()
+
+    def backward_tick(t):
+        @pl.when(t < PAIRS)
+        def _():
+            for s in range(PER):
+
+                @pl.when(t % PER == s)
+                def _():
+                    backward_slot(s, LAYERS - 1 - t // PER)
+
+            scatter_issue(position(t), 0)
+
+        for lag, phase in ((LAG_TWO, 1), (LAG_THREE, 2), (LAG_LAST, 3)):
+
+            @pl.when(jnp.logical_and(t - lag >= 0, t - lag < PAIRS))
+            def _():
+                scatter_issue(position(t - lag), phase)
+
+    loop(PAIRS, backward_tick)
+
+    def finish_tile(i):
+        rows = rows_at(i, TR)
+        flag = FL[rows, :]
+        value = GR[rows, :]
+        SG[4:5, :] += jnp.sum(value * flag, axis=0, keepdims=True)
+        GR[rows, :] = value * (1.0 - flag)
+
+    loop(SEQ // TR, finish_tile)
+    igrad_copy = pltpu.make_async_copy(GRh, out_igrad, lc_s.at[3])
+    igrad_copy.start()
+
+    SR[0, z] = SG[...]
+    sg_z = [
+        (
+            remote(SR.at[0, z], SR.at[0, z], fs_s.at[k - 1], fs_r.at[k - 1], dev_z(k)),
+            remote(SR.at[0, z_from(k)], SR.at[0, z_from(k)], fs_s.at[k - 1], fs_r.at[k - 1], dev_z(k)),
+        )
+        for k in range(1, NZ)
+    ]
+    for s, _ in sg_z:
+        s.start()
+    for _, r in sg_z:
+        r.wait_recv()
+    SR[1, 0] = SR[0, 0] + SR[0, 1] + SR[0, 2] + SR[0, 3]
+    sg_x = remote(SR.at[1, 0], SR.at[1, 1], fs_s.at[3], fs_r.at[3], dev_x)
+    sg_x.start()
+
+    loop(LAG_LAST, lambda i: backward_tick(PAIRS + i))
+
+    sg_x.wait_recv()
+    SR[1, 2] = SR[1, 0] + SR[1, 1]
+    sg_y = remote(SR.at[1, 2], SR.at[1, 3], fs_s.at[4], fs_r.at[4], dev_y)
+    sg_y.start()
+
+    own_square = jnp.sum(jnp.sum(NB[0], axis=1, keepdims=True), axis=0, keepdims=True)
+    NB[1 + z] = jnp.broadcast_to(own_square, (8, 128))
+    nm_z = [
+        (
+            remote(NB.at[1 + z], NB.at[1 + z], nm_s.at[k - 1], nm_r.at[k - 1], dev_z(k)),
+            remote(NB.at[1 + z_from(k)], NB.at[1 + z_from(k)], nm_s.at[k - 1], nm_r.at[k - 1], dev_z(k)),
+        )
+        for k in range(1, NZ)
+    ]
+    for s, _ in nm_z:
+        s.start()
+    sg_y.wait_recv()
+    total_small = SR[1, 2] + SR[1, 3]
+    out_small[...] = total_small
+    small_square = jnp.sum(jnp.sum(total_small * total_small, axis=1, keepdims=True), axis=0, keepdims=True)
+    for _, r in nm_z:
+        r.wait_recv()
+    NB[5] = NB[1] + NB[2] + NB[3] + NB[4]
+    nm_x = remote(NB.at[5], NB.at[6], nm_s.at[3], nm_r.at[3], dev_x)
+    nm_x.start()
+    nm_x.wait_recv()
+    NB[7] = NB[5] + NB[6]
+    nm_y = remote(NB.at[7], NB.at[8], nm_s.at[4], nm_r.at[4], dev_y)
+    nm_y.start()
+    nm_y.wait_recv()
+    NB[9] = NB[7] + NB[8]
+    nm_c = remote(NB.at[9], NB.at[10], nm_s.at[5], nm_r.at[5], dev_core)
+    nm_c.start()
+    nm_c.wait_recv()
+    out_norm[...] = jnp.sqrt(NB[9] + NB[10] + small_square)
+
+    for s, _ in sg_z + nm_z:
+        s.wait_send()
+    for s in (sg_x, sg_y, nm_x, nm_y, nm_c):
+        s.wait_send()
+    loop(PAIRS, scatter_sent)
+    igrad_copy.wait()
+
+
+def big_step(wloc, patches, cotangent, mask_index, mask_count, small):
+    vm = pl.BlockSpec(memory_space=pltpu.VMEM)
+    hb = pl.BlockSpec(memory_space=pl.ANY)
+    sm = pl.BlockSpec(memory_space=pltpu.SMEM)
+    dma = pltpu.SemaphoreType.DMA
+    V = pltpu.VMEM
+    scratch = [
+        V((PAIRS, 2, NZ, NX, 2, HALF, WIDE), BF16),
+        V((2, SEQ, D), F32),
+        V((2, SEQ, D), F32),
+        V((2, SEQ, D), BF16),
+        V((2, SEQ, D), BF16),
+        V((2, 2, SEQ, WIDE), BF16),
+        V((2, 2, SEQ, COL), BF16),
+        V((2, 2, SEQ, COL), BF16),
+        V((2, 2, 2, SEQ, WIDE), BF16),
+        V((2, 2, 2, SEQ, WIDE), BF16),
+        V((SEQ, D), F32),
+        V((SEQ, D), F32),
+        V((SEQ, D), BF16),
+        V((2, SEQ, D), BF16),
+        V((SEQ, D), BF16),
+        V((D, SEQ), BF16),
+        V((D, SEQ), BF16),
+        V((2, SEQ, WIDE), BF16),
+        V((2, SEQ, COL), BF16),
+        V((2, SEQ, WIDE), BF16),
+        V((2, SEQ, COL), BF16),
+        V((SEQ, 1), F32),
+        V((8, D), F32),
+        V((NZ, NX, 8, 128), F32),
+        V((8, D), F32),
+        V((2, 4, 8, D), F32),
+        V((11, 8, 128), F32),
+        V((PAIRS, NZ, NX, HALF, WIDE), BF16),
+        V((PAIRS, 2, NZ, HALF, WIDE), BF16),
+        V((PAIRS, 2, 6, HALF, WIDE), BF16),
+        V((PAIRS, 2, 3, HALF, WIDE), BF16),
+        dma((PAIRS, 2, 5)), dma((PAIRS, 2, 5)),
+        dma((PAIRS, 2, 5)), dma((PAIRS, 2, 5)),
+        dma((2,)), dma((2, 2)),
+        dma((2,)), dma((2,)), dma((4,)),
+        dma((4,)), dma((4,)),
+        dma((5,)), dma((5,)),
+        dma((6,)), dma((6,)),
+    ]
+    return pl.pallas_call(
+        step_kernel,
+        out_shape=(
+            jax.ShapeDtypeStruct((TM, D), F32),
+            jax.ShapeDtypeStruct((TM, D), F32),
+            jax.ShapeDtypeStruct((PAIRS, 2, HALF, WIDE), F32),
+            jax.ShapeDtypeStruct((8, D), F32),
+            jax.ShapeDtypeStruct((8, 128), F32),
+        ),
+        in_specs=[vm, hb, hb, vm, sm, vm],
+        out_specs=(hb, hb, vm, vm, vm),
+        scratch_shapes=scratch,
+        compiler_params=pltpu.CompilerParams(
+            collective_id=0, has_side_effects=True, vmem_limit_bytes=62 << 20
+        ),
+        name="train_step",
+    )(wloc, patches, cotangent, mask_index, mask_count, small)
+
+
+def adam_values(weight_in, moment_one, moment_two, gradient, step_rate, decay_rate):
+    moment_one = BETA_ONE * moment_one + (1.0 - BETA_ONE) * gradient
+    moment_two = BETA_TWO * moment_two + (1.0 - BETA_TWO) * gradient * gradient
+    first_hat = moment_one / (1.0 - BETA_ONE**STEP)
+    second_hat = moment_two / (1.0 - BETA_TWO**STEP)
+    updated = weight_in - step_rate * (
+        first_hat / (jnp.sqrt(second_hat) + EPS_ADAM) + decay_rate * weight_in
+    )
+    return (updated, moment_one, moment_two)
+
+
+def adam_kernel(norm, grad, w, m, v, nw, nm, nv):
+    factor = jnp.minimum(1.0, CLIP_MAX / norm[0:1, 0:1])
+    g = grad[0].reshape(ROWS, WIDE) * factor
+    for j in range(2):
+        nw[j], nm[j], nv[j] = adam_values(w[j], m[j], v[j], g[:, j * COL : (j + 1) * COL], D ** (-0.5), DECAY_RATE)
+
+
+def adam_matrices(norm, grad, weights, first, second):
+    shape = weights.shape
+    flat = (LAYERS * 12, ROWS, COL)
+    blk = pl.BlockSpec((2, ROWS, COL), lambda i: (i, 0, 0))
+    outs = pl.pallas_call(
+        adam_kernel,
+        grid=(PAIRS,),
+        out_shape=tuple(jax.ShapeDtypeStruct(flat, F32) for _ in range(3)),
+        in_specs=[
+            pl.BlockSpec((8, 128), lambda i: (0, 0)),
+            pl.BlockSpec((1, 2, HALF, WIDE), lambda i: (i, 0, 0, 0)),
+            blk, blk, blk,
+        ],
+        out_specs=(blk, blk, blk),
+        name="adam",
+    )(norm, grad, weights.reshape(flat), first.reshape(flat), second.reshape(flat))
+    return tuple(o.reshape(shape) for o in outs)
+
+
+def shards(patches, cotangent, mask_index, mask_count, weights, first_moment, second_moment,
+           small_params, small_first, small_second):
+    owned_rows = weights.shape[2]
+    low = weights.astype(BF16).reshape(PAIRS, 2, ROWS, COL)
+    wloc = jnp.concatenate([low[:, 0], low[:, 1]], axis=-1).reshape(PAIRS, 2, HALF, WIDE)
+    block_output, input_grad, grad_own, small_total, norm = big_step(
+        wloc, patches, cotangent, mask_index, mask_count, small_params
+    )
+    new_weights, new_first, new_second = adam_matrices(norm, grad_own, weights, first_moment, second_moment)
+    grad_norm = norm[0, 0]
+    factor = jnp.minimum(1.0, CLIP_MAX / grad_norm)
+    first_col = lax.axis_index("wide") * owned_rows
+    small_own = lax.dynamic_slice_in_dim(small_total, first_col, owned_rows, 1)[0:5]
+    new_small, new_small_first, new_small_second = adam_values(
+        small_params, small_first, small_second, small_own * factor, RATE_SMALL, 0.0
+    )
+    return (block_output, input_grad, new_weights, new_first, new_second,
+            new_small, new_small_first, new_small_second, grad_norm)
 
 
 def layer_norm(values, gain):
@@ -193,18 +1004,7 @@
     return lax.dynamic_slice_in_dim(flag_all, lax.axis_index("narrow") * row_count, row_count, 0)
 
 
-def adam_step(weight_in, moment_one, moment_two, gradient, step_rate, decay_rate):
-    moment_one = BETA_ONE * moment_one + (1.0 - BETA_ONE) * gradient
-    moment_two = BETA_TWO * moment_two + (1.0 - BETA_TWO) * gradient * gradient
-    first_hat = moment_one / (1.0 - BETA_ONE**STEP)
-    second_hat = moment_two / (1.0 - BETA_TWO**STEP)
-    updated = weight_in - step_rate * (
-        first_hat / (jnp.sqrt(second_hat) + EPS_ADAM) + decay_rate * weight_in
-    )
-    return (updated, moment_one, moment_two)
-
-
-def shards(
+def shards_general(
     patches,
     cotangent,
     mask_index,
@@ -260,10 +1060,10 @@
     local_square = jnp.sum(matrix_own * matrix_own) + jnp.sum(small_own * small_own) / narrow_size
     grad_norm = jnp.sqrt(lax.psum(local_square, ("wide", "narrow")))
     factor = jnp.minimum(1.0, CLIP_MAX / grad_norm)
-    new_weights, new_first, new_second = adam_step(
+    new_weights, new_first, new_second = adam_values(
         weights, first_moment, second_moment, matrix_own * factor, D ** (-0.5), DECAY_RATE
     )
-    new_small, new_small_first, new_small_second = adam_step(
+    new_small, new_small_first, new_small_second = adam_values(
         small_params, small_first, small_second, small_own * factor, RATE_SMALL, 0.0
     )
     return (
@@ -303,4 +1103,6 @@
         P(None, "wide"),
         P(),
     )
-    return jax.shard_map(shards, mesh=mesh, in_specs=in_specs, out_specs=out_specs, check_vma=False)
+    fits = mesh.shape["wide"] == NZ * NX and mesh.shape["narrow"] == 4
+    step = shards if fits else shards_general
+    return jax.shard_map(step, mesh=mesh, in_specs=in_specs, out_specs=out_specs, check_vma=False)

time: 1240 us -> 363 us (0.29)
  waiting for transfers between devices: 765 us -> 0 us
  Pallas kernels: 0 us -> 353 us
  local copies, waits for them, and re-layouts: 136 us -> 3.84 us
  blocking collectives: 112 us -> 0 us
  matrix products: 108 us -> 0 us
  other arithmetic: 89 us -> 3.7 us
  between operations: 18.8 us -> 1.4 us
    psum x1 -> x0, waiting for transfers between devices: 374 us -> none  [shards(): matrix_total = lax.psum(grad_matrix, 'wide')]
    pallas_call x0 -> x2, Pallas kernels: none -> 353 us  [the longest x1 342 us: big_step(): pl.pallas_call(step_kernel, out_shape=(jax.ShapeDtypeStruct((TM, D), F32)...]
    all_gather x9 -> x0, waiting for transfers between devices: 196 us -> none  [the longest x1 110 us: shards(): lax.all_gather(weights.astype(jnp.bfloat16), 'wide', axis=2, tiled=True)]
    reduce_scatter x8 -> x0, waiting for transfers between devices: 194 us -> none  [the longest x4 114 us: branch_total(): lax.psum_scatter(term(jnp.int32(0), row_count * lax.axis_size('narrow'))....]
    psum x2 -> x0, blocking collectives: 83.5 us -> none  [the longest x1 44.1 us: shards(): small_total = lax.psum(grad_small, ('wide', 'narrow'))]
    unnamed x190 -> x12, local copies, waits for them, and re-layouts: 78 us -> 1.79 us
    dot_general x39 -> x0, matrix products: 72.6 us -> none  [the longest x4 9.37 us: attend_clip(): jnp.einsum('hqk,khd->qhd', probs.astype(jnp.bfloat16), value_rows, prefer...]
    convert_element_type x18 -> x1, other arithmetic: 30.3 us -> 1.82 us  [shards(): low = weights.astype(BF16).reshape(PAIRS, 2, ROWS, COL)]
  transfers between devices with their start and end apart: 18 -> 0, of which waited for: 16 -> 0; matrix products, arithmetic and copies ran while one was open for 11% -> 0% of each run, Pallas kernels for 0% -> 0%
where the time goes in v1:
time: 363 us; the launch traced here: 362 us
  Pallas kernels  353 us (97%)
  local copies, waits for them, and re-layouts  3.84 us (1%)
  other arithmetic  3.7 us (1%)
    pallas_call x1, Pallas kernels, big_step(): pl.pallas_call(step_kernel, out_shape=(jax.ShapeDtypeStruct((TM, D), F32)...  342 us
    pallas_call x1, Pallas kernels, adam_matrices(): pl.pallas_call(adam_kernel, grid=(PAIRS,), out_shape=tuple((jax.ShapeDtyp...  11.8 us

profile of v1, /device:TPU:0, one launch (start us, length us, event | category | flops | bytes accessed | tf_op | source)
XLA Modules:
  0.0 362.4 jit_solution(12912170668252116619)
XLA Ops:
  0.6 1.8 convert_element_type.3
  2.5 0.1 fusion.2
  2.6 0.0 copy-start.2
  2.6 0.0 copy-start.3
  2.6 0.0 copy-start.4
  2.6 1.3 pad_maximum_fusion.wloc
  3.9 341.7 %train_step.1 = (f32[256,768]{1,0:T(8,128)}, f32[256,768]{1,0:T(8,128)}, f32[12,2,48,384]{3,2,1,0:T(8,128)}, f32[8,768]{1,0:T(8,128)}, f32[8,128]{1,0:T(8,128)}) custom-call(bf16[12,2,48,384]{3,2,1,0:T(8,128)(2,1)} %pad_maximum_fusion.wloc, bf16[256,768]{1,0:T(8,128)(2,1)} %patch.1, f32[256,768]{1,0:T(8,128)} %cot.1, s32[2,450]{1,0:T(2,128)} %mask_index.1, ...), custom_call_target="tpu_custom_call" | custom-call | tf_op jit(solution)/shard_map/train_step/pallas_call | solution.py:757
  345.6 1.2 slice.15
  347.5 0.8 constant_dynamic-slice_fusion
  348.2 0.0 copy-done.2
  348.2 0.0 copy-done.3
  348.2 0.0 copy-done.4
  348.2 0.6 multiply_subtract_fusion
  348.9 0.0 copy-start.1
  348.9 0.0 copy-start
  348.9 11.8 %adam.1 = (f32[24,96,192]{2,1,0:T(8,128)}, f32[24,96,192]{2,1,0:T(8,128)}, f32[24,96,192]{2,1,0:T(8,128)}) custom-call(f32[8,128]{1,0:T(8,128)} %get-tuple-element.19.norm, f32[12,2,48,384]{3,2,1,0:T(8,128)} %get-tuple-element.20.grad, f32[24,96,192]{2,1,0:T(8,128)} %bitcast.14, f32[24,96,192]{2,1,0:T(8,128)} %bitcast.16, f32[24,96,192]{2,1,0:T(8,128)} %bitcast.17), custom_call_target="tpu_custom_call" | custom-call | tf_op jit(solution)/shard_map/adam/pallas_call | solution.py:798
  360.6 0.0 copy-done.1
  360.7 0.9 copy.25
  361.5 0.0 copy-done
  361.5 0.9 copy.26
Async XLA Ops:
  2.6 345.7 %copy-start.2 = (f32[5,96]{1,0:T(8,128)S(1)}, f32[5,96]{1,0:T(8,128)}, u32[]{:S(2)}) copy-start(f32[5,96]{1,0:T(8,128)} %small.1) | copy-start | bytes 5764
  2.6 345.7 %copy-start.3 = (f32[5,96]{1,0:T(8,128)S(1)}, f32[5,96]{1,0:T(8,128)}, u32[]{:S(2)}) copy-start(f32[5,96]{1,0:T(8,128)} %param.18) | copy-start | bytes 5764
  2.6 345.7 %copy-start.4 = (f32[5,96]{1,0:T(8,128)S(1)}, f32[5,96]{1,0:T(8,128)}, u32[]{:S(2)}) copy-start(f32[5,96]{1,0:T(8,128)} %param.19) | copy-start | bytes 5764
  348.9 11.8 %copy-start.1 = (f32[256,768]{1,0:T(8,128)S(1)}, f32[256,768]{1,0:T(8,128)}, u32[]{:S(2)}) copy-start(f32[256,768]{1,0:T(8,128)} %get-tuple-element.39) | copy-start | bytes 2359300
  348.9 12.7 %copy-start = (f32[256,768]{1,0:T(8,128)S(1)}, f32[256,768]{1,0:T(8,128)}, u32[]{:S(2)}) copy-start(f32[256,768]{1,0:T(8,128)} %get-tuple-element.40) | copy-start | bytes 2359300

commit v2 on v1

--- a/solution.py
+++ b/solution.py
@@ -26,10 +26,12 @@
 BF16 = jnp.bfloat16
 
 PAIRS = 12
+ADAM_STEPS = 2
 PER = 6
 NZ, NX = 4, 2
 ROWS = 96
-HALF = 48
+PARTS = 3
+PART = ROWS // PARTS
 COL = 192
 WIDE = 2 * COL
 SCALE = HD ** (-0.5)
@@ -37,8 +39,9 @@
 TR = 64
 HEADS_Y = COL // HD
 
-LEAD_ONE, LEAD_TWO, LEAD_THREE = 5, 3, 1
-LAG_TWO, LAG_THREE, LAG_LAST = 1, 2, 3
+BACK_ORDER = (4, 5, 2, 3, 1, 0)
+LEAD_ONE, LEAD_TWO, LEAD_THREE = 4, 3, 2
+LAG_TWO, LAG_THREE, LAG_LAST = 2, 4, 6
 
 
 def mm(a, b):
@@ -66,11 +69,11 @@
 
 
 def step_kernel(
-    wloc, patch, cot, mask_index, mask_count, small,
+    weights, patch, cot, mask_index, mask_count, small,
     out_block, out_igrad, out_grad, out_small, out_norm,
-    G, S, R1, NRM, NRM2, QK, V, MIX, GP, HID, GR, ACC, XS, XR, BK, TA, TB, GU, GM, DQK, DV,
-    FL, GAIN, GPIECE, SG, SR, NB, RB0Y, RB0X, RB1, RB2,
-    ag_s, ag_r, rs_s, rs_r, ex_s, ex_r, in_s, in_r, lc_s, gn_s, gn_r, fs_s, fs_r, nm_s, nm_r,
+    G, WF, S, R1, NRM, NRM2, QK, V, MIX, GP, HID, GR, ACC, XS, XR, BK, TA, TB, GU, GM, DQK, DV,
+    FL, GAIN, GPIECE, SG, SR, NB, NZC, NXY, RB0Y, RB0X, RB1, RB1Z, RB2, RB2X,
+    wf_s, ag_s, ag_r, rs_s, rs_r, ex_s, ex_r, in_s, in_r, lc_s, gn_s, gn_r, fs_s, fs_r, nm_s, nm_r,
 ):
     wide = lax.axis_index("wide")
     narrow = lax.axis_index("narrow")
@@ -90,10 +93,22 @@
     def dev_z(k):
         return (z_to(k) * NX + x, narrow)
 
+    dev_xy = (z * NX + 1 - x, 2 * (1 - y) + c)
+
+    def dev_zc(k):
+        return (z_to(k) * NX + x, 2 * y + 1 - c)
+
+    def load_pair(p):
+        return pltpu.make_async_copy(weights.at[pl.ds(2 * p, 2)], WF.at[p % LEAD_ONE], wf_s.at[p % LEAD_ONE])
+
+    for p in range(LEAD_ONE):
+        load_pair(p).start()
+
+    greeted = [dev_core, dev_x, dev_y, dev_xy] + [dev(k) for k in range(1, NZ) for dev in (dev_z, dev_zc)]
     barrier = pltpu.get_barrier_semaphore()
-    for dev in [dev_core, dev_x, dev_y] + [dev_z(k) for k in range(1, NZ)]:
+    for dev in greeted:
         pl.semaphore_signal(barrier, inc=1, device_id=dev, device_id_type=MESH)
-    pl.semaphore_wait(barrier, 3 + NZ - 1)
+    pl.semaphore_wait(barrier, len(greeted))
 
     def remote(src, dst, send, recv, dev):
         return pltpu.make_async_remote_copy(
@@ -114,9 +129,12 @@
     def block(p, h, where):
         return G.at[p, where["y"], where["z"], where["x"], h]
 
-    def gather_order(z_first, h):
-        a, b = ("x", "y") if h == 0 else ("y", "x")
-        return ("z", a, b) if z_first else (a, "z", b)
+    def gather_order(even, h):
+        if h == 0:
+            return ("z", "x", "y")
+        if h == 1:
+            return ("z", "y", "x")
+        return ("x", "z", "y") if even else ("y", "z", "x")
 
     def gather_copies(p, h, order, phase):
         axis = order[phase]
@@ -129,21 +147,19 @@
             recvs.append(lazy(got, got, ag_s.at[p, h, slot], ag_r.at[p, h, slot], dev))
         return sends, recvs
 
-    def by_kind(slot_index, action):
-        z_second = (slot_index % 3) == 2
-
-        @pl.when(jnp.logical_not(z_second))
+    def by_kind(p, action):
+        @pl.when(p % 2 == 0)
         def _():
             action(True)
 
-        @pl.when(z_second)
+        @pl.when(p % 2 == 1)
         def _():
             action(False)
 
     def gather_issue(p, phase):
-        def action(z_first):
-            for h in range(2):
-                order = gather_order(z_first, h)
+        def action(even):
+            for h in range(PARTS):
+                order = gather_order(even, h)
                 if phase > 0:
                     for r in gather_copies(p, h, order, phase - 1)[1]:
                         r().wait_recv()
@@ -151,20 +167,26 @@
                     for s in gather_copies(p, h, order, phase)[0]:
                         s().start()
 
-        by_kind(p % PER, action)
+        by_kind(p, action)
 
     def gather_sent(p):
-        def action(z_first):
-            for h in range(2):
+        def action(even):
+            for h in range(PARTS):
                 for phase in range(3):
-                    for s in gather_copies(p, h, gather_order(z_first, h), phase)[0]:
+                    for s in gather_copies(p, h, gather_order(even, h), phase)[0]:
                         s().wait_send()
 
-        by_kind(p % PER, action)
-
-    for p in range(PAIRS):
-        for h in range(2):
-            G[p, y, z, x, h] = wloc[p, h]
+        by_kind(p, action)
+
+    def pack(p):
+        load_pair(p).wait()
+        slot = p % LEAD_ONE
+        both = jnp.concatenate([WF[slot, 0].astype(BF16), WF[slot, 1].astype(BF16)], axis=1)
+        G[p, y, z, x] = both.reshape(PARTS, PART, WIDE)
+
+        @pl.when(p + LEAD_ONE < PAIRS)
+        def _():
+            load_pair(p + LEAD_ONE).start()
 
     half = TM * c
     BKh = BK.at[pl.ds(pl.multiple_of(half, TM), TM)]
@@ -196,9 +218,13 @@
     )
     for s, _ in gain_z:
         s.start()
-    for p in range(LEAD_ONE):
+    def begin(p):
+        pack(p)
         gather_issue(p, 0)
+
+    loop(LEAD_ONE, begin)
     cot_out.start()
+    loop(PAIRS - LEAD_ONE, lambda i: pack(i + LEAD_ONE))
 
     index_row = mask_index[pl.ds(y, 1), :]
     count = mask_count[y]
@@ -249,30 +275,26 @@
     def matrix(p, yy):
         return G[p, yy].reshape(D, WIDE)
 
-    def exchange(e, make, take):
-        par = e % 2
-
-        def copies(i, par):
-            rows = rows_at(i, TM)
-            return remote(XS.at[rows], XR.at[par, rows], ex_s.at[i], ex_r.at[par, i], dev_core)
-
-        def give(i):
-            XS[rows_at(i, TM), :] = make(i).astype(BF16)
-            copies(i, par).start()
-
-        loop(SEQ // TM, give)
-
-        def receive(i):
-            copies(i, par).wait_recv()
+    def exchange_copy(e, i):
+        rows = rows_at(i, TM)
+        return remote(XS.at[rows], XR.at[e, rows], ex_s.at[i], ex_r.at[e, i], dev_core)
+
+    def give(e, value):
+        XS[...] = value.astype(BF16)
+        loop(SEQ // TM, lambda i: exchange_copy(e, i).start())
+
+    def receive(e, take):
+        def chunk(i):
+            exchange_copy(e, i).wait_recv()
 
             def tile(j):
                 rows = pl.ds(pl.multiple_of(i * TM + j * TR, TR), TR)
-                take(rows, XS[rows, :].astype(F32) + XR[par, rows, :].astype(F32))
+                take(rows, XS[rows, :].astype(F32) + XR[e, rows, :].astype(F32))
 
             loop(TM // TR, tile)
 
-        loop(SEQ // TM, receive)
-        loop(SEQ // TM, lambda i: copies(i, par).wait_send())
+        loop(SEQ // TM, chunk)
+        loop(SEQ // TM, lambda i: exchange_copy(e, i).wait_send())
 
     def attend(l, yy):
         def tile(i):
@@ -319,77 +341,58 @@
             DQK[yy, :, COL + lo : COL + lo + HD] = (dk * SCALE).astype(BF16)
             DV[yy, :, lo : lo + HD] = dv.astype(BF16)
 
-    def forward_slot(slot, l):
+    def up_part(l, u, yy, p):
+        ACC[:, 0:WIDE] = mm(NRM2[l], matrix(p, yy))
+
+        def gelu(i):
+            rows = rows_at(i, TR)
+            v = ACC[rows, 0:WIDE]
+            cdf = 0.5 * (1.0 + lax.erf(v * (2.0 ** -0.5)))
+            HID[l, u, yy, rows, :] = (v * cdf).astype(BF16)
+            pdf = jnp.exp(-0.5 * v * v) * 0.3989422804014327
+            GP[l, u, yy, rows, :] = (cdf + v * pdf).astype(BF16)
+
+        loop(SEQ // TR, gelu)
+
+    def forward_slot(slot, step, l):
         p = l * PER + slot
         if slot == 0:
-            norm_into(NRM.at[l], S.at[l], 2 * l)
-
-            def project(yy):
-                def tile(i):
-                    rows = rows_at(i, TM)
-                    QK[l, yy, rows, :] = mm(NRM[l, rows, :], matrix(p, yy)).astype(BF16)
-
-                loop(SEQ // TM, tile)
-
-            loop(2, project)
+            if step == 0:
+                norm_into(NRM.at[l], S.at[l], 2 * l)
+            else:
+
+                def project(yy):
+                    QK[l, yy] = mm(NRM[l], matrix(p, yy)).astype(BF16)
+
+                loop(2, project)
         elif slot == 1:
-
-            def project_v(yy):
-                def tile(i):
-                    rows = rows_at(i, TM)
-                    V[l, yy, rows, :] = mm(NRM[l, rows, :], matrix(p, yy)[:, :COL]).astype(BF16)
-
-                loop(SEQ // TM, tile)
-                attend(l, yy)
-
-            loop(2, project_v)
-
-            def make(i):
-                rows = rows_at(i, TM)
-                total = mm_nt(MIX[l, 0, rows, :], matrix(p, 0)[:, COL:])
-                return total + mm_nt(MIX[l, 1, rows, :], matrix(p, 1)[:, COL:])
-
-            def take(rows, total):
-                R1[l, rows, :] = S[l, rows, :] + total
-
-            exchange(0, make, take)
+            if step == 0:
+
+                def project_v(yy):
+                    V[l, yy] = mm(NRM[l], matrix(p, yy)[:, :COL]).astype(BF16)
+
+                loop(2, project_v)
+                attend(l, 0)
+            else:
+                attend(l, 1)
+                total = mm_nt(MIX[l, 0], matrix(p, 0)[:, COL:])
+                give(0, total + mm_nt(MIX[l, 1], matrix(p, 1)[:, COL:]))
         elif slot in (2, 3):
-            u = slot - 2
-            if u == 0:
+            if slot == 2 and step == 0:
+
+                def take(rows, total):
+                    R1[l, rows, :] = S[l, rows, :] + total
+
+                receive(0, take)
                 norm_into(NRM2.at[l], R1.at[l], 2 * l + 1)
-
-            def project_up(yy):
-                def tile(i):
-                    rows = rows_at(i, TM)
-                    ACC[rows, 0:WIDE] = mm(NRM2[l, rows, :], matrix(p, yy))
-
-                loop(SEQ // TM, tile)
-
-                def gelu(i):
-                    rows = rows_at(i, TR)
-                    v = ACC[rows, 0:WIDE]
-                    cdf = 0.5 * (1.0 + lax.erf(v * (2.0 ** -0.5)))
-                    HID[l, u, yy, rows, :] = (v * cdf).astype(BF16)
-                    pdf = jnp.exp(-0.5 * v * v) * 0.3989422804014327
-                    GP[l, u, yy, rows, :] = (cdf + v * pdf).astype(BF16)
-
-                loop(SEQ // TR, gelu)
-
-            loop(2, project_up)
+            up_part(l, slot - 2, step, p)
         elif slot == 4:
-
-            def down(i):
-                rows = rows_at(i, TM)
-                total = mm_nt(HID[l, 0, 0, rows, :], matrix(p, 0))
-                ACC[rows, :] = total + mm_nt(HID[l, 0, 1, rows, :], matrix(p, 1))
-
-            loop(SEQ // TM, down)
+            if step == 0:
+                ACC[...] = mm_nt(HID[l, 0, 0], matrix(p, 0)) + mm_nt(HID[l, 0, 1], matrix(p, 1))
+        elif step == 0:
+            total = ACC[...] + mm_nt(HID[l, 1, 0], matrix(p, 0))
+            give(1, total + mm_nt(HID[l, 1, 1], matrix(p, 1)))
         else:
-
-            def make(i):
-                rows = rows_at(i, TM)
-                total = ACC[rows, :] + mm_nt(HID[l, 1, 0, rows, :], matrix(p, 0))
-                return total + mm_nt(HID[l, 1, 1, rows, :], matrix(p, 1))
 
             def take(rows, total):
                 value = R1[l, rows, :] + total
@@ -402,59 +405,36 @@
                 def _():
                     ACC[rows, :] = value
 
-            exchange(1, make, take)
-
-    def forward_tick(t):
-        for lead, phase in ((LEAD_ONE, 0), (LEAD_TWO, 1), (LEAD_THREE, 2)):
-
-            @pl.when(jnp.logical_and(t + lead >= (LEAD_ONE if phase == 0 else 0), t + lead < PAIRS))
+            receive(1, take)
+
+            @pl.when(l == 1)
             def _():
-                gather_issue(t + lead, phase)
-
-        @pl.when(t >= 0)
-        def _():
-            gather_issue(t, 3)
-            for slot in range(PER):
-
-                @pl.when(t % PER == slot)
-                def _():
-                    forward_slot(slot, t // PER)
-
-    lead_in = LEAD_TWO
-
-    loop(PAIRS + lead_in, lambda i: forward_tick(i - lead_in))
+                block_copy.start()
 
     block_copy = pltpu.make_async_copy(ACC.at[pl.ds(pl.multiple_of(half, TM), TM)], out_block, lc_s.at[2])
-    block_copy.start()
-    loop(PAIRS, gather_sent)
-    for s, _ in gain_z:
-        s.wait_send()
-    gain_x[0].wait_send()
-    patch_out.wait_send()
-    block_copy.wait()
-
-    def scatter_copies(p, h, z_first, phase):
-        order = gather_order(z_first, h)[::-1]
+
+    def scatter_copies(p, h, even, phase):
+        order = gather_order(even, h)[::-1]
         axis = order[phase]
         have = {q: (own[q] if q in order[:phase] else ALL) for q in own}
         sends, recvs = [], []
         for slot, dev, to, _ in partners[axis]:
             src = block(p, h, {**have, axis: to})
             if phase == 0:
-                dst = (RB0Y if h == 0 else RB0X).at[p]
+                dst = (RB0Y if axis == "y" else RB0X).at[p if h < 2 else PAIRS + p // 2]
             elif phase == 1:
-                dst = RB1.at[p, h, pl.ds(2 * slot, 2)] if axis == "z" else RB1.at[p, h, pl.ds(0, NZ)]
+                dst = RB1Z.at[p, slot] if axis == "z" else RB1.at[p, h]
             else:
-                dst = RB2.at[p, h, slot] if axis == "z" else RB2.at[p, h, 0]
+                dst = RB2.at[p, h, slot] if axis == "z" else RB2X.at[p]
             sends.append(lazy(src, dst, rs_s.at[p, h, slot], rs_r.at[p, h, slot], dev))
             recvs.append((dst, lazy(dst, dst, rs_s.at[p, h, slot], rs_r.at[p, h, slot], dev)))
         return sends, recvs, {**have, axis: own[axis]}
 
     def scatter_issue(p, phase):
-        def action(z_first):
-            for h in range(2):
+        def action(even):
+            for h in range(PARTS):
                 if phase > 0:
-                    _, recvs, where = scatter_copies(p, h, z_first, phase - 1)
+                    _, recvs, where = scatter_copies(p, h, even, phase - 1)
                     for _, r in recvs:
                         r().wait_recv()
                     view = block(p, h, where)
@@ -465,27 +445,27 @@
                         view[...] = total.astype(BF16)
                     else:
                         out_grad[p, h] = total
-                        NB[0] += fold(total * total)
+                        NB[...] += fold(total * total)
                 if phase < 3:
-                    for s in scatter_copies(p, h, z_first, phase)[0]:
+                    for s in scatter_copies(p, h, even, phase)[0]:
                         s().start()
 
-        by_kind(p % PER, action)
+        by_kind(p, action)
 
     def fold(sq):
-        sq = jnp.sum(sq.reshape(HALF // 8, 8, WIDE), axis=0)
+        sq = jnp.sum(sq.reshape(PART // 8, 8, WIDE), axis=0)
         return sq[:, 0:128] + sq[:, 128:256] + sq[:, 256:384]
 
     def scatter_sent(p):
-        def action(z_first):
-            for h in range(2):
+        def action(even):
+            for h in range(PARTS):
                 for phase in range(3):
-                    for s in scatter_copies(p, h, z_first, phase)[0]:
+                    for s in scatter_copies(p, h, even, phase)[0]:
                         s().wait_send()
 
-        by_kind(p % PER, action)
-
-    NB[0] = jnp.zeros((8, 128), F32)
+        by_kind(p, action)
+
+    NB[...] = jnp.zeros((8, 128), F32)
     SG[...] = jnp.zeros_like(SG)
 
     def transpose_into(dst, src):
@@ -496,12 +476,9 @@
         loop(SEQ // 128, tile)
 
     def put_grad(p, yy, left, right):
-        def tile(i):
-            G[p, yy, i] = mm(left[rows_at(i, D // NZ), :], right).reshape(NX, 2, HALF, WIDE).astype(BF16)
-
-        loop(NZ, tile)
-
-    def back_exchange(e, make, src, gain_row):
+        G[p, yy] = mm(left[...], right).astype(BF16).reshape(NZ, NX, PARTS, PART, WIDE)
+
+    def norm_back(e, src, gain_row):
         gain = GAIN[pl.ds(gain_row, 1), :]
         def take(rows, dn):
             centre, inv = norm_parts(src[rows, :])
@@ -515,7 +492,7 @@
             GR[rows, :] += dv
             SG[pl.ds(gain_row, 1), :] += jnp.sum(dn * xhat, axis=0, keepdims=True)
 
-        exchange(e, make, take)
+        receive(e, take)
 
     def cast_rows(dst, src):
         def tile(i):
@@ -524,198 +501,246 @@
 
         loop(SEQ // TR, tile)
 
-    def backward_slot(s, l):
-        slot = (4, 2, 5, 3, 1, 0)[s]
+    def both(action):
+        loop(2, action)
+
+    def backward_slot(s, step, l):
+        slot = BACK_ORDER[s]
         p = l * PER + slot
+        if step == 0:
+            gather_sent(p)
         if slot in (4, 5):
             u = slot - 4
-            if u == 0:
+            if slot == 4 and step == 0:
+
+                @pl.when(l == 1)
+                def _():
+                    cot_own.wait()
+                    cot_in.wait_recv()
+                    cot_out.wait_send()
+
                 cast_rows(BK, GR)
                 transpose_into(TA, BK)
                 transpose_into(TB, NRM2.at[l])
-
-            def down_back(yy):
-                def tile(i):
-                    rows = rows_at(i, TM)
-                    gh = mm(BK[rows, :], matrix(p, yy))
-                    GU[yy, rows, :] = (gh * GP[l, u, yy, rows, :].astype(F32)).astype(BF16)
-
-                loop(SEQ // TM, tile)
-                put_grad(p, yy, TA, HID[l, u, yy])
-
-            loop(2, down_back)
-        elif slot in (2, 3):
-            u = slot - 2
-            if u == 0:
-
-                def part(i):
-                    rows = rows_at(i, TM)
-                    total = mm_nt(GU[0, rows, :], matrix(p, 0))
-                    ACC[rows, :] = total + mm_nt(GU[1, rows, :], matrix(p, 1))
-
-                loop(SEQ // TM, part)
+            gh = mm(BK[...], matrix(p, step))
+            GU[u, step] = (gh * GP[l, u, step].astype(F32)).astype(BF16)
+            put_grad(p, step, TA, HID[l, u, step])
+        elif slot == 2:
+            if step == 0:
+
+                @pl.when(l == 1)
+                def _():
+                    block_copy.wait()
+
+                ACC[...] = mm_nt(GU[0, 0], matrix(p, 0)) + mm_nt(GU[0, 1], matrix(p, 1))
             else:
-
-                def make(i):
-                    rows = rows_at(i, TM)
-                    total = ACC[rows, :] + mm_nt(GU[0, rows, :], matrix(p, 0))
-                    return total + mm_nt(GU[1, rows, :], matrix(p, 1))
-
-                back_exchange(0, make, R1.at[l], 2 * l + 1)
-            loop(2, lambda yy: put_grad(p, yy, TB, GU[yy]))
+                both(lambda yy: put_grad(p, yy, TB, GU[0, yy]))
+        elif slot == 3:
+            if step == 0:
+                total = ACC[...] + mm_nt(GU[1, 0], matrix(p, 0))
+                give(0, total + mm_nt(GU[1, 1], matrix(p, 1)))
+            else:
+                both(lambda yy: put_grad(p, yy, TB, GU[1, yy]))
+                norm_back(0, R1.at[l], 2 * l + 1)
         elif slot == 1:
-            cast_rows(BK, GR)
-            transpose_into(TA, BK)
-            transpose_into(TB, NRM.at[l])
-
-            def attn_back(yy):
-                def tile(i):
-                    rows = rows_at(i, TM)
-                    GM[yy, rows, :] = mm(BK[rows, :], matrix(p, yy)[:, COL:]).astype(BF16)
-
-                loop(SEQ // TM, tile)
-                attend_back(l, yy)
-
-            loop(2, attn_back)
-
-            def part(i):
-                rows = rows_at(i, TM)
-                total = mm_nt(DV[0, rows, :], matrix(p, 0)[:, :COL])
-                ACC[rows, :] = total + mm_nt(DV[1, rows, :], matrix(p, 1)[:, :COL])
-
-            loop(SEQ // TM, part)
-
-            def grads(yy):
-                def tile(i):
-                    rows = rows_at(i, D // NZ)
-                    gv = mm(TB[rows, :], DV[yy])
-                    go = mm(TA[rows, :], MIX[l, yy])
-                    both = jnp.concatenate([gv, go], axis=1)
-                    G[p, yy, i] = both.reshape(NX, 2, HALF, WIDE).astype(BF16)
-
-                loop(NZ, tile)
-
-            loop(2, grads)
+            if step == 0:
+                cast_rows(BK, GR)
+                transpose_into(TA, BK)
+                transpose_into(TB, NRM.at[l])
+
+                def grad_mix(yy):
+                    GM[yy] = mm(BK[...], matrix(p, yy)[:, COL:]).astype(BF16)
+
+                both(grad_mix)
+                attend_back(l, 0)
+            else:
+                attend_back(l, 1)
+                ACC[...] = mm_nt(DV[0], matrix(p, 0)[:, :COL]) + mm_nt(DV[1], matrix(p, 1)[:, :COL])
+
+                def grads(yy):
+                    gv = mm(TB[...], DV[yy])
+                    go = mm(TA[...], MIX[l, yy])
+                    pair = jnp.concatenate([gv, go], axis=1).astype(BF16)
+                    G[p, yy] = pair.reshape(NZ, NX, PARTS, PART, WIDE)
+
+                both(grads)
         else:
-
-            def make(i):
-                rows = rows_at(i, TM)
-                total = ACC[rows, :] + mm_nt(DQK[0, rows, :], matrix(p, 0))
-                return total + mm_nt(DQK[1, rows, :], matrix(p, 1))
-
-            back_exchange(1, make, S.at[l], 2 * l)
-            loop(2, lambda yy: put_grad(p, yy, TB, DQK[yy]))
-        return p
+            if step == 0:
+                total = ACC[...] + mm_nt(DQK[0], matrix(p, 0))
+                give(1, total + mm_nt(DQK[1], matrix(p, 1)))
+            else:
+                both(lambda yy: put_grad(p, yy, TB, DQK[yy]))
+                norm_back(1, S.at[l], 2 * l)
 
     def position(i):
         s = i % PER
-        slot = jnp.where(s == 0, 4, jnp.where(s == 1, 2, jnp.where(s == 2, 5, jnp.where(s == 3, 3, 5 - s))))
+        slot = jnp.where(s < 2, s + 4, jnp.where(s < 4, s, 5 - s))
         return (LAYERS - 1 - i // PER) * PER + slot
 
-    cot_own.wait()
-    cot_in.wait_recv()
-    cot_out.wait_send()
-
-    def backward_tick(t):
-        @pl.when(t < PAIRS)
+    def within(t, action, phase, first=0):
+        @pl.when(jnp.logical_and(t >= first, t < PAIRS))
         def _():
-            for s in range(PER):
-
-                @pl.when(t % PER == s)
+            action(t, phase)
+
+    def by_slot(t, action):
+        for slot in range(PER):
+
+            @pl.when(t % PER == slot)
+            def _():
+                action(slot)
+
+    def scatter_at(t, phase):
+        scatter_issue(position(t), phase)
+
+    def forward_tick(t, q):
+        for step in range(2):
+
+            @pl.when(q == step)
+            def _():
+                if step == 0:
+                    within(t + LEAD_ONE, gather_issue, 0, LEAD_ONE)
+                    within(t + LEAD_TWO, gather_issue, 1)
+                    within(t + LEAD_THREE, gather_issue, 2)
+                    within(t, gather_issue, 3)
+
+                @pl.when(t >= 0)
                 def _():
-                    backward_slot(s, LAYERS - 1 - t // PER)
-
-            scatter_issue(position(t), 0)
-
-        for lag, phase in ((LAG_TWO, 1), (LAG_THREE, 2), (LAG_LAST, 3)):
-
-            @pl.when(jnp.logical_and(t - lag >= 0, t - lag < PAIRS))
+                    by_slot(t, lambda slot: forward_slot(slot, step, t // PER))
+
+    def backward_tick(t, q):
+        for step in range(2):
+
+            @pl.when(q == step)
             def _():
-                scatter_issue(position(t - lag), phase)
-
-    loop(PAIRS, backward_tick)
-
-    def finish_tile(i):
-        rows = rows_at(i, TR)
-        flag = FL[rows, :]
-        value = GR[rows, :]
-        SG[4:5, :] += jnp.sum(value * flag, axis=0, keepdims=True)
-        GR[rows, :] = value * (1.0 - flag)
-
-    loop(SEQ // TR, finish_tile)
+                @pl.when(t < PAIRS)
+                def _():
+                    by_slot(t, lambda s: backward_slot(s, step, LAYERS - 1 - t // PER))
+
+                if step == 0:
+                    pl.when(t == PAIRS)(rows_done)
+                    pl.when(t == PAIRS + LAG_TWO)(small_sums)
+
+                if step == 0:
+                    within(t - LAG_TWO, scatter_at, 1)
+                    within(t - LAG_LAST, scatter_at, 3)
+                else:
+                    within(t, scatter_at, 0)
+                    within(t - LAG_THREE, scatter_at, 2)
+
     igrad_copy = pltpu.make_async_copy(GRh, out_igrad, lc_s.at[3])
-    igrad_copy.start()
-
-    SR[0, z] = SG[...]
-    sg_z = [
-        (
-            remote(SR.at[0, z], SR.at[0, z], fs_s.at[k - 1], fs_r.at[k - 1], dev_z(k)),
-            remote(SR.at[0, z_from(k)], SR.at[0, z_from(k)], fs_s.at[k - 1], fs_r.at[k - 1], dev_z(k)),
+    place = 2 * y + x
+    around = ((2 * y + 1 - x, dev_x), (2 * (1 - y) + x, dev_y), (2 * (1 - y) + 1 - x, dev_xy))
+
+    def small_z(k):
+        got = SR.at[z_from(k), 0]
+        return (
+            remote(SR.at[z, 0], SR.at[z, 0], fs_s.at[k - 1], fs_r.at[k - 1], dev_z(k)),
+            remote(got, got, fs_s.at[k - 1], fs_r.at[k - 1], dev_z(k)),
         )
-        for k in range(1, NZ)
-    ]
-    for s, _ in sg_z:
-        s.start()
-    for _, r in sg_z:
-        r.wait_recv()
-    SR[1, 0] = SR[0, 0] + SR[0, 1] + SR[0, 2] + SR[0, 3]
-    sg_x = remote(SR.at[1, 0], SR.at[1, 1], fs_s.at[3], fs_r.at[3], dev_x)
-    sg_x.start()
-
-    loop(LAG_LAST, lambda i: backward_tick(PAIRS + i))
-
-    sg_x.wait_recv()
-    SR[1, 2] = SR[1, 0] + SR[1, 1]
-    sg_y = remote(SR.at[1, 2], SR.at[1, 3], fs_s.at[4], fs_r.at[4], dev_y)
-    sg_y.start()
-
-    own_square = jnp.sum(jnp.sum(NB[0], axis=1, keepdims=True), axis=0, keepdims=True)
-    NB[1 + z] = jnp.broadcast_to(own_square, (8, 128))
-    nm_z = [
-        (
-            remote(NB.at[1 + z], NB.at[1 + z], nm_s.at[k - 1], nm_r.at[k - 1], dev_z(k)),
-            remote(NB.at[1 + z_from(k)], NB.at[1 + z_from(k)], nm_s.at[k - 1], nm_r.at[k - 1], dev_z(k)),
+
+    def small_xy(k):
+        there, dev = around[k]
+        return (
+            remote(SR.at[place, 1], SR.at[place, 1], fs_s.at[3 + k], fs_r.at[3 + k], dev),
+            remote(SR.at[there, 1], SR.at[there, 1], fs_s.at[3 + k], fs_r.at[3 + k], dev),
         )
-        for k in range(1, NZ)
-    ]
+
+    def rows_done():
+        def finish_tile(i):
+            rows = rows_at(i, TR)
+            flag = FL[rows, :]
+            value = GR[rows, :]
+            SG[4:5, :] += jnp.sum(value * flag, axis=0, keepdims=True)
+            GR[rows, :] = value * (1.0 - flag)
+
+        loop(SEQ // TR, finish_tile)
+        igrad_copy.start()
+        SR[z, 0] = SG[...]
+        for k in range(1, NZ):
+            small_z(k)[0].start()
+
+    def small_sums():
+        for k in range(1, NZ):
+            small_z(k)[1].wait_recv()
+        SR[place, 1] = SR[0, 0] + SR[1, 0] + SR[2, 0] + SR[3, 0]
+        for k in range(3):
+            small_xy(k)[0].start()
+
+    lead_in = LEAD_TWO
+    merge = PAIRS - 1
+
+    def tick(m):
+        i, q = m // 2 - lead_in, m % 2
+        is_back = jnp.logical_or(i == merge, i > merge + 1)
+
+        @pl.when(jnp.logical_not(is_back))
+        def _():
+            forward_tick(jnp.where(i < merge, i, merge), q)
+
+        @pl.when(is_back)
+        def _():
+            backward_tick(jnp.where(i == merge, 0, i - PAIRS), q)
+
+    loop(2 * (2 * PAIRS + lead_in + LAG_LAST), tick)
+
+    own_square = jnp.sum(jnp.sum(NB[...], axis=1, keepdims=True), axis=0, keepdims=True)
+    NZC[z, c] = jnp.broadcast_to(own_square, (8, 128))
+    nm_z = []
+    for j, (zz, cc, frm, dev) in enumerate(
+        [(z, 1 - c, z, dev_core)]
+        + [(z_to(k), c, z_from(k), dev_z(k)) for k in range(1, NZ)]
+        + [(z_to(k), 1 - c, z_from(k), dev_zc(k)) for k in range(1, NZ)]
+    ):
+        got = NZC.at[frm, cc]
+        nm_z.append(
+            (
+                remote(NZC.at[z, c], NZC.at[z, c], nm_s.at[j], nm_r.at[j], dev),
+                remote(got, got, nm_s.at[j], nm_r.at[j], dev),
+            )
+        )
     for s, _ in nm_z:
         s.start()
-    sg_y.wait_recv()
-    total_small = SR[1, 2] + SR[1, 3]
+    for k in range(3):
+        small_xy(k)[1].wait_recv()
+    total_small = SR[0, 1] + SR[1, 1] + SR[2, 1] + SR[3, 1]
     out_small[...] = total_small
     small_square = jnp.sum(jnp.sum(total_small * total_small, axis=1, keepdims=True), axis=0, keepdims=True)
     for _, r in nm_z:
         r.wait_recv()
-    NB[5] = NB[1] + NB[2] + NB[3] + NB[4]
-    nm_x = remote(NB.at[5], NB.at[6], nm_s.at[3], nm_r.at[3], dev_x)
-    nm_x.start()
-    nm_x.wait_recv()
-    NB[7] = NB[5] + NB[6]
-    nm_y = remote(NB.at[7], NB.at[8], nm_s.at[4], nm_r.at[4], dev_y)
-    nm_y.start()
-    nm_y.wait_recv()
-    NB[9] = NB[7] + NB[8]
-    nm_c = remote(NB.at[9], NB.at[10], nm_s.at[5], nm_r.at[5], dev_core)
-    nm_c.start()
-    nm_c.wait_recv()
-    out_norm[...] = jnp.sqrt(NB[9] + NB[10] + small_square)
-
-    for s, _ in sg_z + nm_z:
+    square = NZC[0, 0] + NZC[0, 1]
+    for zz in range(1, NZ):
+        square = square + (NZC[zz, 0] + NZC[zz, 1])
+    NXY[place] = square
+    nm_xy = [
+        (
+            remote(NXY.at[place], NXY.at[place], nm_s.at[7 + k], nm_r.at[7 + k], dev),
+            remote(NXY.at[there], NXY.at[there], nm_s.at[7 + k], nm_r.at[7 + k], dev),
+        )
+        for k, (there, dev) in enumerate(around)
+    ]
+    for s, _ in nm_xy:
+        s.start()
+    for _, r in nm_xy:
+        r.wait_recv()
+    out_norm[...] = jnp.sqrt(NXY[0] + NXY[1] + NXY[2] + NXY[3] + small_square)
+
+    for s, _ in [small_z(k) for k in range(1, NZ)] + [small_xy(k) for k in range(3)] + nm_z + nm_xy + gain_z:
         s.wait_send()
-    for s in (sg_x, sg_y, nm_x, nm_y, nm_c):
-        s.wait_send()
+    gain_x[0].wait_send()
+    patch_out.wait_send()
     loop(PAIRS, scatter_sent)
     igrad_copy.wait()
 
 
-def big_step(wloc, patches, cotangent, mask_index, mask_count, small):
+def big_step(weights, patches, cotangent, mask_index, mask_count, small):
     vm = pl.BlockSpec(memory_space=pltpu.VMEM)
     hb = pl.BlockSpec(memory_space=pl.ANY)
     sm = pl.BlockSpec(memory_space=pltpu.SMEM)
     dma = pltpu.SemaphoreType.DMA
     V = pltpu.VMEM
     scratch = [
-        V((PAIRS, 2, NZ, NX, 2, HALF, WIDE), BF16),
+        V((PAIRS, 2, NZ, NX, PARTS, PART, WIDE), BF16),
+        V((LEAD_ONE, 2, ROWS, COL), F32),
         V((2, SEQ, D), F32),
         V((2, SEQ, D), F32),
         V((2, SEQ, D), BF16),
@@ -732,7 +757,7 @@
         V((SEQ, D), BF16),
         V((D, SEQ), BF16),
         V((D, SEQ), BF16),
-        V((2, SEQ, WIDE), BF16),
+        V((2, 2, SEQ, WIDE), BF16),
         V((2, SEQ, COL), BF16),
         V((2, SEQ, WIDE), BF16),
         V((2, SEQ, COL), BF16),
@@ -740,37 +765,42 @@
         V((8, D), F32),
         V((NZ, NX, 8, 128), F32),
         V((8, D), F32),
-        V((2, 4, 8, D), F32),
-        V((11, 8, 128), F32),
-        V((PAIRS, NZ, NX, HALF, WIDE), BF16),
-        V((PAIRS, 2, NZ, HALF, WIDE), BF16),
-        V((PAIRS, 2, 6, HALF, WIDE), BF16),
-        V((PAIRS, 2, 3, HALF, WIDE), BF16),
-        dma((PAIRS, 2, 5)), dma((PAIRS, 2, 5)),
-        dma((PAIRS, 2, 5)), dma((PAIRS, 2, 5)),
+        V((4, 2, 8, D), F32),
+        V((8, 128), F32),
+        V((NZ, 2, 8, 128), F32),
+        V((4, 8, 128), F32),
+        V((PAIRS + PAIRS // 2, NZ, NX, PART, WIDE), BF16),
+        V((PAIRS + PAIRS // 2, 2, NZ, PART, WIDE), BF16),
+        V((PAIRS, 2, NZ, PART, WIDE), BF16),
+        V((PAIRS, NZ - 1, 2, PART, WIDE), BF16),
+        V((PAIRS, 2, NZ - 1, PART, WIDE), BF16),
+        V((PAIRS, PART, WIDE), BF16),
+        dma((LEAD_ONE,)),
+        dma((PAIRS, PARTS, 5)), dma((PAIRS, PARTS, 5)),
+        dma((PAIRS, PARTS, 5)), dma((PAIRS, PARTS, 5)),
         dma((2,)), dma((2, 2)),
         dma((2,)), dma((2,)), dma((4,)),
         dma((4,)), dma((4,)),
-        dma((5,)), dma((5,)),
         dma((6,)), dma((6,)),
+        dma((10,)), dma((10,)),
     ]
     return pl.pallas_call(
         step_kernel,
         out_shape=(
             jax.ShapeDtypeStruct((TM, D), F32),
             jax.ShapeDtypeStruct((TM, D), F32),
-            jax.ShapeDtypeStruct((PAIRS, 2, HALF, WIDE), F32),
+            jax.ShapeDtypeStruct((PAIRS, PARTS, PART, WIDE), F32),
             jax.ShapeDtypeStruct((8, D), F32),
             jax.ShapeDtypeStruct((8, 128), F32),
         ),
-        in_specs=[vm, hb, hb, vm, sm, vm],
+        in_specs=[hb, hb, hb, vm, sm, vm],
         out_specs=(hb, hb, vm, vm, vm),
         scratch_shapes=scratch,
         compiler_params=pltpu.CompilerParams(
             collective_id=0, has_side_effects=True, vmem_limit_bytes=62 << 20
         ),
         name="train_step",
-    )(wloc, patches, cotangent, mask_index, mask_count, small)
+    )(weights, patches, cotangent, mask_index, mask_count, small)
 
 
 def adam_values(weight_in, moment_one, moment_two, gradient, step_rate, decay_rate):
@@ -784,50 +814,82 @@
     return (updated, moment_one, moment_two)
 
 
-def adam_kernel(norm, grad, w, m, v, nw, nm, nv):
+def adam_kernel(
+    norm, grad, small_total, small, small_one, small_two, block, igrad, w, m, v,
+    nw, nm, nv, ns, nsm, nsv, grad_norm, block_out, igrad_out,
+):
     factor = jnp.minimum(1.0, CLIP_MAX / norm[0:1, 0:1])
-    g = grad[0].reshape(ROWS, WIDE) * factor
-    for j in range(2):
-        nw[j], nm[j], nv[j] = adam_values(w[j], m[j], v[j], g[:, j * COL : (j + 1) * COL], D ** (-0.5), DECAY_RATE)
-
-
-def adam_matrices(norm, grad, weights, first, second):
-    shape = weights.shape
+    for i in range(PAIRS // ADAM_STEPS):
+        g = grad[i].reshape(ROWS, WIDE) * factor
+        for j in range(2):
+            k = 2 * i + j
+            nw[k], nm[k], nv[k] = adam_values(
+                w[k], m[k], v[k], g[:, j * COL : (j + 1) * COL], D ** (-0.5), DECAY_RATE
+            )
+    block_out[...] = block[...]
+    igrad_out[...] = igrad[...]
+
+    @pl.when(pl.program_id(0) == 0)
+    def _():
+        first = ROWS * lax.axis_index("wide")
+        row = lax.broadcasted_iota(jnp.int32, (D, ROWS), 0)
+        column = lax.broadcasted_iota(jnp.int32, (D, ROWS), 1)
+        pick = jnp.where(row == column + first, 1.0, 0.0)
+        own = lax.dot_general(
+            small_total[...], pick, (((1,), (0,)), ((), ())),
+            precision=lax.Precision.HIGHEST, preferred_element_type=F32,
+        )[0:5]
+        ns[...], nsm[...], nsv[...] = adam_values(
+            small[...], small_one[...], small_two[...], own * factor, RATE_SMALL, 0.0
+        )
+        grad_norm[...] = norm[0:1, 0:1]
+
+
+def adam_all(norm, grad, small_total, smalls, rows, matrices):
+    shape = matrices[0].shape
     flat = (LAYERS * 12, ROWS, COL)
-    blk = pl.BlockSpec((2, ROWS, COL), lambda i: (i, 0, 0))
+    blk = pl.BlockSpec((2 * PAIRS // ADAM_STEPS, ROWS, COL), lambda i: (i, 0, 0))
+    row_blk = pl.BlockSpec((TM // ADAM_STEPS, D), lambda i: (i, 0))
+
+    def whole(*dims):
+        return pl.BlockSpec(dims, lambda i: (0,) * len(dims))
+
     outs = pl.pallas_call(
         adam_kernel,
-        grid=(PAIRS,),
-        out_shape=tuple(jax.ShapeDtypeStruct(flat, F32) for _ in range(3)),
+        grid=(ADAM_STEPS,),
+        out_shape=(
+            *(jax.ShapeDtypeStruct(flat, F32) for _ in range(3)),
+            *(jax.ShapeDtypeStruct((5, ROWS), F32) for _ in range(3)),
+            jax.ShapeDtypeStruct((1, 1), F32),
+            *(jax.ShapeDtypeStruct((TM, D), F32) for _ in range(2)),
+        ),
         in_specs=[
-            pl.BlockSpec((8, 128), lambda i: (0, 0)),
-            pl.BlockSpec((1, 2, HALF, WIDE), lambda i: (i, 0, 0, 0)),
+            whole(8, 128),
+            pl.BlockSpec((PAIRS // ADAM_STEPS, PARTS, PART, WIDE), lambda i: (i, 0, 0, 0)),
+            whole(8, D),
+            *(whole(5, ROWS) for _ in range(3)),
+            row_blk, row_blk,
             blk, blk, blk,
         ],
-        out_specs=(blk, blk, blk),
+        out_specs=(
+            blk, blk, blk, *(whole(5, ROWS) for _ in range(3)), whole(1, 1), row_blk, row_blk,
+        ),
+        compiler_params=pltpu.CompilerParams(vmem_limit_bytes=62 << 20),
         name="adam",
-    )(norm, grad, weights.reshape(flat), first.reshape(flat), second.reshape(flat))
-    return tuple(o.reshape(shape) for o in outs)
+    )(norm, grad, small_total, *smalls, *rows, *(a.reshape(flat) for a in matrices))
+    return tuple(o.reshape(shape) for o in outs[:3]), outs[3:6], outs[6].reshape(()), outs[7:]
 
 
 def shards(patches, cotangent, mask_index, mask_count, weights, first_moment, second_moment,
            small_params, small_first, small_second):
-    owned_rows = weights.shape[2]
-    low = weights.astype(BF16).reshape(PAIRS, 2, ROWS, COL)
-    wloc = jnp.concatenate([low[:, 0], low[:, 1]], axis=-1).reshape(PAIRS, 2, HALF, WIDE)
     block_output, input_grad, grad_own, small_total, norm = big_step(
-        wloc, patches, cotangent, mask_index, mask_count, small_params
-    )
-    new_weights, new_first, new_second = adam_matrices(norm, grad_own, weights, first_moment, second_moment)
-    grad_norm = norm[0, 0]
-    factor = jnp.minimum(1.0, CLIP_MAX / grad_norm)
-    first_col = lax.axis_index("wide") * owned_rows
-    small_own = lax.dynamic_slice_in_dim(small_total, first_col, owned_rows, 1)[0:5]
-    new_small, new_small_first, new_small_second = adam_values(
-        small_params, small_first, small_second, small_own * factor, RATE_SMALL, 0.0
-    )
-    return (block_output, input_grad, new_weights, new_first, new_second,
-            new_small, new_small_first, new_small_second, grad_norm)
+        weights.reshape(LAYERS * 12, ROWS, COL), patches, cotangent, mask_index, mask_count, small_params
+    )
+    new_matrices, new_smalls, grad_norm, rows = adam_all(
+        norm, grad_own, small_total, (small_params, small_first, small_second),
+        (block_output, input_grad), (weights, first_moment, second_moment),
+    )
+    return (*rows, *new_matrices, *new_smalls, grad_norm)
 
 
 def layer_norm(values, gain):

time: 363 us -> 288 us (0.79)
  Pallas kernels: 353 us -> 287 us
  local copies, waits for them, and re-layouts: 3.84 us -> 0 us
  other arithmetic: 3.7 us -> 0 us
    pallas_call x1, Pallas kernels: 342 us -> 279 us  [big_step(): pl.pallas_call(step_kernel, out_shape=(jax.ShapeDtypeStruct((TM, D), F32)...]
    pallas_call x1, Pallas kernels: 11.8 us -> 7.82 us  [adam_all(): pl.pallas_call(adam_kernel, grid=(ADAM_STEPS,), out_shape=(*(jax.ShapeDty...]
where the time goes in v2:
time: 288 us
  Pallas kernels  287 us (100%)
    pallas_call x1, Pallas kernels, big_step(): pl.pallas_call(step_kernel, out_shape=(jax.ShapeDtypeStruct((TM, D), F32)...  279 us
    pallas_call x1, Pallas kernels, adam_all(): pl.pallas_call(adam_kernel, grid=(ADAM_STEPS,), out_shape=(*(jax.ShapeDty...  7.82 us

profile of v2, /device:TPU:0, one launch (start us, length us, event | category | flops | bytes accessed | tf_op | source)
XLA Modules:
  0.0 287.5 jit_solution(18016793760263949900)
XLA Ops:
  0.6 278.9 %train_step.1 = (f32[256,768]{1,0:T(8,128)}, f32[256,768]{1,0:T(8,128)}, f32[12,3,32,384]{3,2,1,0:T(8,128)}, f32[8,768]{1,0:T(8,128)}, f32[8,128]{1,0:T(8,128)}) custom-call(f32[24,96,192]{2,1,0:T(8,128)} %bitcast.7, bf16[256,768]{1,0:T(8,128)(2,1)} %patch.1, f32[256,768]{1,0:T(8,128)} %cot.1, s32[2,450]{1,0:T(2,128)} %mask_index.1, s32[2]{0:T(128)} %mask_count.1, ...), custom_call_target="tpu_custom_call" | custom-call | tf_op jit(solution)/shard_map/train_step/pallas_call | solution.py:787
  279.6 7.8 %adam.1 = (f32[24,96,192]{2,1,0:T(8,128)}, f32[24,96,192]{2,1,0:T(8,128)}, f32[24,96,192]{2,1,0:T(8,128)}, f32[5,96]{1,0:T(8,128)}, f32[5,96]{1,0:T(8,128)}, /*i...) custom-call(f32[8,128]{1,0:T(8,128)} %get-tuple-element.23.norm, ...), custom_call_target="tpu_custom_call" | custom-call | tf_op jit(solution)/shard_map/adam/pallas_call | solution.py:857

commit v3 on v2

--- a/solution.py
+++ b/solution.py
@@ -39,9 +39,66 @@
 TR = 64
 HEADS_Y = COL // HD
 
-BACK_ORDER = (4, 5, 2, 3, 1, 0)
-LEAD_ONE, LEAD_TWO, LEAD_THREE = 4, 3, 2
-LAG_TWO, LAG_THREE, LAG_LAST = 2, 4, 6
+WSLOTS = 4
+STEPS = 100
+BEGUN = 3
+PLAN_WORDS = (
+    (
+        0, 0, 0, 0, 32, 516, 0, 8240, 4608, 131073, 0, 4112,
+        0, 256, 272, 4099, 65792, 32, 4096, 65537, 256, 65552, 8192, 65792,
+        0, 0, 0, 65536, 256, 69664, 0, 4352, 256, 0, 0, 69632,
+        0, 65536, 4096, 0, 65536, 0, 0, 0, 65536, 0, 0, 0,
+        0, 0, 0, 0, 0, 0, 0, 0, 0, 0, 0, 0,
+        0, 0, 0, 0, 0, 0, 0, 0, 0, 0, 0, 0,
+        0, 0, 0, 0, 0, 0, 0, 0, 0, 0, 0, 0,
+        0, 0, 0, 0, 0, 0, 0, 0, 0, 0, 0, 0,
+        0, 0, 0, 0,
+    ),
+    (
+        0, 0, 0, 0, 0, 3, 0, 32, 8704, 7, 0, 12368,
+        0, 1024, 1376, 16392, 132608, 112, 20480, 196619, 1792, 262288, 24576, 329728,
+        0, 0, 0, 393216, 2304, 491680, 0, 39424, 2816, 0, 0, 565248,
+        0, 589824, 45056, 0, 655360, 0, 0, 0, 720896, 0, 0, 0,
+        0, 0, 0, 0, 0, 0, 0, 0, 0, 0, 0, 0,
+        0, 0, 0, 0, 0, 0, 0, 0, 0, 0, 0, 0,
+        0, 0, 0, 0, 0, 0, 0, 0, 0, 0, 0, 0,
+        0, 0, 0, 0, 0, 0, 0, 0, 0, 0, 0, 0,
+        0, 0, 0, 0,
+    ),
+    (
+        0, 0, 0, 0, 0, 0, 0, 0, 0, 0, 0, 0,
+        0, 0, 0, 0, 0, 0, 0, 0, 0, 0, 0, 0,
+        0, 0, 0, 0, 0, 0, 0, 0, 0, 0, 0, 0,
+        0, 0, 0, 0, 0, 0, 0, 1, 0, 0, 0, 1,
+        0, 0, 1, 16, 1, 0, 0, 0, 256, 0, 0, 16,
+        0, 33, 0, 257, 4096, 16, 256, 257, 0, 0, 4352, 1,
+        16, 0, 4096, 4128, 4353, 256, 1, 256, 0, 0, 1, 69648,
+        0, 0, 0, 0, 0, 0, 16, 0, 200705, 0, 256, 65536,
+        0, 4352, 16, 475664,
+    ),
+    (
+        0, 0, 0, 0, 0, 0, 0, 0, 0, 0, 0, 0,
+        0, 0, 0, 0, 0, 0, 0, 0, 0, 0, 0, 0,
+        0, 0, 0, 0, 0, 0, 0, 0, 0, 0, 0, 0,
+        0, 0, 0, 0, 0, 0, 0, 0, 0, 0, 0, 1,
+        0, 0, 2, 0, 3, 0, 0, 0, 0, 0, 0, 16,
+        0, 36, 0, 261, 0, 64, 512, 774, 0, 0, 5120, 7,
+        80, 0, 8192, 12384, 17672, 1536, 9, 1792, 0, 0, 10, 20608,
+        0, 0, 0, 0, 0, 0, 144, 0, 90123, 0, 2048, 262144,
+        0, 30976, 160, 363184,
+    ),
+    (
+        0, 0, 1, 0, 0, 2, 0, 3, 0, 4, 0, 5,
+        6, 70, 7, 8, 0, 9, 0, 73, 0, 10, 0, 11,
+        12, 35, 0, 36, 0, 37, 38, 102, 39, 40, 0, 41,
+        0, 105, 45, 0, 42, 46, 110, 0, 43, 47, 111, 44,
+        48, 49, 50, 51, 52, 53, 54, 55, 56, 118, 119, 120,
+        57, 58, 59, 60, 13, 14, 78, 15, 79, 16, 17, 18,
+        19, 20, 21, 22, 23, 24, 86, 87, 88, 25, 26, 27,
+        28, 29, 0, 0, 0, 0, 0, 0, 0, 30, 0, 0,
+        0, 0, 0, 0,
+    ),
+)
 
 
 def mm(a, b):
@@ -72,8 +129,8 @@
     weights, patch, cot, mask_index, mask_count, small,
     out_block, out_igrad, out_grad, out_small, out_norm,
     G, WF, S, R1, NRM, NRM2, QK, V, MIX, GP, HID, GR, ACC, XS, XR, BK, TA, TB, GU, GM, DQK, DV,
-    FL, GAIN, GPIECE, SG, SR, NB, NZC, NXY, RB0Y, RB0X, RB1, RB1Z, RB2, RB2X,
-    wf_s, ag_s, ag_r, rs_s, rs_r, ex_s, ex_r, in_s, in_r, lc_s, gn_s, gn_r, fs_s, fs_r, nm_s, nm_r,
+    FL, GAIN, GPIECE, SG, SR, NB, NZC, NXY, RB0Y, RB0X, RB1, RB2, RB2X, RBZ, RBM, RBMZ,
+    wf_s, ag_s, ag_r, ex_s, ex_r, in_s, in_r, lc_s, gn_s, gn_r, fs_s, fs_r, nm_s, nm_r,
 ):
     wide = lax.axis_index("wide")
     narrow = lax.axis_index("narrow")
@@ -99,9 +156,9 @@
         return (z_to(k) * NX + x, 2 * y + 1 - c)
 
     def load_pair(p):
-        return pltpu.make_async_copy(weights.at[pl.ds(2 * p, 2)], WF.at[p % LEAD_ONE], wf_s.at[p % LEAD_ONE])
-
-    for p in range(LEAD_ONE):
+        return pltpu.make_async_copy(weights.at[pl.ds(2 * p, 2)], WF.at[p % WSLOTS], wf_s.at[p % WSLOTS])
+
+    for p in range(WSLOTS):
         load_pair(p).start()
 
     greeted = [dev_core, dev_x, dev_y, dev_xy] + [dev(k) for k in range(1, NZ) for dev in (dev_z, dev_zc)]
@@ -119,74 +176,121 @@
         return lambda: remote(*what)
 
     ALL = slice(None)
-    partners = {
-        "x": [(3, dev_x, 1 - x, 1 - x)],
-        "y": [(4, dev_y, 1 - y, 1 - y)],
-        "z": [(k - 1, dev_z(k), z_to(k), z_from(k)) for k in range(1, NZ)],
-    }
     own = {"x": x, "y": y, "z": z}
+    far = NZ - 1
+    inner = jnp.logical_and(z > 0, z < far)
+    outer = jnp.logical_or(z == 0, z == far)
 
     def block(p, h, where):
         return G.at[p, where["y"], where["z"], where["x"], h]
 
     def gather_order(even, h):
         if h == 0:
-            return ("z", "x", "y")
-        if h == 1:
-            return ("z", "y", "x")
-        return ("x", "z", "y") if even else ("y", "z", "x")
-
-    def gather_copies(p, h, order, phase):
-        axis = order[phase]
-        have = {q: (ALL if q in order[:phase] else own[q]) for q in own}
-        src = block(p, h, have)
-        sends, recvs = [], []
-        for slot, dev, _, frm in partners[axis]:
-            sends.append(lazy(src, src, ag_s.at[p, h, slot], ag_r.at[p, h, slot], dev))
-            got = block(p, h, {**have, axis: frm})
-            recvs.append(lazy(got, got, ag_s.at[p, h, slot], ag_r.at[p, h, slot], dev))
-        return sends, recvs
-
-    def by_kind(p, action):
+            return ("z", "x", "y") if even else ("z", "y", "x")
+        return ("x", "z", "y") if h == 1 else ("y", "z", "x")
+
+    def holding(axes):
+        return {q: (ALL if q in axes else own[q]) for q in own}
+
+    def along(axis):
+        return (3, dev_x, 1 - x) if axis == "x" else (4, dev_y, 1 - y)
+
+    def along_z(action):
+        @pl.when(z != far)
+        def _():
+            action(1)
+
+        action(2)
+
+        @pl.when(z != 0)
+        def _():
+            action(3)
+
+    def each_part(p, action):
         @pl.when(p % 2 == 0)
         def _():
-            action(True)
+            action(0, gather_order(True, 0))
 
         @pl.when(p % 2 == 1)
         def _():
-            action(False)
-
-    def gather_issue(p, phase):
-        def action(even):
-            for h in range(PARTS):
-                order = gather_order(even, h)
-                if phase > 0:
-                    for r in gather_copies(p, h, order, phase - 1)[1]:
-                        r().wait_recv()
-                if phase < 3:
-                    for s in gather_copies(p, h, order, phase)[0]:
-                        s().start()
-
-        by_kind(p, action)
+            action(0, gather_order(False, 0))
+
+        for h in range(1, PARTS):
+            action(h, gather_order(True, h))
+
+    def gather_plain(p, h, order, axis):
+        slot, dev, there = along(axis)
+        have = holding(order[: order.index(axis)])
+        src = block(p, h, have)
+        got = block(p, h, {**have, axis: there})
+        send, recv = ag_s.at[p, h, slot], ag_r.at[p, h, slot]
+        return lazy(src, src, send, recv, dev), lazy(got, got, send, recv, dev)
+
+    def gather_z(p, h, order, k):
+        have = holding(order[: order.index("z")])
+        src = block(p, h, have)
+        got = block(p, h, {**have, "z": z_from(k)})
+        send, recv = ag_s.at[p, h, k - 1], ag_r.at[p, h, k - 1]
+        return lazy(src, src, send, recv, dev_z(k)), lazy(got, got, send, recv, dev_z(k))
+
+    def gather_relay(p, h, order):
+        have = holding(order[: order.index("z")])
+        src = block(p, h, {**have, "z": z_from(2)})
+        dev = (far * (z - 1) * NX + x, narrow)
+        return lazy(src, src, ag_s.at[p, h, 5], ag_r.at[p, h, 2 * (z - 1)], dev)
+
+    def gather_steps(order):
+        at = order.index("z") + 1
+        return order[:at] + ("relay",) + order[at:]
+
+    def gather_issue(p, step):
+        def action(h, order):
+            steps = gather_steps(order)
+            before = steps[step - 1] if step > 0 else None
+            if before == "z":
+                gather_z(p, h, order, 2)[1]().wait_recv()
+            elif before == "relay":
+                for k in (1, 3):
+                    gather_z(p, h, order, k)[1]().wait_recv()
+            elif before is not None:
+                gather_plain(p, h, order, before)[1]().wait_recv()
+            if step == len(steps):
+                return
+            if steps[step] == "z":
+                along_z(lambda k: gather_z(p, h, order, k)[0]().start())
+            elif steps[step] == "relay":
+
+                @pl.when(inner)
+                def _():
+                    gather_relay(p, h, order)().start()
+
+            else:
+                gather_plain(p, h, order, steps[step])[0]().start()
+
+        each_part(p, action)
 
     def gather_sent(p):
-        def action(even):
-            for h in range(PARTS):
-                for phase in range(3):
-                    for s in gather_copies(p, h, gather_order(even, h), phase)[0]:
-                        s().wait_send()
-
-        by_kind(p, action)
+        def action(h, order):
+            along_z(lambda k: gather_z(p, h, order, k)[0]().wait_send())
+
+            @pl.when(inner)
+            def _():
+                gather_relay(p, h, order)().wait_send()
+
+            for axis in ("x", "y"):
+                gather_plain(p, h, order, axis)[0]().wait_send()
+
+        each_part(p, action)
 
     def pack(p):
         load_pair(p).wait()
-        slot = p % LEAD_ONE
+        slot = p % WSLOTS
         both = jnp.concatenate([WF[slot, 0].astype(BF16), WF[slot, 1].astype(BF16)], axis=1)
         G[p, y, z, x] = both.reshape(PARTS, PART, WIDE)
 
-        @pl.when(p + LEAD_ONE < PAIRS)
+        @pl.when(p + WSLOTS < PAIRS)
         def _():
-            load_pair(p + LEAD_ONE).start()
+            load_pair(p + WSLOTS).start()
 
     half = TM * c
     BKh = BK.at[pl.ds(pl.multiple_of(half, TM), TM)]
@@ -222,9 +326,9 @@
         pack(p)
         gather_issue(p, 0)
 
-    loop(LEAD_ONE, begin)
+    loop(BEGUN, begin)
     cot_out.start()
-    loop(PAIRS - LEAD_ONE, lambda i: pack(i + LEAD_ONE))
+    loop(PAIRS - BEGUN, lambda i: pack(i + BEGUN))
 
     index_row = mask_index[pl.ds(y, 1), :]
     count = mask_count[y]
@@ -233,29 +337,31 @@
     hits = jnp.where(jnp.logical_and(spot == index_row, live), 1.0, 0.0)
     FL[...] = jnp.max(hits, axis=1, keepdims=True)
 
-    for _, r in gain_z:
-        r.wait_recv()
-    gain_x[0].start()
-    gain_x[1].wait_recv()
-    lane = lax.broadcasted_iota(jnp.int32, (128, D), 0)
-    feature = lax.broadcasted_iota(jnp.int32, (128, D), 1)
-    gains = jnp.zeros((8, D), F32)
-    for zz in range(NZ):
-        for xx in range(NX):
-            place = jnp.logical_and(feature - ROWS * (zz * NX + xx) == lane, lane < ROWS)
-            gains = gains + mm(GPIECE[zz, xx].astype(BF16), jnp.where(place, 1.0, 0.0).astype(BF16))
-    GAIN[...] = gains
-
-    patch_own.wait()
-    patch_in.wait_recv()
-    embed = GAIN[4:5, :]
-
-    def mask_tile(i):
-        rows = rows_at(i, TR)
-        flag = FL[rows, :]
-        S[0, rows, :] = BK[rows, :].astype(F32) * (1.0 - flag) + flag * embed
-
-    loop(SEQ // TR, mask_tile)
+    def gains_across(l, yy):
+        for _, r in gain_z:
+            r.wait_recv()
+        gain_x[0].start()
+
+    def first_rows(l, yy):
+        gain_x[1].wait_recv()
+        lane = lax.broadcasted_iota(jnp.int32, (128, D), 0)
+        feature = lax.broadcasted_iota(jnp.int32, (128, D), 1)
+        gains = jnp.zeros((8, D), F32)
+        for zz in range(NZ):
+            for xx in range(NX):
+                place = jnp.logical_and(feature - ROWS * (zz * NX + xx) == lane, lane < ROWS)
+                gains = gains + mm(GPIECE[zz, xx].astype(BF16), jnp.where(place, 1.0, 0.0).astype(BF16))
+        GAIN[...] = gains
+        patch_own.wait()
+        patch_in.wait_recv()
+        embed = GAIN[4:5, :]
+
+        def mask_tile(i):
+            rows = rows_at(i, TR)
+            flag = FL[rows, :]
+            S[0, rows, :] = BK[rows, :].astype(F32) * (1.0 - flag) + flag * embed
+
+        loop(SEQ // TR, mask_tile)
 
     def norm_parts(values):
         centre = values - jnp.mean(values, axis=-1, keepdims=True)
@@ -313,33 +419,32 @@
 
         loop(SEQ // TM, tile)
 
-    def attend_back(l, yy):
-        for hd in range(HEADS_Y):
-            lo = hd * HD
-            k = QK[l, yy, :, COL + lo : COL + lo + HD]
-            v = V[l, yy, :, lo : lo + HD]
-
-            def tile(i, carry):
-                dk, dv = carry
-                rows = rows_at(i, TM)
-                q = QK[l, yy, rows, lo : lo + HD]
-                dm = GM[yy, rows, lo : lo + HD]
-                s = mm_nt(k, q) * SCALE
-                e = jnp.exp(s - jnp.max(s, axis=0, keepdims=True))
-                probs = e / jnp.sum(e, axis=0, keepdims=True)
-                dp = mm_nt(v, dm)
-                ds = probs * (dp - jnp.sum(probs * dp, axis=0, keepdims=True))
-                ds = ds.astype(BF16)
-                dv = dv + mm(probs.astype(BF16), dm)
-                dk = dk + mm(ds, q)
-                dq = mm_tn(ds, k) * SCALE
-                DQK[yy, rows, lo : lo + HD] = dq.astype(BF16)
-                return dk, dv
-
-            zero = jnp.zeros((SEQ, HD), F32)
-            dk, dv = lax.fori_loop(0, SEQ // TM, tile, (zero, zero))
-            DQK[yy, :, COL + lo : COL + lo + HD] = (dk * SCALE).astype(BF16)
-            DV[yy, :, lo : lo + HD] = dv.astype(BF16)
+    def attend_back(l, yy, hd):
+        lo = hd * HD
+        k = QK[l, yy, :, COL + lo : COL + lo + HD]
+        v = V[l, yy, :, lo : lo + HD]
+
+        def tile(i, carry):
+            dk, dv = carry
+            rows = rows_at(i, TM)
+            q = QK[l, yy, rows, lo : lo + HD]
+            dm = GM[yy, rows, lo : lo + HD]
+            s = mm_nt(k, q) * SCALE
+            e = jnp.exp(s - jnp.max(s, axis=0, keepdims=True))
+            probs = e / jnp.sum(e, axis=0, keepdims=True)
+            dp = mm_nt(v, dm)
+            ds = probs * (dp - jnp.sum(probs * dp, axis=0, keepdims=True))
+            ds = ds.astype(BF16)
+            dv = dv + mm(probs.astype(BF16), dm)
+            dk = dk + mm(ds, q)
+            dq = mm_tn(ds, k) * SCALE
+            DQK[yy, rows, lo : lo + HD] = dq.astype(BF16)
+            return dk, dv
+
+        zero = jnp.zeros((SEQ, HD), F32)
+        dk, dv = lax.fori_loop(0, SEQ // TM, tile, (zero, zero))
+        DQK[yy, :, COL + lo : COL + lo + HD] = (dk * SCALE).astype(BF16)
+        DV[yy, :, lo : lo + HD] = dv.astype(BF16)
 
     def up_part(l, u, yy, p):
         ACC[:, 0:WIDE] = mm(NRM2[l], matrix(p, yy))
@@ -354,116 +459,170 @@
 
         loop(SEQ // TR, gelu)
 
-    def forward_slot(slot, step, l):
-        p = l * PER + slot
-        if slot == 0:
-            if step == 0:
-                norm_into(NRM.at[l], S.at[l], 2 * l)
-            else:
-
-                def project(yy):
-                    QK[l, yy] = mm(NRM[l], matrix(p, yy)).astype(BF16)
-
-                loop(2, project)
-        elif slot == 1:
-            if step == 0:
-
-                def project_v(yy):
-                    V[l, yy] = mm(NRM[l], matrix(p, yy)[:, :COL]).astype(BF16)
-
-                loop(2, project_v)
-                attend(l, 0)
-            else:
-                attend(l, 1)
-                total = mm_nt(MIX[l, 0], matrix(p, 0)[:, COL:])
-                give(0, total + mm_nt(MIX[l, 1], matrix(p, 1)[:, COL:]))
-        elif slot in (2, 3):
-            if slot == 2 and step == 0:
-
-                def take(rows, total):
-                    R1[l, rows, :] = S[l, rows, :] + total
-
-                receive(0, take)
-                norm_into(NRM2.at[l], R1.at[l], 2 * l + 1)
-            up_part(l, slot - 2, step, p)
-        elif slot == 4:
-            if step == 0:
-                ACC[...] = mm_nt(HID[l, 0, 0], matrix(p, 0)) + mm_nt(HID[l, 0, 1], matrix(p, 1))
-        elif step == 0:
-            total = ACC[...] + mm_nt(HID[l, 1, 0], matrix(p, 0))
-            give(1, total + mm_nt(HID[l, 1, 1], matrix(p, 1)))
-        else:
-
-            def take(rows, total):
-                value = R1[l, rows, :] + total
-
-                @pl.when(l == 0)
-                def _():
-                    S[1, rows, :] = value
-
-                @pl.when(l == 1)
-                def _():
-                    ACC[rows, :] = value
-
-            receive(1, take)
+    def ln_one(l, yy):
+        norm_into(NRM.at[l], S.at[l], 2 * l)
+
+    def project_qk(l, yy):
+        def one(side):
+            QK[l, side] = mm(NRM[l], matrix(l * PER, side)).astype(BF16)
+
+        loop(2, one)
+
+    def project_v(l, yy):
+        def one(side):
+            V[l, side] = mm(NRM[l], matrix(l * PER + 1, side)[:, :COL]).astype(BF16)
+
+        loop(2, one)
+
+    def attn_out(l, yy):
+        p = l * PER + 1
+        total = mm_nt(MIX[l, 0], matrix(p, 0)[:, COL:])
+        give(0, total + mm_nt(MIX[l, 1], matrix(p, 1)[:, COL:]))
+
+    def attn_resid(l, yy):
+        def take(rows, total):
+            R1[l, rows, :] = S[l, rows, :] + total
+
+        receive(0, take)
+        norm_into(NRM2.at[l], R1.at[l], 2 * l + 1)
+
+    def up(l, u):
+        loop(2, lambda side: up_part(l, u, side, l * PER + 2 + u))
+
+    def down_one(l, yy):
+        p = l * PER + 4
+        ACC[...] = mm_nt(HID[l, 0, 0], matrix(p, 0)) + mm_nt(HID[l, 0, 1], matrix(p, 1))
+
+    def down_two(l, yy):
+        p = l * PER + 5
+        total = ACC[...] + mm_nt(HID[l, 1, 0], matrix(p, 0))
+        give(1, total + mm_nt(HID[l, 1, 1], matrix(p, 1)))
+
+    def layer_end(l, yy):
+        def take(rows, total):
+            value = R1[l, rows, :] + total
+
+            @pl.when(l == 0)
+            def _():
+                S[1, rows, :] = value
 
             @pl.when(l == 1)
             def _():
-                block_copy.start()
+                ACC[rows, :] = value
+
+        receive(1, take)
+
+        @pl.when(l == 1)
+        def _():
+            block_copy.start()
 
     block_copy = pltpu.make_async_copy(ACC.at[pl.ds(pl.multiple_of(half, TM), TM)], out_block, lc_s.at[2])
 
-    def scatter_copies(p, h, even, phase):
-        order = gather_order(even, h)[::-1]
-        axis = order[phase]
-        have = {q: (own[q] if q in order[:phase] else ALL) for q in own}
-        sends, recvs = [], []
-        for slot, dev, to, _ in partners[axis]:
-            src = block(p, h, {**have, axis: to})
-            if phase == 0:
-                dst = (RB0Y if axis == "y" else RB0X).at[p if h < 2 else PAIRS + p // 2]
-            elif phase == 1:
-                dst = RB1Z.at[p, slot] if axis == "z" else RB1.at[p, h]
+    def scatter_plain(p, h, order, axis):
+        slot, dev, there = along(axis)
+        place = order.index(axis)
+        have = {q: (own[q] if q in order[:place] else ALL) for q in own}
+        if place == 0:
+            dst = (RB0Y if axis == "y" else RB0X).at[p if h > 0 else PAIRS + p // 2]
+        else:
+            dst = RB1.at[p] if h == 0 else RB2X.at[p, h - 1]
+        send, recv = ag_s.at[p, h, slot], ag_r.at[late(p), h, slot]
+        src = block(p, h, {**have, axis: there})
+        return lazy(src, dst, send, recv, dev), lazy(dst, dst, send, recv, dev), dst
+
+    def late(p):
+        return (p + PER) % PAIRS
+
+    def scatter_have(order):
+        return {q: (own[q] if q in order[: order.index("z")] else ALL) for q in own}
+
+    def scatter_z(p, h, order, k):
+        dst = RB2.at[p, k - 1] if h == 0 else RBZ.at[p, h - 1, k - 1]
+        send, recv = ag_s.at[p, h, k - 1], ag_r.at[late(p), h, k - 1]
+        src = block(p, h, {**scatter_have(order), "z": z_to(k)})
+        return lazy(src, dst, send, recv, dev_z(k)), lazy(dst, dst, send, recv, dev_z(k)), dst
+
+    def scatter_merge(p, h, order):
+        dst = RBM.at[p] if h == 0 else RBMZ.at[p, h - 1]
+        dev = ((1 + z // far) * NX + x, narrow)
+        send, recv = ag_s.at[p, h, 5], ag_r.at[late(p), h, 5]
+        src = block(p, h, {**scatter_have(order), "z": far - z})
+        return lazy(src, dst, send, recv, dev), lazy(dst, dst, send, recv, dev), dst
+
+    def scatter_steps(order):
+        at = order.index("z")
+        return order[:at] + ("merge",) + order[at:]
+
+    def scatter_issue(p, step):
+        def action(h, forward_order):
+            order = forward_order[::-1]
+            steps = scatter_steps(order)
+            before = steps[step - 1] if step > 0 else None
+            if before is not None and before != "merge":
+                have = {q: (own[q] if q in order[: order.index(before) + 1] else ALL) for q in own}
+                view = block(p, h, have)
+                if before == "z":
+                    scatter_z(p, h, order, 2)[1]().wait_recv()
+
+                    @pl.when(z != 0)
+                    def _():
+                        scatter_z(p, h, order, 1)[1]().wait_recv()
+
+                    @pl.when(z != far)
+                    def _():
+                        scatter_z(p, h, order, 3)[1]().wait_recv()
+
+                    total = view[...].astype(F32) + scatter_z(p, h, order, 2)[2][...].astype(F32)
+                    for k, there in ((1, z != 0), (3, z != far)):
+                        total = total + jnp.where(there, scatter_z(p, h, order, k)[2][...].astype(F32), 0.0)
+                else:
+                    scatter_plain(p, h, order, before)[1]().wait_recv()
+                    total = view[...].astype(F32) + scatter_plain(p, h, order, before)[2][...].astype(F32)
+                if step < len(steps):
+                    view[...] = total.astype(BF16)
+                else:
+                    out_grad[p, h] = total
+                    NB[...] += fold(total * total)
+            if step == len(steps):
+                return
+            if steps[step] == "merge":
+
+                @pl.when(outer)
+                def _():
+                    scatter_merge(p, h, order)[0]().start()
+
+            elif steps[step] == "z":
+
+                @pl.when(inner)
+                def _():
+                    scatter_merge(p, h, order)[1]().wait_recv()
+                    view = block(p, h, {**scatter_have(order), "z": z_to(2)})
+                    term = scatter_merge(p, h, order)[2][...].astype(F32)
+                    view[...] = (view[...].astype(F32) + term).astype(BF16)
+
+                along_z(lambda k: scatter_z(p, h, order, k)[0]().start())
             else:
-                dst = RB2.at[p, h, slot] if axis == "z" else RB2X.at[p]
-            sends.append(lazy(src, dst, rs_s.at[p, h, slot], rs_r.at[p, h, slot], dev))
-            recvs.append((dst, lazy(dst, dst, rs_s.at[p, h, slot], rs_r.at[p, h, slot], dev)))
-        return sends, recvs, {**have, axis: own[axis]}
-
-    def scatter_issue(p, phase):
-        def action(even):
-            for h in range(PARTS):
-                if phase > 0:
-                    _, recvs, where = scatter_copies(p, h, even, phase - 1)
-                    for _, r in recvs:
-                        r().wait_recv()
-                    view = block(p, h, where)
-                    total = view[...].astype(F32)
-                    for dst, _ in recvs:
-                        total = total + dst[...].astype(F32)
-                    if phase < 3:
-                        view[...] = total.astype(BF16)
-                    else:
-                        out_grad[p, h] = total
-                        NB[...] += fold(total * total)
-                if phase < 3:
-                    for s in scatter_copies(p, h, even, phase)[0]:
-                        s().start()
-
-        by_kind(p, action)
+                scatter_plain(p, h, order, steps[step])[0]().start()
+
+        each_part(p, action)
 
     def fold(sq):
         sq = jnp.sum(sq.reshape(PART // 8, 8, WIDE), axis=0)
         return sq[:, 0:128] + sq[:, 128:256] + sq[:, 256:384]
 
     def scatter_sent(p):
-        def action(even):
-            for h in range(PARTS):
-                for phase in range(3):
-                    for s in scatter_copies(p, h, even, phase)[0]:
-                        s().wait_send()
-
-        by_kind(p, action)
+        def action(h, forward_order):
+            order = forward_order[::-1]
+            for axis in ("x", "y"):
+                scatter_plain(p, h, order, axis)[0]().wait_send()
+
+            @pl.when(outer)
+            def _():
+                scatter_merge(p, h, order)[0]().wait_send()
+
+            along_z(lambda k: scatter_z(p, h, order, k)[0]().wait_send())
+
+        each_part(p, action)
 
     NB[...] = jnp.zeros((8, 128), F32)
     SG[...] = jnp.zeros_like(SG)
@@ -504,128 +663,93 @@
     def both(action):
         loop(2, action)
 
-    def backward_slot(s, step, l):
-        slot = BACK_ORDER[s]
-        p = l * PER + slot
-        if step == 0:
+    def back_prepare(l, yy):
+        @pl.when(l == 1)
+        def _():
+            cot_own.wait()
+            cot_in.wait_recv()
+            cot_out.wait_send()
+
+        cast_rows(BK, GR)
+        transpose_into(TA, BK)
+        transpose_into(TB, NRM2.at[l])
+
+    def back_down(l, u, side):
+        p = l * PER + 4 + u
+
+        @pl.when(side == 0)
+        def _():
             gather_sent(p)
-        if slot in (4, 5):
-            u = slot - 4
-            if slot == 4 and step == 0:
-
-                @pl.when(l == 1)
-                def _():
-                    cot_own.wait()
-                    cot_in.wait_recv()
-                    cot_out.wait_send()
-
-                cast_rows(BK, GR)
-                transpose_into(TA, BK)
-                transpose_into(TB, NRM2.at[l])
-            gh = mm(BK[...], matrix(p, step))
-            GU[u, step] = (gh * GP[l, u, step].astype(F32)).astype(BF16)
-            put_grad(p, step, TA, HID[l, u, step])
-        elif slot == 2:
-            if step == 0:
-
-                @pl.when(l == 1)
-                def _():
-                    block_copy.wait()
-
-                ACC[...] = mm_nt(GU[0, 0], matrix(p, 0)) + mm_nt(GU[0, 1], matrix(p, 1))
-            else:
-                both(lambda yy: put_grad(p, yy, TB, GU[0, yy]))
-        elif slot == 3:
-            if step == 0:
-                total = ACC[...] + mm_nt(GU[1, 0], matrix(p, 0))
-                give(0, total + mm_nt(GU[1, 1], matrix(p, 1)))
-            else:
-                both(lambda yy: put_grad(p, yy, TB, GU[1, yy]))
-                norm_back(0, R1.at[l], 2 * l + 1)
-        elif slot == 1:
-            if step == 0:
-                cast_rows(BK, GR)
-                transpose_into(TA, BK)
-                transpose_into(TB, NRM.at[l])
-
-                def grad_mix(yy):
-                    GM[yy] = mm(BK[...], matrix(p, yy)[:, COL:]).astype(BF16)
-
-                both(grad_mix)
-                attend_back(l, 0)
-            else:
-                attend_back(l, 1)
-                ACC[...] = mm_nt(DV[0], matrix(p, 0)[:, :COL]) + mm_nt(DV[1], matrix(p, 1)[:, :COL])
-
-                def grads(yy):
-                    gv = mm(TB[...], DV[yy])
-                    go = mm(TA[...], MIX[l, yy])
-                    pair = jnp.concatenate([gv, go], axis=1).astype(BF16)
-                    G[p, yy] = pair.reshape(NZ, NX, PARTS, PART, WIDE)
-
-                both(grads)
-        else:
-            if step == 0:
-                total = ACC[...] + mm_nt(DQK[0], matrix(p, 0))
-                give(1, total + mm_nt(DQK[1], matrix(p, 1)))
-            else:
-                both(lambda yy: put_grad(p, yy, TB, DQK[yy]))
-                norm_back(1, S.at[l], 2 * l)
+
+        gh = mm(BK[...], matrix(p, side))
+        GU[u, side] = (gh * GP[l, u, side].astype(F32)).astype(BF16)
+        put_grad(p, side, TA, HID[l, u, side])
+
+    def back_up_sum(l, yy):
+        p = l * PER + 2
+
+        @pl.when(l == 1)
+        def _():
+            block_copy.wait()
+
+        ACC[...] = mm_nt(GU[0, 0], matrix(p, 0)) + mm_nt(GU[0, 1], matrix(p, 1))
+
+    def back_up_give(l, yy):
+        p = l * PER + 3
+        total = ACC[...] + mm_nt(GU[1, 0], matrix(p, 0))
+        give(0, total + mm_nt(GU[1, 1], matrix(p, 1)))
+
+    def back_up(l, u):
+        p = l * PER + 2 + u
+        gather_sent(p)
+        both(lambda side: put_grad(p, side, TB, GU[u, side]))
+
+    def back_norm_two(l, yy):
+        norm_back(0, R1.at[l], 2 * l + 1)
+
+    def back_attn_prepare(l, yy):
+        cast_rows(BK, GR)
+        transpose_into(TA, BK)
+        transpose_into(TB, NRM.at[l])
+
+        def grad_mix(side):
+            GM[side] = mm(BK[...], matrix(l * PER + 1, side)[:, COL:]).astype(BF16)
+
+        both(grad_mix)
+
+    def back_attn_grads(l, yy):
+        p = l * PER + 1
+        gather_sent(p)
+        ACC[...] = mm_nt(DV[0], matrix(p, 0)[:, :COL]) + mm_nt(DV[1], matrix(p, 1)[:, :COL])
+
+        def grads(side):
+            gv = mm(TB[...], DV[side])
+            go = mm(TA[...], MIX[l, side])
+            pair = jnp.concatenate([gv, go], axis=1).astype(BF16)
+            G[p, side] = pair.reshape(NZ, NX, PARTS, PART, WIDE)
+
+        both(grads)
+
+    def back_qk_give(l, yy):
+        p = l * PER
+        total = ACC[...] + mm_nt(DQK[0], matrix(p, 0))
+        give(1, total + mm_nt(DQK[1], matrix(p, 1)))
+
+    def back_qk(l, yy):
+        p = l * PER
+        gather_sent(p)
+        both(lambda side: put_grad(p, side, TB, DQK[side]))
+
+    def back_norm_one(l, yy):
+        norm_back(1, S.at[l], 2 * l)
 
     def position(i):
         s = i % PER
         slot = jnp.where(s < 2, s + 4, jnp.where(s < 4, s, 5 - s))
         return (LAYERS - 1 - i // PER) * PER + slot
 
-    def within(t, action, phase, first=0):
-        @pl.when(jnp.logical_and(t >= first, t < PAIRS))
-        def _():
-            action(t, phase)
-
-    def by_slot(t, action):
-        for slot in range(PER):
-
-            @pl.when(t % PER == slot)
-            def _():
-                action(slot)
-
     def scatter_at(t, phase):
         scatter_issue(position(t), phase)
-
-    def forward_tick(t, q):
-        for step in range(2):
-
-            @pl.when(q == step)
-            def _():
-                if step == 0:
-                    within(t + LEAD_ONE, gather_issue, 0, LEAD_ONE)
-                    within(t + LEAD_TWO, gather_issue, 1)
-                    within(t + LEAD_THREE, gather_issue, 2)
-                    within(t, gather_issue, 3)
-
-                @pl.when(t >= 0)
-                def _():
-                    by_slot(t, lambda slot: forward_slot(slot, step, t // PER))
-
-    def backward_tick(t, q):
-        for step in range(2):
-
-            @pl.when(q == step)
-            def _():
-                @pl.when(t < PAIRS)
-                def _():
-                    by_slot(t, lambda s: backward_slot(s, step, LAYERS - 1 - t // PER))
-
-                if step == 0:
-                    pl.when(t == PAIRS)(rows_done)
-                    pl.when(t == PAIRS + LAG_TWO)(small_sums)
-
-                if step == 0:
-                    within(t - LAG_TWO, scatter_at, 1)
-                    within(t - LAG_LAST, scatter_at, 3)
-                else:
-                    within(t, scatter_at, 0)
-                    within(t - LAG_THREE, scatter_at, 2)
 
     igrad_copy = pltpu.make_async_copy(GRh, out_igrad, lc_s.at[3])
     place = 2 * y + x
@@ -666,22 +790,76 @@
         for k in range(3):
             small_xy(k)[0].start()
 
-    lead_in = LEAD_TWO
-    merge = PAIRS - 1
-
-    def tick(m):
-        i, q = m // 2 - lead_in, m % 2
-        is_back = jnp.logical_or(i == merge, i > merge + 1)
-
-        @pl.when(jnp.logical_not(is_back))
+    pieces = {
+        "g1": gains_across,
+        "g2": first_rows,
+        "ln1": ln_one,
+        "qk": project_qk,
+        "v": project_v,
+        "at": attend,
+        "out": attn_out,
+        "res": attn_resid,
+        "up": up,
+        "dn0": down_one,
+        "dn1": down_two,
+        "fin": layer_end,
+        "b4p": back_prepare,
+        "b4": lambda l, side: back_down(l, 0, side),
+        "b5": lambda l, side: back_down(l, 1, side),
+        "b2a": back_up_sum,
+        "b2b": lambda l, yy: back_up(l, 0),
+        "b3a": back_up_give,
+        "b3b": lambda l, yy: back_up(l, 1),
+        "b3c": back_norm_two,
+        "b1p": back_attn_prepare,
+        "ab0": lambda l, side: attend_back(l, side, 0),
+        "ab1": lambda l, side: attend_back(l, side, 1),
+        "ab2": lambda l, side: attend_back(l, side, 2),
+        "b1f": back_attn_grads,
+        "b0a": back_qk_give,
+        "b0b": back_qk,
+        "b0c": back_norm_one,
+        "rows": lambda l, yy: rows_done(),
+        "small": lambda l, yy: small_sums(),
+    }
+    def digit(word, k, base):
+        return lax.rem(lax.div(word, base**k), base)
+
+    def plan_of(m, low, high):
+        if high - low == 1:
+            return tuple(jnp.int32(words[low]) for words in PLAN_WORDS)
+        middle = (low + high) // 2
+        return lax.cond(m < middle, lambda: plan_of(m, low, middle), lambda: plan_of(m, middle, high))
+
+    def micro(m):
+        plan = plan_of(m, 0, STEPS)
+        for counts, firsts, action in ((plan[0], plan[1], gather_issue), (plan[2], plan[3], scatter_at)):
+
+            @pl.when(counts > 0)
+            def _():
+                for kind in range(5):
+                    count, first = digit(counts, kind, 16), digit(firsts, kind, 16)
+
+                    @pl.when(count > 0)
+                    def _():
+                        def one(i, carry):
+                            action(first + i, kind)
+                            return carry
+
+                        lax.fori_loop(0, count, one, 0)
+
+        word = plan[4]
+
+        @pl.when(word > 0)
         def _():
-            forward_tick(jnp.where(i < merge, i, merge), q)
-
-        @pl.when(is_back)
-        def _():
-            backward_tick(jnp.where(i == merge, 0, i - PAIRS), q)
-
-    loop(2 * (2 * PAIRS + lead_in + LAG_LAST), tick)
+            what, l, yy = lax.rem(word, 32), digit(lax.div(word, 32), 0, 2), lax.div(word, 64)
+            for i, action in enumerate(pieces.values()):
+
+                @pl.when(what == i + 1)
+                def _():
+                    action(l, yy)
+
+    loop(STEPS, micro)
 
     own_square = jnp.sum(jnp.sum(NB[...], axis=1, keepdims=True), axis=0, keepdims=True)
     NZC[z, c] = jnp.broadcast_to(own_square, (8, 128))
@@ -740,7 +918,7 @@
     V = pltpu.VMEM
     scratch = [
         V((PAIRS, 2, NZ, NX, PARTS, PART, WIDE), BF16),
-        V((LEAD_ONE, 2, ROWS, COL), F32),
+        V((WSLOTS, 2, ROWS, COL), F32),
         V((2, SEQ, D), F32),
         V((2, SEQ, D), F32),
         V((2, SEQ, D), BF16),
@@ -771,13 +949,14 @@
         V((4, 8, 128), F32),
         V((PAIRS + PAIRS // 2, NZ, NX, PART, WIDE), BF16),
         V((PAIRS + PAIRS // 2, 2, NZ, PART, WIDE), BF16),
-        V((PAIRS, 2, NZ, PART, WIDE), BF16),
-        V((PAIRS, NZ - 1, 2, PART, WIDE), BF16),
-        V((PAIRS, 2, NZ - 1, PART, WIDE), BF16),
+        V((PAIRS, NZ, PART, WIDE), BF16),
+        V((PAIRS, NZ - 1, PART, WIDE), BF16),
+        V((PAIRS, 2, PART, WIDE), BF16),
+        V((PAIRS, 2, NZ - 1, 2, PART, WIDE), BF16),
         V((PAIRS, PART, WIDE), BF16),
-        dma((LEAD_ONE,)),
-        dma((PAIRS, PARTS, 5)), dma((PAIRS, PARTS, 5)),
-        dma((PAIRS, PARTS, 5)), dma((PAIRS, PARTS, 5)),
+        V((PAIRS, 2, 2, PART, WIDE), BF16),
+        dma((WSLOTS,)),
+        dma((PAIRS, PARTS, 6)), dma((PAIRS, PARTS, 6)),
         dma((2,)), dma((2, 2)),
         dma((2,)), dma((2,)), dma((4,)),
         dma((4,)), dma((4,)),

time: 288 us -> 276 us (0.958)
  Pallas kernels: 287 us -> 275 us
    pallas_call x1, Pallas kernels: 279 us -> 267 us  [big_step(): pl.pallas_call(step_kernel, out_shape=(jax.ShapeDtypeStruct((TM, D), F32)...]
where the time goes in v3:
time: 276 us; the launch traced here: 275 us
  Pallas kernels  275 us (100%)
    pallas_call x1, Pallas kernels, big_step(): pl.pallas_call(step_kernel, out_shape=(jax.ShapeDtypeStruct((TM, D), F32)...  267 us
    pallas_call x1, Pallas kernels, adam_all(): pl.pallas_call(adam_kernel, grid=(ADAM_STEPS,), out_shape=(*(jax.ShapeDty...  7.86 us

profile of v3, /device:TPU:0, one launch (start us, length us, event | category | flops | bytes accessed | tf_op | source)
XLA Modules:
  0.0 275.4 jit_solution(16394184492959773309)
XLA Ops:
  0.6 266.7 %train_step.1 = (f32[256,768]{1,0:T(8,128)}, f32[256,768]{1,0:T(8,128)}, f32[12,3,32,384]{3,2,1,0:T(8,128)}, f32[8,768]{1,0:T(8,128)}, f32[8,128]{1,0:T(8,128)}) custom-call(f32[24,96,192]{2,1,0:T(8,128)} %bitcast.7, bf16[256,768]{1,0:T(8,128)(2,1)} %patch.1, f32[256,768]{1,0:T(8,128)} %cot.1, s32[2,450]{1,0:T(2,128)} %mask_index.1, s32[2]{0:T(128)} %mask_count.1, ...), custom_call_target="tpu_custom_call" | custom-call | tf_op jit(solution)/shard_map/train_step/pallas_call | solution.py:966
  267.4 7.9 %adam.1 = (f32[24,96,192]{2,1,0:T(8,128)}, f32[24,96,192]{2,1,0:T(8,128)}, f32[24,96,192]{2,1,0:T(8,128)}, f32[5,96]{1,0:T(8,128)}, f32[5,96]{1,0:T(8,128)}, /*i...) custom-call(f32[8,128]{1,0:T(8,128)} %get-tuple-element.23.norm, ...), custom_call_target="tpu_custom_call" | custom-call | tf_op jit(solution)/shard_map/adam/pallas_call | solution.py:1036

commit v4 on v3

--- a/solution.py
+++ b/solution.py
@@ -44,10 +44,10 @@
 BEGUN = 3
 PLAN_WORDS = (
     (
-        0, 0, 0, 0, 32, 516, 0, 8240, 4608, 131073, 0, 4112,
-        0, 256, 272, 4099, 65792, 32, 4096, 65537, 256, 65552, 8192, 65792,
-        0, 0, 0, 65536, 256, 69664, 0, 4352, 256, 0, 0, 69632,
-        0, 65536, 4096, 0, 65536, 0, 0, 0, 65536, 0, 0, 0,
+        0, 4401, 17, 8704, 16, 65536, 0, 256, 131331, 4112, 16, 4097,
+        0, 0, 0, 65792, 272, 4098, 4112, 65792, 0, 65536, 0, 1,
+        4368, 16, 65536, 4352, 16, 65536, 4352, 0, 256, 4096, 0, 69632,
+        0, 65536, 0, 0, 65536, 0, 0, 0, 65536, 0, 0, 0,
         0, 0, 0, 0, 0, 0, 0, 0, 0, 0, 0, 0,
         0, 0, 0, 0, 0, 0, 0, 0, 0, 0, 0, 0,
         0, 0, 0, 0, 0, 0, 0, 0, 0, 0, 0, 0,
@@ -55,10 +55,10 @@
         0, 0, 0, 0,
     ),
     (
-        0, 0, 0, 0, 0, 3, 0, 32, 8704, 7, 0, 12368,
-        0, 1024, 1376, 16392, 132608, 112, 20480, 196619, 1792, 262288, 24576, 329728,
-        0, 0, 0, 393216, 2304, 491680, 0, 39424, 2816, 0, 0, 565248,
-        0, 589824, 45056, 0, 655360, 0, 0, 0, 720896, 0, 0, 0,
+        0, 3, 52, 4352, 64, 0, 0, 768, 66565, 12368, 96, 16392,
+        0, 0, 0, 197888, 1648, 20489, 24704, 263936, 0, 327680, 0, 11,
+        30864, 160, 393216, 35072, 176, 458752, 39424, 0, 2816, 40960, 0, 569344,
+        0, 589824, 0, 0, 655360, 0, 0, 0, 720896, 0, 0, 0,
         0, 0, 0, 0, 0, 0, 0, 0, 0, 0, 0, 0,
         0, 0, 0, 0, 0, 0, 0, 0, 0, 0, 0, 0,
         0, 0, 0, 0, 0, 0, 0, 0, 0, 0, 0, 0,
@@ -69,23 +69,23 @@
         0, 0, 0, 0, 0, 0, 0, 0, 0, 0, 0, 0,
         0, 0, 0, 0, 0, 0, 0, 0, 0, 0, 0, 0,
         0, 0, 0, 0, 0, 0, 0, 0, 0, 0, 0, 0,
-        0, 0, 0, 0, 0, 0, 0, 1, 0, 0, 0, 1,
-        0, 0, 1, 16, 1, 0, 0, 0, 256, 0, 0, 16,
-        0, 33, 0, 257, 4096, 16, 256, 257, 0, 0, 4352, 1,
-        16, 0, 4096, 4128, 4353, 256, 1, 256, 0, 0, 1, 69648,
-        0, 0, 0, 0, 0, 0, 16, 0, 200705, 0, 256, 65536,
-        0, 4352, 16, 475664,
+        0, 0, 0, 0, 0, 0, 0, 1, 0, 0, 0, 0,
+        1, 0, 16, 1, 0, 0, 272, 1, 0, 256, 0, 4096,
+        32, 257, 256, 1, 0, 16, 4096, 4097, 272, 1, 0, 256,
+        0, 16, 8193, 256, 4112, 1, 4112, 256, 0, 0, 272, 257,
+        0, 0, 4096, 16, 0, 4097, 0, 65792, 65536, 16, 65536, 4096,
+        65536, 256, 131072, 401408,
     ),
     (
         0, 0, 0, 0, 0, 0, 0, 0, 0, 0, 0, 0,
         0, 0, 0, 0, 0, 0, 0, 0, 0, 0, 0, 0,
         0, 0, 0, 0, 0, 0, 0, 0, 0, 0, 0, 0,
-        0, 0, 0, 0, 0, 0, 0, 0, 0, 0, 0, 1,
-        0, 0, 2, 0, 3, 0, 0, 0, 0, 0, 0, 16,
-        0, 36, 0, 261, 0, 64, 512, 774, 0, 0, 5120, 7,
-        80, 0, 8192, 12384, 17672, 1536, 9, 1792, 0, 0, 10, 20608,
-        0, 0, 0, 0, 0, 0, 144, 0, 90123, 0, 2048, 262144,
-        0, 30976, 160, 363184,
+        0, 0, 0, 0, 0, 0, 0, 0, 0, 0, 0, 0,
+        1, 0, 0, 2, 0, 0, 16, 3, 0, 256, 0, 0,
+        32, 516, 768, 5, 0, 64, 4096, 8198, 1104, 7, 0, 1280,
+        0, 96, 12296, 1536, 20592, 9, 24704, 1792, 0, 0, 2192, 2314,
+        0, 0, 28672, 160, 0, 32779, 0, 2560, 65536, 176, 131072, 36864,
+        196608, 2816, 262144, 434176,
     ),
     (
         0, 0, 1, 0, 0, 2, 0, 3, 0, 4, 0, 5,
@@ -165,7 +165,6 @@
     barrier = pltpu.get_barrier_semaphore()
     for dev in greeted:
         pl.semaphore_signal(barrier, inc=1, device_id=dev, device_id_type=MESH)
-    pl.semaphore_wait(barrier, len(greeted))
 
     def remote(src, dst, send, recv, dev):
         return pltpu.make_async_remote_copy(
@@ -306,7 +305,6 @@
     cot_own = pltpu.make_async_copy(cot, GRh, lc_s.at[1])
     patch_own.start()
     cot_own.start()
-    patch_out.start()
     GPIECE[z, x] = jnp.zeros((8, 128), F32)
     GPIECE[z, x, 0:5, 0:ROWS] = small[...].astype(BF16).astype(F32)
     gain_z = [
@@ -320,13 +318,12 @@
         remote(GPIECE.at[:, x], GPIECE.at[:, x], gn_s.at[3], gn_r.at[3], dev_x),
         remote(GPIECE.at[:, 1 - x], GPIECE.at[:, 1 - x], gn_s.at[3], gn_r.at[3], dev_x),
     )
+    loop(BEGUN, pack)
+    pl.semaphore_wait(barrier, len(greeted))
     for s, _ in gain_z:
         s.start()
-    def begin(p):
-        pack(p)
-        gather_issue(p, 0)
-
-    loop(BEGUN, begin)
+    patch_out.start()
+    loop(BEGUN, lambda p: gather_issue(p, 0))
     cot_out.start()
     loop(PAIRS - BEGUN, lambda i: pack(i + BEGUN))
 

time: 276 us -> 270 us (0.978)
  Pallas kernels: 275 us -> 269 us
    pallas_call x1, Pallas kernels: 267 us -> 261 us  [big_step(): pl.pallas_call(step_kernel, out_shape=(jax.ShapeDtypeStruct((TM, D), F32)...]
where the time goes in v4:
time: 270 us; the launch traced here: 269 us
  Pallas kernels  269 us (100%)
    pallas_call x1, Pallas kernels, big_step(): pl.pallas_call(step_kernel, out_shape=(jax.ShapeDtypeStruct((TM, D), F32)...  261 us
    pallas_call x1, Pallas kernels, adam_all(): pl.pallas_call(adam_kernel, grid=(ADAM_STEPS,), out_shape=(*(jax.ShapeDty...  7.86 us

profile of v4, /device:TPU:0, one launch (start us, length us, event | category | flops | bytes accessed | tf_op | source)
XLA Modules:
  0.0 269.4 jit_solution(9675126611239652618)
XLA Ops:
  0.6 260.7 %train_step.1 = (f32[256,768]{1,0:T(8,128)}, f32[256,768]{1,0:T(8,128)}, f32[12,3,32,384]{3,2,1,0:T(8,128)}, f32[8,768]{1,0:T(8,128)}, f32[8,128]{1,0:T(8,128)}) custom-call(f32[24,96,192]{2,1,0:T(8,128)} %bitcast.7, bf16[256,768]{1,0:T(8,128)(2,1)} %patch.1, f32[256,768]{1,0:T(8,128)} %cot.1, s32[2,450]{1,0:T(2,128)} %mask_index.1, s32[2]{0:T(128)} %mask_count.1, ...), custom_call_target="tpu_custom_call" | custom-call | tf_op jit(solution)/shard_map/train_step/pallas_call | solution.py:963
  261.4 7.9 %adam.1 = (f32[24,96,192]{2,1,0:T(8,128)}, f32[24,96,192]{2,1,0:T(8,128)}, f32[24,96,192]{2,1,0:T(8,128)}, f32[5,96]{1,0:T(8,128)}, f32[5,96]{1,0:T(8,128)}, /*i...) custom-call(f32[8,128]{1,0:T(8,128)} %get-tuple-element.23.norm, ...), custom_call_target="tpu_custom_call" | custom-call | tf_op jit(solution)/shard_map/adam/pallas_call | solution.py:1033

commit v5 on v4

--- a/solution.py
+++ b/solution.py
@@ -31,6 +31,7 @@
 NZ, NX = 4, 2
 ROWS = 96
 PARTS = 3
+EARLY = 2
 PART = ROWS // PARTS
 COL = 192
 WIDE = 2 * COL
@@ -44,10 +45,10 @@
 BEGUN = 3
 PLAN_WORDS = (
     (
-        0, 4401, 17, 8704, 16, 65536, 0, 256, 131331, 4112, 16, 4097,
-        0, 0, 0, 65792, 272, 4098, 4112, 65792, 0, 65536, 0, 1,
-        4368, 16, 65536, 4352, 16, 65536, 4352, 0, 256, 4096, 0, 69632,
-        0, 65536, 0, 0, 65536, 0, 0, 0, 65536, 0, 0, 0,
+        0, 0, 17, 257, 0, 272, 32, 4098, 256, 69648, 4352, 65568,
+        0, 4096, 0, 256, 65793, 0, 0, 69633, 256, 69665, 257, 69632,
+        257, 4112, 16, 65552, 256, 69632, 0, 4352, 0, 256, 0, 69632,
+        0, 69632, 0, 0, 65536, 0, 0, 65536, 0, 0, 0, 0,
         0, 0, 0, 0, 0, 0, 0, 0, 0, 0, 0, 0,
         0, 0, 0, 0, 0, 0, 0, 0, 0, 0, 0, 0,
         0, 0, 0, 0, 0, 0, 0, 0, 0, 0, 0, 0,
@@ -55,10 +56,10 @@
         0, 0, 0, 0,
     ),
     (
-        0, 3, 52, 4352, 64, 0, 0, 768, 66565, 12368, 96, 16392,
-        0, 0, 0, 197888, 1648, 20489, 24704, 263936, 0, 327680, 0, 11,
-        30864, 160, 393216, 35072, 176, 458752, 39424, 0, 2816, 40960, 0, 569344,
-        0, 589824, 0, 0, 655360, 0, 0, 0, 720896, 0, 0, 0,
+        0, 0, 3, 4, 0, 272, 32, 5, 512, 4160, 8960, 65616,
+        0, 12288, 0, 1024, 132359, 0, 0, 213000, 1536, 282745, 1802, 352256,
+        2059, 28816, 160, 393392, 2304, 491520, 0, 39424, 0, 2816, 0, 565248,
+        0, 634880, 0, 0, 655360, 0, 0, 720896, 0, 0, 0, 0,
         0, 0, 0, 0, 0, 0, 0, 0, 0, 0, 0, 0,
         0, 0, 0, 0, 0, 0, 0, 0, 0, 0, 0, 0,
         0, 0, 0, 0, 0, 0, 0, 0, 0, 0, 0, 0,
@@ -69,23 +70,23 @@
         0, 0, 0, 0, 0, 0, 0, 0, 0, 0, 0, 0,
         0, 0, 0, 0, 0, 0, 0, 0, 0, 0, 0, 0,
         0, 0, 0, 0, 0, 0, 0, 0, 0, 0, 0, 0,
-        0, 0, 0, 0, 0, 0, 0, 1, 0, 0, 0, 0,
-        1, 0, 16, 1, 0, 0, 272, 1, 0, 256, 0, 4096,
-        32, 257, 256, 1, 0, 16, 4096, 4097, 272, 1, 0, 256,
-        0, 16, 8193, 256, 4112, 1, 4112, 256, 0, 0, 272, 257,
-        0, 0, 4096, 16, 0, 4097, 0, 65792, 65536, 16, 65536, 4096,
-        65536, 256, 131072, 401408,
+        0, 0, 0, 0, 0, 0, 0, 1, 0, 0, 0, 1,
+        0, 0, 0, 16, 2, 0, 16, 256, 16, 0, 0, 4096,
+        272, 1, 512, 1, 0, 0, 16, 1, 272, 1, 0, 256,
+        0, 12304, 17, 4097, 4096, 256, 0, 16, 256, 16, 257, 0,
+        69889, 0, 0, 0, 0, 0, 16, 16, 0, 12288, 69888, 0,
+        0, 0, 0, 659712,
     ),
     (
         0, 0, 0, 0, 0, 0, 0, 0, 0, 0, 0, 0,
         0, 0, 0, 0, 0, 0, 0, 0, 0, 0, 0, 0,
         0, 0, 0, 0, 0, 0, 0, 0, 0, 0, 0, 0,
-        0, 0, 0, 0, 0, 0, 0, 0, 0, 0, 0, 0,
-        1, 0, 0, 2, 0, 0, 16, 3, 0, 256, 0, 0,
-        32, 516, 768, 5, 0, 64, 4096, 8198, 1104, 7, 0, 1280,
-        0, 96, 12296, 1536, 20592, 9, 24704, 1792, 0, 0, 2192, 2314,
-        0, 0, 28672, 160, 0, 32779, 0, 2560, 65536, 176, 131072, 36864,
-        196608, 2816, 262144, 434176,
+        0, 0, 0, 0, 0, 0, 0, 0, 0, 0, 0, 1,
+        0, 0, 0, 0, 2, 0, 16, 0, 32, 0, 0, 0,
+        304, 4, 512, 5, 0, 0, 64, 6, 1104, 7, 0, 1280,
+        0, 4192, 120, 16393, 20480, 1536, 0, 128, 1792, 144, 2058, 0,
+        26891, 0, 0, 0, 0, 0, 160, 176, 0, 28672, 109056, 0,
+        0, 0, 0, 178944,
     ),
     (
         0, 0, 1, 0, 0, 2, 0, 3, 0, 4, 0, 5,
@@ -183,11 +184,6 @@
     def block(p, h, where):
         return G.at[p, where["y"], where["z"], where["x"], h]
 
-    def gather_order(even, h):
-        if h == 0:
-            return ("z", "x", "y") if even else ("z", "y", "x")
-        return ("x", "z", "y") if h == 1 else ("y", "z", "x")
-
     def holding(axes):
         return {q: (ALL if q in axes else own[q]) for q in own}
 
@@ -206,16 +202,18 @@
             action(3)
 
     def each_part(p, action):
-        @pl.when(p % 2 == 0)
-        def _():
-            action(0, gather_order(True, 0))
-
-        @pl.when(p % 2 == 1)
-        def _():
-            action(0, gather_order(False, 0))
-
-        for h in range(1, PARTS):
-            action(h, gather_order(True, h))
+        for test, h, order in (
+            (p % 2 == 0, 0, ("z", "x", "y")),
+            (p % 2 == 1, 0, ("z", "y", "x")),
+            (p < EARLY, 1, ("z", "y", "x")),
+            (p >= EARLY, 1, ("x", "z", "y")),
+            (p < EARLY, 2, ("z", "x", "y")),
+            (p >= EARLY, 2, ("y", "z", "x")),
+        ):
+
+            @pl.when(test)
+            def _():
+                action(h, order)
 
     def gather_plain(p, h, order, axis):
         slot, dev, there = along(axis)
@@ -522,11 +520,17 @@
         if place == 0:
             dst = (RB0Y if axis == "y" else RB0X).at[p if h > 0 else PAIRS + p // 2]
         else:
-            dst = RB1.at[p] if h == 0 else RB2X.at[p, h - 1]
+            dst = RB1.at[first_slot(p, h)] if z_last(order) else RB2X.at[p - EARLY, h - 1]
         send, recv = ag_s.at[p, h, slot], ag_r.at[late(p), h, slot]
         src = block(p, h, {**have, axis: there})
         return lazy(src, dst, send, recv, dev), lazy(dst, dst, send, recv, dev), dst
 
+    def z_last(order):
+        return order[2] == "z"
+
+    def first_slot(p, h):
+        return p if h == 0 else PAIRS + EARLY * (h - 1) + p
+
     def late(p):
         return (p + PER) % PAIRS
 
@@ -534,13 +538,13 @@
         return {q: (own[q] if q in order[: order.index("z")] else ALL) for q in own}
 
     def scatter_z(p, h, order, k):
-        dst = RB2.at[p, k - 1] if h == 0 else RBZ.at[p, h - 1, k - 1]
+        dst = RB2.at[first_slot(p, h), k - 1] if z_last(order) else RBZ.at[p - EARLY, h - 1, k - 1]
         send, recv = ag_s.at[p, h, k - 1], ag_r.at[late(p), h, k - 1]
         src = block(p, h, {**scatter_have(order), "z": z_to(k)})
         return lazy(src, dst, send, recv, dev_z(k)), lazy(dst, dst, send, recv, dev_z(k)), dst
 
     def scatter_merge(p, h, order):
-        dst = RBM.at[p] if h == 0 else RBMZ.at[p, h - 1]
+        dst = RBM.at[first_slot(p, h)] if z_last(order) else RBMZ.at[p - EARLY, h - 1]
         dev = ((1 + z // far) * NX + x, narrow)
         send, recv = ag_s.at[p, h, 5], ag_r.at[late(p), h, 5]
         src = block(p, h, {**scatter_have(order), "z": far - z})
@@ -946,12 +950,12 @@
         V((4, 8, 128), F32),
         V((PAIRS + PAIRS // 2, NZ, NX, PART, WIDE), BF16),
         V((PAIRS + PAIRS // 2, 2, NZ, PART, WIDE), BF16),
-        V((PAIRS, NZ, PART, WIDE), BF16),
-        V((PAIRS, NZ - 1, PART, WIDE), BF16),
-        V((PAIRS, 2, PART, WIDE), BF16),
-        V((PAIRS, 2, NZ - 1, 2, PART, WIDE), BF16),
-        V((PAIRS, PART, WIDE), BF16),
-        V((PAIRS, 2, 2, PART, WIDE), BF16),
+        V((PAIRS + 2 * EARLY, NZ, PART, WIDE), BF16),
+        V((PAIRS + 2 * EARLY, NZ - 1, PART, WIDE), BF16),
+        V((PAIRS - EARLY, 2, PART, WIDE), BF16),
+        V((PAIRS - EARLY, 2, NZ - 1, 2, PART, WIDE), BF16),
+        V((PAIRS + 2 * EARLY, PART, WIDE), BF16),
+        V((PAIRS - EARLY, 2, 2, PART, WIDE), BF16),
         dma((WSLOTS,)),
         dma((PAIRS, PARTS, 6)), dma((PAIRS, PARTS, 6)),
         dma((2,)), dma((2, 2)),

time: 270 us -> 259 us (0.959)
  Pallas kernels: 269 us -> 258 us
    pallas_call x1, Pallas kernels: 261 us -> 250 us  [big_step(): pl.pallas_call(step_kernel, out_shape=(jax.ShapeDtypeStruct((TM, D), F32)...]
where the time goes in v5:
time: 259 us
  Pallas kernels  258 us (100%)
    pallas_call x1, Pallas kernels, big_step(): pl.pallas_call(step_kernel, out_shape=(jax.ShapeDtypeStruct((TM, D), F32)...  250 us
    pallas_call x1, Pallas kernels, adam_all(): pl.pallas_call(adam_kernel, grid=(ADAM_STEPS,), out_shape=(*(jax.ShapeDty...  7.86 us

profile of v5, /device:TPU:0, one launch (start us, length us, event | category | flops | bytes accessed | tf_op | source)
XLA Modules:
  0.0 259.0 jit_solution(17128014661806714895)
XLA Ops:
  0.6 250.4 %train_step.1 = (f32[256,768]{1,0:T(8,128)}, f32[256,768]{1,0:T(8,128)}, f32[12,3,32,384]{3,2,1,0:T(8,128)}, f32[8,768]{1,0:T(8,128)}, f32[8,128]{1,0:T(8,128)}) custom-call(f32[24,96,192]{2,1,0:T(8,128)} %bitcast.7, bf16[256,768]{1,0:T(8,128)(2,1)} %patch.1, f32[256,768]{1,0:T(8,128)} %cot.1, s32[2,450]{1,0:T(2,128)} %mask_index.1, s32[2]{0:T(128)} %mask_count.1, ...), custom_call_target="tpu_custom_call" | custom-call | tf_op jit(solution)/shard_map/train_step/pallas_call | solution.py:967
  251.0 7.9 %adam.1 = (f32[24,96,192]{2,1,0:T(8,128)}, f32[24,96,192]{2,1,0:T(8,128)}, f32[24,96,192]{2,1,0:T(8,128)}, f32[5,96]{1,0:T(8,128)}, f32[5,96]{1,0:T(8,128)}, /*i...) custom-call(f32[8,128]{1,0:T(8,128)} %get-tuple-element.23.norm, ...), custom_call_target="tpu_custom_call" | custom-call | tf_op jit(solution)/shard_map/adam/pallas_call | solution.py:1037

commit v6 on v5

--- a/solution.py
+++ b/solution.py
@@ -41,63 +41,26 @@
 HEADS_Y = COL // HD
 
 WSLOTS = 4
-STEPS = 100
+STEPS = 82
 BEGUN = 3
 PLAN_WORDS = (
     (
-        0, 0, 17, 257, 0, 272, 32, 4098, 256, 69648, 4352, 65568,
-        0, 4096, 0, 256, 65793, 0, 0, 69633, 256, 69665, 257, 69632,
-        257, 4112, 16, 65552, 256, 69632, 0, 4352, 0, 256, 0, 69632,
-        0, 69632, 0, 0, 65536, 0, 0, 65536, 0, 0, 0, 0,
-        0, 0, 0, 0, 0, 0, 0, 0, 0, 0, 0, 0,
-        0, 0, 0, 0, 0, 0, 0, 0, 0, 0, 0, 0,
-        0, 0, 0, 0, 0, 0, 0, 0, 0, 0, 0, 0,
-        0, 0, 0, 0, 0, 0, 0, 0, 0, 0, 0, 0,
-        0, 0, 0, 0,
+        8, 66, 520, 72, 8, 579, 1096, 4104, 8, 64, 4097, 1,
+        576, 584, 8, 4097, 4672, 4105, 4096, 576, 0, 4096, 4688, 0,
+        576, 0, 576, 4096, 4096, 512, 4096, 0, 0, 36864, 0, 0,
+        32768, 0, 0, 0, 262144, 32768, 0, 2359296, 32768, 262144, 2097152, 0,
+        0, 17039360, 32768, 4194304, 32768, 16777216, 134217728, 262144, 16809984, 2359296, 32768, 0,
+        2097152, 0, 17039360, 32768, 2359296, 16809984, 16777216, 0, 16777216, 2359296, 262144, 2129920,
+        0, 2129920, 262144, 150994944, 33554432, 134479872, 134217728, 18874368, 958398464, 134217728,
     ),
     (
-        0, 0, 3, 4, 0, 272, 32, 5, 512, 4160, 8960, 65616,
-        0, 12288, 0, 1024, 132359, 0, 0, 213000, 1536, 282745, 1802, 352256,
-        2059, 28816, 160, 393392, 2304, 491520, 0, 39424, 0, 2816, 0, 565248,
-        0, 634880, 0, 0, 655360, 0, 0, 720896, 0, 0, 0, 0,
-        0, 0, 0, 0, 0, 0, 0, 0, 0, 0, 0, 0,
-        0, 0, 0, 0, 0, 0, 0, 0, 0, 0, 0, 0,
-        0, 0, 0, 0, 0, 0, 0, 0, 0, 0, 0, 0,
-        0, 0, 0, 0, 0, 0, 0, 0, 0, 0, 0, 0,
-        0, 0, 0, 0,
-    ),
-    (
-        0, 0, 0, 0, 0, 0, 0, 0, 0, 0, 0, 0,
-        0, 0, 0, 0, 0, 0, 0, 0, 0, 0, 0, 0,
-        0, 0, 0, 0, 0, 0, 0, 0, 0, 0, 0, 0,
-        0, 0, 0, 0, 0, 0, 0, 1, 0, 0, 0, 1,
-        0, 0, 0, 16, 2, 0, 16, 256, 16, 0, 0, 4096,
-        272, 1, 512, 1, 0, 0, 16, 1, 272, 1, 0, 256,
-        0, 12304, 17, 4097, 4096, 256, 0, 16, 256, 16, 257, 0,
-        69889, 0, 0, 0, 0, 0, 16, 16, 0, 12288, 69888, 0,
-        0, 0, 0, 659712,
-    ),
-    (
-        0, 0, 0, 0, 0, 0, 0, 0, 0, 0, 0, 0,
-        0, 0, 0, 0, 0, 0, 0, 0, 0, 0, 0, 0,
-        0, 0, 0, 0, 0, 0, 0, 0, 0, 0, 0, 0,
-        0, 0, 0, 0, 0, 0, 0, 0, 0, 0, 0, 1,
-        0, 0, 0, 0, 2, 0, 16, 0, 32, 0, 0, 0,
-        304, 4, 512, 5, 0, 0, 64, 6, 1104, 7, 0, 1280,
-        0, 4192, 120, 16393, 20480, 1536, 0, 128, 1792, 144, 2058, 0,
-        26891, 0, 0, 0, 0, 0, 160, 176, 0, 28672, 109056, 0,
-        0, 0, 0, 178944,
-    ),
-    (
-        0, 0, 1, 0, 0, 2, 0, 3, 0, 4, 0, 5,
-        6, 70, 7, 8, 0, 9, 0, 73, 0, 10, 0, 11,
-        12, 35, 0, 36, 0, 37, 38, 102, 39, 40, 0, 41,
-        0, 105, 45, 0, 42, 46, 110, 0, 43, 47, 111, 44,
-        48, 49, 50, 51, 52, 53, 54, 55, 56, 118, 119, 120,
-        57, 58, 59, 60, 13, 14, 78, 15, 79, 16, 17, 18,
-        19, 20, 21, 22, 23, 24, 86, 87, 88, 25, 26, 27,
-        28, 29, 0, 0, 0, 0, 0, 0, 0, 30, 0, 0,
-        0, 0, 0, 0,
+        0, 0, 1, 0, 0, 2, 3, 0, 4, 0, 5, 6,
+        70, 7, 8, 9, 73, 10, 11, 12, 35, 36, 37, 38,
+        102, 39, 40, 41, 105, 45, 42, 46, 110, 43, 47, 111,
+        44, 48, 49, 50, 51, 52, 53, 54, 55, 56, 118, 119,
+        120, 57, 58, 59, 60, 13, 14, 78, 15, 79, 16, 17,
+        18, 19, 20, 21, 22, 23, 24, 86, 87, 88, 25, 26,
+        27, 28, 29, 0, 0, 30, 0, 0, 0, 0,
     ),
 )
 
@@ -323,16 +286,14 @@
     patch_out.start()
     loop(BEGUN, lambda p: gather_issue(p, 0))
     cot_out.start()
-    loop(PAIRS - BEGUN, lambda i: pack(i + BEGUN))
-
-    index_row = mask_index[pl.ds(y, 1), :]
-    count = mask_count[y]
-    spot = lax.broadcasted_iota(jnp.int32, (SEQ, index_row.shape[1]), 0)
-    live = lax.broadcasted_iota(jnp.int32, (1, index_row.shape[1]), 1) < count
-    hits = jnp.where(jnp.logical_and(spot == index_row, live), 1.0, 0.0)
-    FL[...] = jnp.max(hits, axis=1, keepdims=True)
 
     def gains_across(l, yy):
+        index_row = mask_index[pl.ds(y, 1), :]
+        count = mask_count[y]
+        spot = lax.broadcasted_iota(jnp.int32, (SEQ, index_row.shape[1]), 0)
+        live = lax.broadcasted_iota(jnp.int32, (1, index_row.shape[1]), 1) < count
+        hits = jnp.where(jnp.logical_and(spot == index_row, live), 1.0, 0.0)
+        FL[...] = jnp.max(hits, axis=1, keepdims=True)
         for _, r in gain_z:
             r.wait_recv()
         gain_x[0].start()
@@ -832,24 +793,25 @@
         middle = (low + high) // 2
         return lax.cond(m < middle, lambda: plan_of(m, low, middle), lambda: plan_of(m, middle, high))
 
-    def micro(m):
-        plan = plan_of(m, 0, STEPS)
-        for counts, firsts, action in ((plan[0], plan[1], gather_issue), (plan[2], plan[3], scatter_at)):
-
-            @pl.when(counts > 0)
-            def _():
-                for kind in range(5):
-                    count, first = digit(counts, kind, 16), digit(firsts, kind, 16)
-
-                    @pl.when(count > 0)
-                    def _():
-                        def one(i, carry):
-                            action(first + i, kind)
-                            return carry
-
-                        lax.fori_loop(0, count, one, 0)
-
-        word = plan[4]
+    def micro(m, firsts):
+        counts, word = plan_of(m, 0, STEPS)
+        count = tuple(digit(counts, kind, 8) for kind in range(10))
+
+        @pl.when(counts > 0)
+        def _():
+            for kind in range(10):
+                action = gather_issue if kind < 5 else scatter_at
+
+                @pl.when(count[kind] > 0)
+                def _():
+                    def one(i, carry):
+                        if kind == 0:
+                            pack(firsts[kind] + i)
+                        action(firsts[kind] + i, kind % 5)
+                        return carry
+
+                    lax.fori_loop(0, count[kind], one, 0)
+
 
         @pl.when(word > 0)
         def _():
@@ -860,7 +822,9 @@
                 def _():
                     action(l, yy)
 
-    loop(STEPS, micro)
+        return tuple(f + n for f, n in zip(firsts, count))
+
+    lax.fori_loop(0, STEPS, micro, (jnp.int32(BEGUN),) + (jnp.int32(0),) * 9)
 
     own_square = jnp.sum(jnp.sum(NB[...], axis=1, keepdims=True), axis=0, keepdims=True)
     NZC[z, c] = jnp.broadcast_to(own_square, (8, 128))

time: 259 us -> 258 us (level)
  no operation moved by 1% of the time
where the time goes in v6:
time: 258 us; the launch traced here: 257 us
  Pallas kernels  256 us (99%)
    pallas_call x1, Pallas kernels, big_step(): pl.pallas_call(step_kernel, out_shape=(jax.ShapeDtypeStruct((TM, D), F32)...  249 us
    pallas_call x1, Pallas kernels, adam_all(): pl.pallas_call(adam_kernel, grid=(ADAM_STEPS,), out_shape=(*(jax.ShapeDty...  7.86 us

profile of v6, /device:TPU:0, one launch (start us, length us, event | category | flops | bytes accessed | tf_op | source)
XLA Modules:
  0.0 257.3 jit_solution(14356100580661060838)
XLA Ops:
  0.6 248.6 %train_step.1 = (f32[256,768]{1,0:T(8,128)}, f32[256,768]{1,0:T(8,128)}, f32[12,3,32,384]{3,2,1,0:T(8,128)}, f32[8,768]{1,0:T(8,128)}, f32[8,128]{1,0:T(8,128)}) custom-call(f32[24,96,192]{2,1,0:T(8,128)} %bitcast.7, bf16[256,768]{1,0:T(8,128)(2,1)} %patch.1, f32[256,768]{1,0:T(8,128)} %cot.1, s32[2,450]{1,0:T(2,128)} %mask_index.1, s32[2]{0:T(128)} %mask_count.1, ...), custom_call_target="tpu_custom_call" | custom-call | tf_op jit(solution)/shard_map/train_step/pallas_call | solution.py:931
  249.3 7.9 %adam.1 = (f32[24,96,192]{2,1,0:T(8,128)}, f32[24,96,192]{2,1,0:T(8,128)}, f32[24,96,192]{2,1,0:T(8,128)}, f32[5,96]{1,0:T(8,128)}, f32[5,96]{1,0:T(8,128)}, /*i...) custom-call(f32[8,128]{1,0:T(8,128)} %get-tuple-element.23.norm, ...), custom_call_target="tpu_custom_call" | custom-call | tf_op jit(solution)/shard_map/adam/pallas_call | solution.py:1001

commit v7 on v6

--- a/solution.py
+++ b/solution.py
@@ -369,7 +369,7 @@
                 v = V[l, yy, :, lo : lo + HD]
                 s = mm_nt(q, k) * SCALE
                 e = jnp.exp(s - jnp.max(s, axis=1, keepdims=True))
-                probs = e / jnp.sum(e, axis=1, keepdims=True)
+                probs = e * (1.0 / jnp.sum(e, axis=1, keepdims=True))
                 outs.append(mm(probs.astype(BF16), v))
             MIX[l, yy, rows, :] = jnp.concatenate(outs, axis=1).astype(BF16)
 
@@ -387,7 +387,7 @@
             dm = GM[yy, rows, lo : lo + HD]
             s = mm_nt(k, q) * SCALE
             e = jnp.exp(s - jnp.max(s, axis=0, keepdims=True))
-            probs = e / jnp.sum(e, axis=0, keepdims=True)
+            probs = e * (1.0 / jnp.sum(e, axis=0, keepdims=True))
             dp = mm_nt(v, dm)
             ds = probs * (dp - jnp.sum(probs * dp, axis=0, keepdims=True))
             ds = ds.astype(BF16)

time: 258 us -> 258 us (level)
  no operation moved by 1% of the time
where the time goes in v7:
time: 258 us; the launch traced here: 257 us
  Pallas kernels  256 us (99%)
    pallas_call x1, Pallas kernels, big_step(): pl.pallas_call(step_kernel, out_shape=(jax.ShapeDtypeStruct((TM, D), F32)...  249 us
    pallas_call x1, Pallas kernels, adam_all(): pl.pallas_call(adam_kernel, grid=(ADAM_STEPS,), out_shape=(*(jax.ShapeDty...  7.86 us

profile of v7, /device:TPU:0, one launch (start us, length us, event | category | flops | bytes accessed | tf_op | source)
XLA Modules:
  0.0 257.3 jit_solution(14356100580661060838)
XLA Ops:
  0.6 248.6 %train_step.1 = (f32[256,768]{1,0:T(8,128)}, f32[256,768]{1,0:T(8,128)}, f32[12,3,32,384]{3,2,1,0:T(8,128)}, f32[8,768]{1,0:T(8,128)}, f32[8,128]{1,0:T(8,128)}) custom-call(f32[24,96,192]{2,1,0:T(8,128)} %bitcast.7, bf16[256,768]{1,0:T(8,128)(2,1)} %patch.1, f32[256,768]{1,0:T(8,128)} %cot.1, s32[2,450]{1,0:T(2,128)} %mask_index.1, s32[2]{0:T(128)} %mask_count.1, ...), custom_call_target="tpu_custom_call" | custom-call | tf_op jit(solution)/shard_map/train_step/pallas_call | solution.py:931
  249.3 7.9 %adam.1 = (f32[24,96,192]{2,1,0:T(8,128)}, f32[24,96,192]{2,1,0:T(8,128)}, f32[24,96,192]{2,1,0:T(8,128)}, f32[5,96]{1,0:T(8,128)}, f32[5,96]{1,0:T(8,128)}, /*i...) custom-call(f32[8,128]{1,0:T(8,128)} %get-tuple-element.23.norm, ...), custom_call_target="tpu_custom_call" | custom-call | tf_op jit(solution)/shard_map/adam/pallas_call | solution.py:1001
